TPU v7x, 512 devices: a whole 4x8x8 slice. The times are simulated.
512 devices in a mesh: cells: 32 (over y, x), genes: 16 (over z, core).
Axes of the slice: x: 4, y: 8, z: 8, core: 2. Of those that a mesh axis runs over, the one named last changes fastest.
Arguments:
- counts: int32 [32768, 4096], P('cells', 'genes'), may hold values from 0 to 128, as said below
- batch: int32 [32768, 1], P(('cells', 'genes')), may hold values from 0 to 63
- seeds: int32 [32768, 1], P(('cells', 'genes')), may hold values from 0 to 1023
- loadings: bfloat16 [4096, 256], P('genes'), may hold values from -0.09375 to 0.09375
Outputs:
- embedding: float32 [32768, 256], P(('cells', 'genes'))
- assign: float32 [32768, 1024], P(('cells', 'genes'))
- centroids: bfloat16 [1024, 256], replicated
Inputs may be any that keep to these rules, and one draw needn't show every extreme that they name: counts[i, g] >= 1 wherever g mod 64 equals i mod 64. `batch`: every label occurs. `seeds`: every cluster is the seed of some cell.
All inputs are finite; a program needn't handle non-finite values.
Results may differ from a plain program's by a relative error of at most 0.012.
The roundings to bfloat16 on the way count: a program that leaves them out, or rounds other values in their place, can miss the bound.
Values may be sent and summed in bfloat16 or wider, within the bound.
No kernel may reach another device: no remote copies, remote signals or barrier semaphores. Data moves between devices by JAX's collectives and lax.ppermute only.
A program may use at most 64 MiB of HBM per device.

v0:
```python
import jax
import jax.numpy as jnp
from jax import lax
from jax.sharding import PartitionSpec as P

K = 1024
B = 64
ITERS = 2


epsilon = 1e-06
cluster_spread = 0.1


def cluster_tables(cluster_sums, observed, batch_total, total_cells):
    scaled = cluster_sums * lax.rsqrt(
        jnp.sum(cluster_sums * cluster_sums, axis=1, keepdims=True) + epsilon
    )
    cluster_mass = jnp.sum(observed, axis=1, keepdims=True)
    expected = cluster_mass * batch_total[None, :] / total_cells
    ratio = (expected + 1.0) / (observed + 1.0)
    return (scaled.astype(jnp.bfloat16), ratio * ratio)


def per_device(counts, batch, seeds, loadings):
    cell_rows = batch.shape[0]
    total_cells = cell_rows * lax.axis_size("cells") * lax.axis_size("genes")
    values = counts.astype(jnp.float32)
    depth_total = lax.psum(jnp.sum(values, axis=1), "genes")
    logged = jnp.log1p(10000.0 * values / depth_total[:, None]).astype(jnp.bfloat16)
    projected = lax.psum_scatter(
        jnp.dot(logged, loadings, preferred_element_type=jnp.float32),
        "genes",
        scatter_dimension=0,
        tiled=True,
    )
    batch_full = (batch == jnp.arange(B, dtype=jnp.int32)[None, :]).astype(jnp.float32)
    column_sum, batch_total = lax.psum(
        (jnp.sum(projected, axis=0), jnp.sum(batch_full, axis=0)), ("cells", "genes")
    )
    embedding = projected - column_sum / total_cells
    unit_rows = (
        embedding * lax.rsqrt(jnp.sum(embedding * embedding, axis=1, keepdims=True) + epsilon)
    ).astype(jnp.bfloat16)
    batch_low = batch_full.astype(jnp.bfloat16)
    assign = (seeds == jnp.arange(K, dtype=jnp.int32)[None, :]).astype(jnp.float32)
    centroids = jnp.zeros((K, unit_rows.shape[1]), jnp.bfloat16)
    leading = (((0,), (0,)), ((), ()))
    for iteration in range(ITERS):
        rounded = assign.astype(jnp.bfloat16)
        cluster_sums = lax.dot_general(
            rounded, unit_rows, leading, preferred_element_type=jnp.float32
        )
        observed = lax.dot_general(rounded, batch_low, leading, preferred_element_type=jnp.float32)
        whole_sums, whole_observed = lax.psum((cluster_sums, observed), ("cells", "genes"))
        centroids, penalty = cluster_tables(whole_sums, whole_observed, batch_total, total_cells)
        similarity = lax.dot_general(
            unit_rows, centroids, (((1,), (1,)), ((), ())), preferred_element_type=jnp.float32
        )
        distance = 2.0 - 2.0 * similarity
        lookup = lax.dot_general(
            batch_full,
            penalty,
            (((1,), (1,)), ((), ())),
            precision=lax.Precision.HIGHEST,
            preferred_element_type=jnp.float32,
        )
        weights = jnp.exp(-distance / cluster_spread) * lookup
        assign = weights / jnp.sum(weights, axis=1, keepdims=True)
    return (embedding, assign, centroids)


def solution(mesh):
    placed = (
        P("cells", "genes"),
        P(("cells", "genes"), None),
        P(("cells", "genes"), None),
        P("genes", None),
    )
    return jax.shard_map(
        per_device,
        mesh=mesh,
        in_specs=placed,
        out_specs=(P(("cells", "genes"), None), P(("cells", "genes"), None), P()),
        check_vma=False,
    )
```

profile of v0, /device:TPU:1, one launch (start us, length us, event | category | flops | bytes accessed | tf_op | source)
XLA Modules:
  0.0 762.3 jit_solution(6656614358482532397)
XLA Ops:
  7.2 0.0 copy-start
  7.2 0.0 copy-start.4
  7.2 0.0 reduce-scatter.2.cloned.1.call-start
  7.2 1.5 convert_reduce_fusion
  8.8 30.6 %psum.49 = f32[1024]{0:T(1024)S(1)} all-reduce(f32[1024]{0:T(1024)S(1)} %convert_reduce_fusion), channel_id=1, replica_groups=mesh['cells'=32,'genes'=16] {'genes'}, use_global_device_ids=true, to_apply=%region_1.0 | all-reduce | flops 1024 | bytes 8192 | tf_op jit(solution)/shard_map/psum | solution.py:29
  39.4 0.0 copy-done
  39.4 0.0 copy-done.4
  39.4 1.6 fusion.9
  41.0 0.0 reduce-scatter.2.cloned.1.call-update
  41.0 0.0 copy-start.10
  41.0 0.0 all-reduce.8.cloned.1.call-start
  41.1 0.6 copy-done.10
  41.7 0.1 convert_reduce_fusion.1
  41.8 0.0 copy-start.9
  41.8 0.7 copy-done.9
  42.4 1.0 fusion.22
  43.4 55.0 %reduce-scatter.2.cloned.1.call-done = f32[64,256]{1,0:T(8,128)} async-done(((f32[1024,256]{1,0:T(8,128)}), f32[64,256]{1,0:T(8,128)}) %reduce-scatter.2.cloned.1.call-update) | async-done | bytes 65552 | tf_op jit(solution)/shard_map/reduce_scatter | solution.py:31
  98.4 0.0 copy-start.8
  98.4 0.9 reduce_sum.91
  99.4 99.6 %all-reduce = (f32[256]{0:T(256)S(1)}, f32[64]{0:T(128)S(1)}) all-reduce(f32[256]{0:T(256)S(1)} %reduce_sum.91, f32[64]{0:T(128)S(1)} %convert_reduce_fusion.1), channel_id=1, replica_groups=mesh['cells'=32,'genes'=16] {'cells','genes'}, use_global_device_ids=true, to_apply=%region_4.0 | all-reduce | flops 320 | bytes 2560 | tf_op jit(solution)/shard_map/psum | solution.py:38
  199.0 0.0 copy-done.8
  199.0 0.1 multiply_reduce_fusion.2
  199.1 0.0 copy-start.7
  199.1 0.1 multiply_convert_fusion.3
  199.2 1.4 fusion.23
  200.6 0.0 copy-done.7
  200.6 0.0 all-reduce.8.cloned.1.call-update
  200.7 0.0 all-reduce.6.cloned.1.call-start
  200.7 272.0 %all-reduce.8.cloned.1.call-done = (f32[1024,256]{1,0:T(8,128)}, f32[1024,64]{0,1:T(8,128)}) async-done(((f32[1024,256]{1,0:T(8,128)}, f32[1024,64]{0,1:T(8,128)}), (f32[1024,256]{1,0:T(8,128)}, f32[1024,64]{0,1:T(8,128)})) %all-reduce.8.cloned.1.call-update) | async-done | bytes 1310736 | tf_op jit(solution)/shard_map/psum | solution.py:55
  472.7 0.0 copy-start.1
  472.7 1.5 multiply_reduce_fusion.1
  474.2 0.0 copy-done.1
  474.3 0.0 copy-start.6
  474.3 0.4 fusion.7
  474.6 0.6 copy-done.6
  475.2 0.5 fusion.45
  475.7 1.0 fusion.34
  476.7 1.4 fusion.44
  478.2 0.0 all-reduce.6.cloned.1.call-update
  478.2 273.5 %all-reduce.6.cloned.1.call-done = (f32[1024,256]{1,0:T(8,128)}, f32[1024,64]{0,1:T(8,128)}) async-done(((f32[1024,256]{1,0:T(8,128)}, f32[1024,64]{0,1:T(8,128)}), (f32[1024,256]{1,0:T(8,128)}, f32[1024,64]{0,1:T(8,128)})) %all-reduce.6.cloned.1.call-update) | async-done | bytes 1310736 | tf_op jit(solution)/shard_map/psum | solution.py:55
  751.7 0.0 copy-start.2
  751.7 1.5 multiply_reduce_fusion
  753.2 0.0 copy-done.2
  753.2 0.0 copy-start.5
  753.2 0.2 multiply_convert_fusion
  753.4 0.0 copy-start.3
  753.4 0.7 copy-done.5
  754.2 0.3 fusion.3
  754.5 0.0 copy-done.3
  754.5 0.5 fusion.46
  755.0 0.8 broadcast_divide_fusion
  (6 shorter events, 0.1 us)
Async XLA Ops:
  7.2 32.2 %copy-start = (bf16[256,256]{1,0:T(8,128)(2,1)S(1)}, bf16[256,256]{1,0:T(8,128)(2,1)}, u32[]{:S(2)}) copy-start(bf16[256,256]{1,0:T(8,128)(2,1)} %param.7) | copy-start | bytes 393220
  7.2 32.2 %copy-start.4 = (s32[1024,256]{1,0:T(8,128)S(1)}, s32[1024,256]{1,0:T(8,128)}, u32[]{:S(2)}) copy-start(s32[1024,256]{1,0:T(8,128)} %param.4) | copy-start | bytes 3145732
  7.2 91.2 %reduce-scatter.2.cloned.1.call-start = ((), (), s32[]{:S(2)}) async-start(), calls=%async_computation.1 | async-start | bytes 1114112 | tf_op jit(solution)/shard_map/reduce_scatter | solution.py:31
  41.0 0.7 copy-start.10
  41.0 431.7 %all-reduce.8.cloned.1.call-start = ((), (), s32[]{:S(2)}) async-start(), calls=%async_computation.3 | async-start | bytes 2621440 | tf_op jit(solution)/shard_map/psum | solution.py:55
  41.8 0.7 copy-start.9
  98.4 100.6 %copy-start.8 = (f32[64,256]{1,0:T(8,128)S(1)}, f32[64,256]{1,0:T(8,128)}, u32[]{:S(2)}) copy-start(f32[64,256]{1,0:T(8,128)} %reduce-scatter.2.cloned.1.call-done) | copy-start | bytes 196612
  199.1 1.5 copy-start.7
  200.7 551.0 %all-reduce.6.cloned.1.call-start = ((), (), s32[]{:S(2)}) async-start(), calls=%async_computation.2 | async-start | bytes 2621440 | tf_op jit(solution)/shard_map/psum | solution.py:55
  472.7 1.5 copy-start.1
  474.3 1.0 copy-start.6
  751.7 1.5 copy-start.2
  753.2 1.0 copy-start.5
  753.4 1.1 copy-start.3
Sparse Core Ops, SparseCore 0:
  41.1 57.2 reduce-scatter.1
  200.8 271.8 all-reduce.7
  478.4 273.2 all-reduce.5
where the time goes:
time: 764 us; the launch traced here: 762 us
  waiting for transfers between devices  601 us (79%)
  blocking collectives  130 us (17%)
  between operations  13.9 us (2%)
  matrix products  8.1 us (1%)
    psum x2, waiting for transfers between devices, per_device(): lax.psum((cluster_sums, observed), ('cells', 'genes'))  545 us
    psum x1, blocking collectives, per_device(): lax.psum((jnp.sum(projected, axis=0), jnp.sum(batch_full, axis=0)), ('cel...  99.6 us
    reduce_scatter x1, waiting for transfers between devices, per_device(): lax.psum_scatter(jnp.dot(logged, loadings, preferred_element_type=jnp.flo...  55 us
    psum x1, blocking collectives, per_device(): depth_total = lax.psum(jnp.sum(values, axis=1), 'genes')  30.6 us
  transfers between devices with their start and end apart: 3, of which 3 were waited for; matrix products, arithmetic and copies ran while one was open for 0% of the time, Pallas kernels for 0%

commit v1 on v0

v1 whole, which is shorter than its diff:
```python
import jax
import jax.numpy as jnp
from jax import lax
from jax.sharding import PartitionSpec as P

K = 1024
B = 64
ITERS = 2
CELL_AXIS = "cells"
GENE_AXIS = "genes"

epsilon = 1e-06
cluster_spread = 0.1

f32 = jnp.float32
bf16 = jnp.bfloat16
leading = (((0,), (0,)), ((), ()))
trailing = (((1,), (1,)), ((), ()))


def exchange(blocks, axis):
    return lax.all_to_all(blocks, axis, 0, 0, tiled=False)


def share(block, axis):
    return exchange(jnp.broadcast_to(block[None], (lax.axis_size(axis),) + block.shape), axis)


def one_hot(labels, first, count, dtype):
    return (labels == first + jnp.arange(count, dtype=jnp.int32)[None, :]).astype(dtype)


def halves(value):
    high = value.astype(bf16)
    return high, (value - high.astype(f32)).astype(bf16)


def cluster_rows(sums, observed, batch_total, total_cells):
    scaled = sums * lax.rsqrt(jnp.sum(sums * sums, axis=1, keepdims=True) + epsilon)
    mass = jnp.sum(observed, axis=1, keepdims=True)
    ratio = (mass * batch_total / total_cells + 1.0) / (observed + 1.0)
    high, low = halves(ratio * ratio)
    return jnp.concatenate([scaled.astype(bf16), high, low], axis=1)


def cluster_weights(unit_rows, batch_twice, rows):
    depth = unit_rows.shape[1]
    similarity = lax.dot_general(unit_rows, rows[:, :depth], trailing, preferred_element_type=f32)
    lookup = lax.dot_general(batch_twice, rows[:, depth:], trailing, preferred_element_type=f32)
    distance = 2.0 - 2.0 * similarity
    return jnp.exp(-distance / cluster_spread) * lookup


def per_device(counts, batch, seeds, loadings):
    n_cells, n_genes = lax.axis_size(CELL_AXIS), lax.axis_size(GENE_AXIS)
    group, own = counts.shape[0], batch.shape[0]
    total_cells = group * n_cells
    width = loadings.shape[1]
    mine = K // n_genes
    piece = mine // n_cells

    values = counts.astype(f32)
    packet = jnp.concatenate(
        [jnp.sum(values, axis=1), batch[:, 0].astype(f32), seeds[:, 0].astype(f32)]
    )
    packets = share(packet, GENE_AXIS)
    depth_total = jnp.sum(packets[:, :group], axis=0)
    group_batch = packets[:, group : group + own].reshape(group, 1).astype(jnp.int32)
    group_seeds = packets[:, group + own :].reshape(group, 1).astype(jnp.int32)

    logged = jnp.log1p(10000.0 * values / depth_total[:, None]).astype(bf16)
    partial = jnp.dot(logged, loadings, preferred_element_type=f32)

    batch_hot = one_hot(group_batch, 0, B, bf16)
    first = lax.axis_index(GENE_AXIS) * mine
    assign = one_hot(group_seeds, first, mine, bf16)
    first_observed = lax.dot_general(assign, batch_hot, leading, preferred_element_type=f32)
    group_labels = jnp.sum(batch_hot.astype(f32), axis=0)

    everyone = jnp.concatenate([jnp.sum(partial, axis=0), group_labels])
    packet = jnp.concatenate(
        [
            jnp.broadcast_to(everyone[None], (n_cells, width + B)),
            first_observed.reshape(n_cells, piece * B),
        ],
        axis=1,
    )
    arrived = jnp.sum(exchange(packet, CELL_AXIS), axis=0)
    center = arrived[:width] / total_cells
    batch_total = arrived[width : width + B][None]
    observed = arrived[width + B :].reshape(piece, B)

    centred = (partial - center[None]).astype(bf16).reshape(n_genes, own, width)
    embedding = jnp.sum(exchange(centred, GENE_AXIS).astype(f32), axis=0)
    own_rows = (
        embedding * lax.rsqrt(jnp.sum(embedding * embedding, axis=1, keepdims=True) + epsilon)
    ).astype(bf16)
    unit_rows = share(own_rows, GENE_AXIS).reshape(group, width)

    batch_twice = jnp.concatenate([batch_hot, batch_hot], axis=1)
    for iteration in range(ITERS):
        if iteration == 0:
            sums = lax.dot_general(assign, unit_rows, leading, preferred_element_type=f32)
            sums = jnp.sum(exchange(sums.reshape(n_cells, piece, width), CELL_AXIS), axis=0)
        else:
            weights = cluster_weights(unit_rows, batch_twice, rows)
            norm = jnp.sum(share(jnp.sum(weights, axis=1), GENE_AXIS), axis=0)
            rounded = (weights / norm[:, None]).astype(bf16)
            both = jnp.concatenate([unit_rows, batch_hot], axis=1)
            sums = lax.dot_general(rounded, both, leading, preferred_element_type=f32)
            sums = jnp.sum(exchange(sums.reshape(n_cells, piece, width + B), CELL_AXIS), axis=0)
            sums, observed = sums[:, :width], sums[:, width:]
        rows = cluster_rows(sums, observed, batch_total, total_cells)
        rows = share(rows, CELL_AXIS).reshape(mine, width + 2 * B)

    rows = share(rows, GENE_AXIS).reshape(K, width + 2 * B)
    own_hot = one_hot(batch, 0, B, bf16)
    weights = cluster_weights(own_rows, jnp.concatenate([own_hot, own_hot], axis=1), rows)
    assign = weights / jnp.sum(weights, axis=1, keepdims=True)
    return (embedding, assign, rows[:, :width])


def solution(mesh):
    placed = (
        P("cells", "genes"),
        P(("cells", "genes"), None),
        P(("cells", "genes"), None),
        P("genes", None),
    )
    return jax.shard_map(
        per_device,
        mesh=mesh,
        in_specs=placed,
        out_specs=(P(("cells", "genes"), None), P(("cells", "genes"), None), P()),
        check_vma=False,
    )
```

time: 764 us -> 184 us (0.24)
  waiting for transfers between devices: 601 us -> 64.5 us
  blocking collectives: 130 us -> 76.6 us
  starting transfers between devices: 0.12 us -> 29 us
  between operations: 13.9 us -> 0.91 us
    psum x2 -> x0, waiting for transfers between devices: 545 us -> none  [per_device(): lax.psum((cluster_sums, observed), ('cells', 'genes'))]
    psum x2 -> x0, blocking collectives: 130 us -> none  [the longest x1 99.6 us: per_device(): lax.psum((jnp.sum(projected, axis=0), jnp.sum(batch_full, axis=0)), ('cel...]
    all_to_all x0 -> x5, blocking collectives: none -> 76.6 us  [exchange(): return lax.all_to_all(blocks, axis, 0, 0, tiled=False)]
    all_to_all x0 -> x5, waiting for transfers between devices: none -> 64.5 us  [exchange(): return lax.all_to_all(blocks, axis, 0, 0, tiled=False)]
    reduce_scatter x1 -> x0, waiting for transfers between devices: 55 us -> none  [per_device(): lax.psum_scatter(jnp.dot(logged, loadings, preferred_element_type=jnp.flo...]
    all_to_all x0 -> x5, starting transfers between devices: none -> 29 us  [exchange(): return lax.all_to_all(blocks, axis, 0, 0, tiled=False)]
  transfers between devices with their start and end apart: 3 -> 5, of which waited for: 3 -> 5; matrix products, arithmetic and copies ran while one was open for 0% -> 0% of each run, Pallas kernels for 0% -> 0%
where the time goes in v1:
time: 184 us; the launch traced here: 183 us
  blocking collectives  76.6 us (42%)
  waiting for transfers between devices  64.5 us (35%)
  starting transfers between devices  29 us (16%)
  local copies, waits for them, and re-layouts  4.59 us (2%)
  other arithmetic  4.52 us (2%)
  matrix products  2.95 us (2%)
    all_to_all x5, blocking collectives, exchange(): return lax.all_to_all(blocks, axis, 0, 0, tiled=False)  76.6 us
    all_to_all x5, waiting for transfers between devices, exchange(): return lax.all_to_all(blocks, axis, 0, 0, tiled=False)  64.5 us
    all_to_all x5, starting transfers between devices, exchange(): return lax.all_to_all(blocks, axis, 0, 0, tiled=False)  29 us
  transfers between devices with their start and end apart: 5, of which 5 were waited for; matrix products, arithmetic and copies ran while one was open for 0% of the time, Pallas kernels for 0%

profile of v1, /device:TPU:1, one launch (start us, length us, event | category | flops | bytes accessed | tf_op | source)
XLA Modules:
  0.0 183.0 jit_solution(10477905900326389477)
XLA Ops:
  0.6 0.0 copy-start
  0.6 0.0 copy-start.2
  0.7 1.5 convert_reduce_fusion.1
  2.2 0.1 concatenate.27
  2.3 0.7 broadcast_in_dim.16
  3.0 11.8 %all-to-all-start = ((f32[16,1,1152]{2,1,0:T(1,128)}), f32[16,1,1152]{2,1,0:T(1,128)S(1)}, u32[]{:S(2)}, u32[]{:S(2)}) async-start(f32[16,1,1152]{2,1,0:T(1,128)} %broadcast_in_dim.16), calls=%async_computation | async-start | bytes 147456 | tf_op jit(solution)/shard_map/all_to_all | solution.py:22
  14.8 7.9 %all-to-all-done = f32[16,1,1152]{2,1,0:T(1,128)S(1)} async-done(((f32[16,1,1152]{2,1,0:T(1,128)}), f32[16,1,1152]{2,1,0:T(1,128)S(1)}, u32[]{:S(2)}, u32[]{:S(2)}) %all-to-all-start) | async-done | bytes 73760 | tf_op jit(solution)/shard_map/all_to_all | solution.py:22
  22.8 0.1 slice_convert_fusion
  22.9 0.1 convert_element_type.91
  22.9 0.1 convert_element_type.95
  23.0 0.2 convert_reduce_fusion.2
  23.2 0.6 fusion.12
  23.8 0.1 reshape.132
  23.9 0.0 copy-done
  23.9 0.6 fusion.37
  24.6 0.1 pad_maximum_fusion
  24.7 18.3 %all_to_all.59 = f32[32,1,448]{2,1,0:T(1,128)S(1)} all-to-all(f32[32,1,448]{2,1,0:T(1,128)S(1)} %all_to_all.39), channel_id=1, replica_groups=mesh['cells'=32,'genes'=16] {'cells'}, dimensions={0} | all-to-all | bytes 114688 | tf_op jit(solution)/shard_map/all_to_all | solution.py:22
  43.0 0.1 reduce_sum.148
  43.1 0.1 subtract_convert_fusion
  43.1 21.3 %all_to_all.60 = bf16[16,64,256]{2,1,0:T(8,128)(2,1)S(1)} all-to-all(bf16[16,64,256]{2,1,0:T(8,128)(2,1)S(1)} %bitcast.22), channel_id=1, replica_groups=mesh['cells'=32,'genes'=16] {'genes'}, dimensions={0} | all-to-all | bytes 1048576 | tf_op jit(solution)/shard_map/all_to_all | solution.py:22
  64.4 0.1 convert_reduce_fusion
  64.5 0.0 copy-start.3
  64.5 0.1 multiply_reduce_fusion
  64.6 0.1 multiply_convert_fusion
  64.7 0.9 broadcast_in_dim.18
  65.6 3.5 %all-to-all-start.3 = ((bf16[16,64,256]{2,1,0:T(8,128)(2,1)}), bf16[16,64,256]{2,1,0:T(8,128)(2,1)S(1)}, u32[]{:S(2)}, u32[]{:S(2)}) async-start(bf16[16,64,256]{2,1,0:T(8,128)(2,1)} %broadcast_in_dim.18), calls=%async_computation.3 | async-start | bytes 1048576 | tf_op jit(solution)/shard_map/all_to_all | solution.py:22
  69.1 0.1 slice.49
  69.2 0.1 reshape.135
  69.2 0.1 reduce_sum.153
  69.4 16.3 %all-to-all-done.3 = bf16[16,64,256]{2,1,0:T(8,128)(2,1)S(1)} async-done(((bf16[16,64,256]{2,1,0:T(8,128)(2,1)}), bf16[16,64,256]{2,1,0:T(8,128)(2,1)S(1)}, u32[]{:S(2)}, u32[]{:S(2)}) %all-to-all-start.3) | async-done | bytes 524320 | tf_op jit(solution)/shard_map/all_to_all | solution.py:22
  85.7 0.2 fusion.23
  86.0 0.7 copy.9
  86.6 3.9 %all-to-all-start.4 = ((f32[32,2,256]{2,1,0:T(2,128)}), f32[32,2,256]{2,1,0:T(2,128)S(1)}, u32[]{:S(2)}, u32[]{:S(2)}) async-start(f32[32,2,256]{2,1,0:T(2,128)} %copy.9), calls=%async_computation.4 | async-start | bytes 131072 | tf_op jit(solution)/shard_map/all_to_all | solution.py:22
  90.5 0.1 subtract_convert_fusion.2
  90.6 9.0 %all-to-all-done.4 = f32[32,2,256]{2,1,0:T(2,128)S(1)} async-done(((f32[32,2,256]{2,1,0:T(2,128)}), f32[32,2,256]{2,1,0:T(2,128)S(1)}, u32[]{:S(2)}, u32[]{:S(2)}) %all-to-all-start.4) | async-done | bytes 65568 | tf_op jit(solution)/shard_map/all_to_all | solution.py:22
  99.6 0.1 multiply_reduce_fusion.2
  99.7 0.1 multiply_convert_fusion.2
  99.8 0.1 pad_maximum_fusion.2
  99.9 0.7 broadcast_in_dim.19
  100.6 3.9 %all-to-all-start.5 = ((bf16[32,2,384]{2,1,0:T(2,128)(2,1)}), bf16[32,2,384]{2,1,0:T(2,128)(2,1)S(1)}, u32[]{:S(2)}, u32[]{:S(2)}) async-start(bf16[32,2,384]{2,1,0:T(2,128)(2,1)} %broadcast_in_dim.19), calls=%async_computation.5 | async-start | bytes 98304 | tf_op jit(solution)/shard_map/all_to_all | solution.py:22
  104.4 0.2 fusion.13
  104.6 8.5 %all-to-all-done.5 = bf16[32,2,384]{2,1,0:T(2,128)(2,1)S(1)} async-done(((bf16[32,2,384]{2,1,0:T(2,128)(2,1)}), bf16[32,2,384]{2,1,0:T(2,128)(2,1)S(1)}, u32[]{:S(2)}, u32[]{:S(2)}) %all-to-all-start.5) | async-done | bytes 49184 | tf_op jit(solution)/shard_map/all_to_all | solution.py:22
  113.2 0.3 fusion.7
  113.5 0.3 fusion.38
  113.8 12.7 %all_to_all.61 = f32[16,1,1024]{2,1,0:T(1,128)S(1)} all-to-all(f32[16,1,1024]{2,1,0:T(1,128)S(1)} %broadcast_in_dim.20), channel_id=1, replica_groups=mesh['cells'=32,'genes'=16] {'genes'}, dimensions={0} | all-to-all | bytes 131072 | tf_op jit(solution)/shard_map/all_to_all | solution.py:22
  126.5 0.1 reduce_sum.155
  126.6 0.2 fusion.8
  126.8 0.1 reshape.137
  126.9 12.5 %all_to_all.62 = f32[32,2,320]{2,1,0:T(2,128)S(1)} all-to-all(f32[32,2,320]{2,1,0:T(2,128)S(1)} %reshape.137), channel_id=1, replica_groups=mesh['cells'=32,'genes'=16] {'cells'}, dimensions={0} | all-to-all | bytes 163840 | tf_op jit(solution)/shard_map/all_to_all | solution.py:22
  139.4 0.1 reduce_sum.156
  139.4 0.1 multiply_reduce_fusion.1
  139.5 0.1 slice_reduce_fusion.1
  139.7 0.1 multiply_convert_fusion.1
  139.7 0.1 subtract_convert_fusion.1
  139.8 0.1 pad_maximum_fusion.3
  139.9 11.8 %all_to_all.63 = bf16[32,2,384]{2,1,0:T(2,128)(2,1)S(1)} all-to-all(bf16[32,2,384]{2,1,0:T(2,128)(2,1)S(1)} %broadcast_in_dim.21), channel_id=1, replica_groups=mesh['cells'=32,'genes'=16] {'cells'}, dimensions={0} | all-to-all | bytes 98304 | tf_op jit(solution)/shard_map/all_to_all | solution.py:22
  151.8 1.0 broadcast_in_dim.23
  152.7 6.0 %all-to-all-start.9 = ((bf16[16,64,384]{2,1,0:T(8,128)(2,1)}), bf16[16,64,384]{2,1,0:T(8,128)(2,1)S(1)}, u32[]{:S(2)}, u32[]{:S(2)}) async-start(bf16[16,64,384]{2,1,0:T(8,128)(2,1)} %broadcast_in_dim.23), calls=%async_computation.9 | async-start | bytes 1572864 | tf_op jit(solution)/shard_map/all_to_all | solution.py:22
  158.7 0.1 iota_compare_fusion.2
  158.8 22.7 %all-to-all-done.9 = bf16[16,64,384]{2,1,0:T(8,128)(2,1)S(1)} async-done(((bf16[16,64,384]{2,1,0:T(8,128)(2,1)}), bf16[16,64,384]{2,1,0:T(8,128)(2,1)S(1)}, u32[]{:S(2)}, u32[]{:S(2)}) %all-to-all-start.9) | async-done | bytes 786464 | tf_op jit(solution)/shard_map/all_to_all | solution.py:22
  181.5 0.0 copy-start.1
  181.5 0.3 fusion.3
  181.8 0.3 fusion.39
  182.2 0.8 broadcast_divide_fusion
  (25 shorter events, 0.3 us)
Async XLA Ops:
  0.6 23.3 %copy-start = (bf16[256,256]{1,0:T(8,128)(2,1)S(1)}, bf16[256,256]{1,0:T(8,128)(2,1)}, u32[]{:S(2)}) copy-start(bf16[256,256]{1,0:T(8,128)(2,1)} %param.7) | copy-start | bytes 393220
  0.6 23.2 %copy-start.2 = (s32[1024,256]{1,0:T(8,128)S(1)}, s32[1024,256]{1,0:T(8,128)}, u32[]{:S(2)}) copy-start(s32[1024,256]{1,0:T(8,128)} %param.4) | copy-start | bytes 3145732
  0.7 1.6 copy-start.4
  0.7 1.6 copy-start.5
  3.0 19.8 %all-to-all-start = ((f32[16,1,1152]{2,1,0:T(1,128)}), f32[16,1,1152]{2,1,0:T(1,128)S(1)}, u32[]{:S(2)}, u32[]{:S(2)}) async-start(f32[16,1,1152]{2,1,0:T(1,128)} %broadcast_in_dim.16), calls=%async_computation | async-start | bytes 147456 | tf_op jit(solution)/shard_map/all_to_all | solution.py:22
  64.5 21.4 %copy-start.3 = (f32[64,256]{1,0:T(8,128)}, f32[64,256]{1,0:T(8,128)S(1)}, u32[]{:S(2)}) copy-start(f32[64,256]{1,0:T(8,128)S(1)} %convert_reduce_fusion) | copy-start | bytes 196612
  65.6 20.1 %all-to-all-start.3 = ((bf16[16,64,256]{2,1,0:T(8,128)(2,1)}), bf16[16,64,256]{2,1,0:T(8,128)(2,1)S(1)}, u32[]{:S(2)}, u32[]{:S(2)}) async-start(bf16[16,64,256]{2,1,0:T(8,128)(2,1)} %broadcast_in_dim.18), calls=%async_computation.3 | async-start | bytes 1048576 | tf_op jit(solution)/shard_map/all_to_all | solution.py:22
  86.6 12.9 %all-to-all-start.4 = ((f32[32,2,256]{2,1,0:T(2,128)}), f32[32,2,256]{2,1,0:T(2,128)S(1)}, u32[]{:S(2)}, u32[]{:S(2)}) async-start(f32[32,2,256]{2,1,0:T(2,128)} %copy.9), calls=%async_computation.4 | async-start | bytes 131072 | tf_op jit(solution)/shard_map/all_to_all | solution.py:22
  100.6 12.6 %all-to-all-start.5 = ((bf16[32,2,384]{2,1,0:T(2,128)(2,1)}), bf16[32,2,384]{2,1,0:T(2,128)(2,1)S(1)}, u32[]{:S(2)}, u32[]{:S(2)}) async-start(bf16[32,2,384]{2,1,0:T(2,128)(2,1)} %broadcast_in_dim.19), calls=%async_computation.5 | async-start | bytes 98304 | tf_op jit(solution)/shard_map/all_to_all | solution.py:22
  152.7 28.7 %all-to-all-start.9 = ((bf16[16,64,384]{2,1,0:T(8,128)(2,1)}), bf16[16,64,384]{2,1,0:T(8,128)(2,1)S(1)}, u32[]{:S(2)}, u32[]{:S(2)}) async-start(bf16[16,64,384]{2,1,0:T(8,128)(2,1)} %broadcast_in_dim.23), calls=%async_computation.9 | async-start | bytes 1572864 | tf_op jit(solution)/shard_map/all_to_all | solution.py:22
  181.5 1.5 copy-start.1

commit v2 on v1

--- a/solution.py
+++ b/solution.py
@@ -26,8 +26,15 @@
     return exchange(jnp.broadcast_to(block[None], (lax.axis_size(axis),) + block.shape), axis)
 
 
-def one_hot(labels, first, count, dtype):
-    return (labels == first + jnp.arange(count, dtype=jnp.int32)[None, :]).astype(dtype)
+def gather(block, axis):
+    return lax.all_gather(block, axis, tiled=True)
+
+
+def one_hot(labels, count, dtype):
+    return (labels == jnp.arange(count, dtype=jnp.int32)[None, :]).astype(dtype)
+
+
+together = lax.optimization_barrier
 
 
 def halves(value):
@@ -35,12 +42,15 @@
     return high, (value - high.astype(f32)).astype(bf16)
 
 
-def cluster_rows(sums, observed, batch_total, total_cells):
+def unit_centroids(sums):
     scaled = sums * lax.rsqrt(jnp.sum(sums * sums, axis=1, keepdims=True) + epsilon)
+    return scaled.astype(bf16)
+
+
+def penalty_halves(observed, batch_total, total_cells):
     mass = jnp.sum(observed, axis=1, keepdims=True)
     ratio = (mass * batch_total / total_cells + 1.0) / (observed + 1.0)
-    high, low = halves(ratio * ratio)
-    return jnp.concatenate([scaled.astype(bf16), high, low], axis=1)
+    return jnp.concatenate(halves(ratio * ratio), axis=1)
 
 
 def cluster_weights(unit_rows, batch_twice, rows):
@@ -63,6 +73,11 @@
     packet = jnp.concatenate(
         [jnp.sum(values, axis=1), batch[:, 0].astype(f32), seeds[:, 0].astype(f32)]
     )
+    own_hot = one_hot(batch, B, bf16)
+    first = lax.axis_index(GENE_AXIS) * mine
+    packet, own_twice, first = together(
+        (packet, jnp.concatenate([own_hot, own_hot], axis=1), first)
+    )
     packets = share(packet, GENE_AXIS)
     depth_total = jnp.sum(packets[:, :group], axis=0)
     group_batch = packets[:, group : group + own].reshape(group, 1).astype(jnp.int32)
@@ -71,9 +86,8 @@
     logged = jnp.log1p(10000.0 * values / depth_total[:, None]).astype(bf16)
     partial = jnp.dot(logged, loadings, preferred_element_type=f32)
 
-    batch_hot = one_hot(group_batch, 0, B, bf16)
-    first = lax.axis_index(GENE_AXIS) * mine
-    assign = one_hot(group_seeds, first, mine, bf16)
+    batch_hot = one_hot(group_batch, B, bf16)
+    assign = one_hot(group_seeds - first, mine, bf16)
     first_observed = lax.dot_general(assign, batch_hot, leading, preferred_element_type=f32)
     group_labels = jnp.sum(batch_hot.astype(f32), axis=0)
 
@@ -85,19 +99,22 @@
         ],
         axis=1,
     )
+    batch_twice = jnp.concatenate([batch_hot, batch_hot], axis=1)
+    packet, batch_hot, batch_twice, assign = together((packet, batch_hot, batch_twice, assign))
     arrived = jnp.sum(exchange(packet, CELL_AXIS), axis=0)
     center = arrived[:width] / total_cells
     batch_total = arrived[width : width + B][None]
     observed = arrived[width + B :].reshape(piece, B)
+    penalty = penalty_halves(observed, batch_total, total_cells)
 
     centred = (partial - center[None]).astype(bf16).reshape(n_genes, own, width)
+    centred, penalty, batch_total = together((centred, penalty, batch_total))
     embedding = jnp.sum(exchange(centred, GENE_AXIS).astype(f32), axis=0)
     own_rows = (
         embedding * lax.rsqrt(jnp.sum(embedding * embedding, axis=1, keepdims=True) + epsilon)
     ).astype(bf16)
-    unit_rows = share(own_rows, GENE_AXIS).reshape(group, width)
+    unit_rows = gather(own_rows, GENE_AXIS)
 
-    batch_twice = jnp.concatenate([batch_hot, batch_hot], axis=1)
     for iteration in range(ITERS):
         if iteration == 0:
             sums = lax.dot_general(assign, unit_rows, leading, preferred_element_type=f32)
@@ -109,13 +126,13 @@
             both = jnp.concatenate([unit_rows, batch_hot], axis=1)
             sums = lax.dot_general(rounded, both, leading, preferred_element_type=f32)
             sums = jnp.sum(exchange(sums.reshape(n_cells, piece, width + B), CELL_AXIS), axis=0)
-            sums, observed = sums[:, :width], sums[:, width:]
-        rows = cluster_rows(sums, observed, batch_total, total_cells)
+            penalty = penalty_halves(sums[:, width:], batch_total, total_cells)
+            sums = sums[:, :width]
+        rows = jnp.concatenate([unit_centroids(sums), penalty], axis=1)
         rows = share(rows, CELL_AXIS).reshape(mine, width + 2 * B)
 
-    rows = share(rows, GENE_AXIS).reshape(K, width + 2 * B)
-    own_hot = one_hot(batch, 0, B, bf16)
-    weights = cluster_weights(own_rows, jnp.concatenate([own_hot, own_hot], axis=1), rows)
+    rows = gather(rows, GENE_AXIS)
+    weights = cluster_weights(own_rows, own_twice, rows)
     assign = weights / jnp.sum(weights, axis=1, keepdims=True)
     return (embedding, assign, rows[:, :width])
 

time: 184 us -> 167 us (0.908)
  blocking collectives: 76.6 us -> 157 us
  waiting for transfers between devices: 64.5 us -> 0 us
  starting transfers between devices: 29 us -> 0 us
  local copies, waits for them, and re-layouts: 4.59 us -> 0.87 us
    all_to_all x5 -> x0, waiting for transfers between devices: 64.5 us -> none  [exchange(): return lax.all_to_all(blocks, axis, 0, 0, tiled=False)]
    all_to_all x5 -> x8, blocking collectives: 76.6 us -> 122 us  [exchange(): return lax.all_to_all(blocks, axis, 0, 0, tiled=False)]
    all_gather x0 -> x2, blocking collectives: none -> 35.1 us  [gather(): return lax.all_gather(block, axis, tiled=True)]
    all_to_all x5 -> x0, starting transfers between devices: 29 us -> none  [exchange(): return lax.all_to_all(blocks, axis, 0, 0, tiled=False)]
    broadcast_in_dim x7 -> x4, local copies, waits for them, and re-layouts: 3.26 us -> 0.15 us  [share(): jnp.broadcast_to(block[None], (lax.axis_size(axis),) + block.shape)]
  transfers between devices with their start and end apart: 5 -> 0, of which waited for: 5 -> 0; matrix products, arithmetic and copies ran while one was open for 0% -> 0% of each run, Pallas kernels for 0% -> 0%
where the time goes in v2:
time: 167 us
  blocking collectives  157 us (94%)
  other arithmetic  4.9 us (3%)
  matrix products  2.82 us (2%)
    all_to_all x8, blocking collectives, exchange(): return lax.all_to_all(blocks, axis, 0, 0, tiled=False)  122 us
    all_gather x2, blocking collectives, gather(): return lax.all_gather(block, axis, tiled=True)  35.1 us

profile of v2, /device:TPU:1, one launch (start us, length us, event | category | flops | bytes accessed | tf_op | source)
XLA Modules:
  0.0 166.8 jit_solution(10941668958827580596)
XLA Ops:
  0.6 0.0 copy-start
  0.6 0.0 copy-start.4
  0.7 0.0 copy-start.5
  0.7 1.5 convert_reduce_fusion.1
  2.1 0.0 copy-done.4
  2.2 0.0 copy-done.5
  2.2 0.0 copy-start.2
  2.2 0.1 iota_compare_fusion.4
  2.3 0.1 add_convert_fusion
  2.3 0.1 concatenate.30
  2.5 19.6 %all_to_all.49 = f32[16,1,1152]{2,1,0:T(1,128)S(1)} all-to-all(f32[16,1,1152]{2,1,0:T(1,128)S(1)} %broadcast_in_dim.12), channel_id=1, replica_groups=mesh['cells'=32,'genes'=16] {'genes'}, dimensions={0} | all-to-all | bytes 147456 | tf_op jit(solution)/shard_map/all_to_all | solution.py:22
  22.1 0.1 fusion.22
  22.1 0.1 sub.36
  22.2 0.1 convert_element_type.87
  22.3 0.2 convert_reduce_fusion.2
  22.5 0.6 fusion.13
  23.1 0.2 fusion.12
  23.3 0.2 fusion.14
  23.5 0.1 reshape.100
  23.6 0.1 pad_maximum_fusion
  23.7 0.0 copy-done
  23.8 0.0 copy-done.2
  23.8 0.6 fusion.25
  24.4 0.1 pad_maximum_fusion.1
  24.6 18.3 %all_to_all.50 = f32[32,1,448]{2,1,0:T(1,128)S(1)} all-to-all(f32[32,1,448]{2,1,0:T(1,128)S(1)} %all_to_all.33), channel_id=1, replica_groups=mesh['cells'=32,'genes'=16] {'cells'}, dimensions={0} | all-to-all | bytes 114688 | tf_op jit(solution)/shard_map/all_to_all | solution.py:22
  42.9 0.1 reduce_sum.148
  42.9 0.1 slice.49
  43.0 0.1 reshape.102
  43.1 0.1 reduce_sum.149
  43.2 0.1 subtract_convert_fusion.2
  43.3 0.1 pad_maximum_fusion.5
  43.4 0.1 subtract_convert_fusion
  43.5 21.3 %all_to_all.51 = bf16[16,64,256]{2,1,0:T(8,128)(2,1)S(1)} all-to-all(bf16[16,64,256]{2,1,0:T(8,128)(2,1)S(1)} %bitcast.19), channel_id=1, replica_groups=mesh['cells'=32,'genes'=16] {'genes'}, dimensions={0} | all-to-all | bytes 1048576 | tf_op jit(solution)/shard_map/all_to_all | solution.py:22
  64.7 0.1 convert_reduce_fusion
  64.8 0.0 copy-start.3
  64.8 0.1 multiply_reduce_fusion
  64.9 0.1 multiply_convert_fusion
  65.0 15.9 %all_gather.6 = bf16[1024,256]{1,0:T(8,128)(2,1)S(1)} all-gather(bf16[64,256]{1,0:T(8,128)(2,1)S(1)} %multiply_convert_fusion), channel_id=1, replica_groups=mesh['cells'=32,'genes'=16] {'genes'}, dimensions={0}, use_global_device_ids=true | all-gather | bytes 557056 | tf_op jit(solution)/shard_map/all_gather | solution.py:30
  80.9 0.2 fusion.28
  81.2 11.9 %all_to_all.52 = f32[32,2,256]{2,1,0:T(2,128)S(1)} all-to-all(f32[32,2,256]{2,1,0:T(2,128)S(1)} %reshape.103), channel_id=1, replica_groups=mesh['cells'=32,'genes'=16] {'cells'}, dimensions={0} | all-to-all | bytes 131072 | tf_op jit(solution)/shard_map/all_to_all | solution.py:22
  93.2 0.1 multiply_reduce_fusion.2
  93.3 0.1 multiply_convert_fusion.2
  93.5 11.7 %all_to_all.53 = bf16[32,2,384]{2,1,0:T(2,128)(2,1)S(1)} all-to-all(bf16[32,2,384]{2,1,0:T(2,128)(2,1)S(1)} %broadcast_in_dim.15), channel_id=1, replica_groups=mesh['cells'=32,'genes'=16] {'cells'}, dimensions={0} | all-to-all | bytes 98304 | tf_op jit(solution)/shard_map/all_to_all | solution.py:22
  105.2 0.0 copy-done.3
  105.2 0.3 fusion.7
  105.5 0.2 fusion.26
  105.8 15.2 %all_to_all.54 = f32[16,1,1024]{2,1,0:T(1,128)S(1)} all-to-all(f32[16,1,1024]{2,1,0:T(1,128)S(1)} %broadcast_in_dim.16), channel_id=1, replica_groups=mesh['cells'=32,'genes'=16] {'genes'}, dimensions={0} | all-to-all | bytes 131072 | tf_op jit(solution)/shard_map/all_to_all | solution.py:22
  120.9 0.1 reduce_sum.155
  121.0 0.2 fusion.8
  121.2 0.1 reshape.105
  121.3 12.5 %all_to_all.55 = f32[32,2,320]{2,1,0:T(2,128)S(1)} all-to-all(f32[32,2,320]{2,1,0:T(2,128)S(1)} %reshape.105), channel_id=1, replica_groups=mesh['cells'=32,'genes'=16] {'cells'}, dimensions={0} | all-to-all | bytes 163840 | tf_op jit(solution)/shard_map/all_to_all | solution.py:22
  133.7 0.1 reduce_sum.156
  133.8 0.1 multiply_reduce_fusion.1
  133.9 0.1 slice_reduce_fusion.1
  134.0 0.1 multiply_convert_fusion.1
  134.1 0.1 subtract_convert_fusion.1
  134.2 0.1 pad_maximum_fusion.4
  134.3 11.7 %all_to_all.56 = bf16[32,2,384]{2,1,0:T(2,128)(2,1)S(1)} all-to-all(bf16[32,2,384]{2,1,0:T(2,128)(2,1)S(1)} %broadcast_in_dim.17), channel_id=1, replica_groups=mesh['cells'=32,'genes'=16] {'cells'}, dimensions={0} | all-to-all | bytes 98304 | tf_op jit(solution)/shard_map/all_to_all | solution.py:22
  146.1 19.2 %all_gather.7 = bf16[1024,384]{1,0:T(8,128)(2,1)S(1)} all-gather(bf16[64,384]{1,0:T(8,128)(2,1)S(1)} %reshape.106), channel_id=1, replica_groups=mesh['cells'=32,'genes'=16] {'genes'}, dimensions={0}, use_global_device_ids=true | all-gather | bytes 835584 | tf_op jit(solution)/shard_map/all_gather | solution.py:30
  165.3 0.0 copy-start.1
  165.4 0.3 fusion.3
  165.7 0.3 fusion.27
  166.0 0.8 broadcast_divide_fusion
  166.8 0.0 copy-done.1
  (21 shorter events, 0.4 us)
Async XLA Ops:
  0.6 23.1 %copy-start = (bf16[256,256]{1,0:T(8,128)(2,1)S(1)}, bf16[256,256]{1,0:T(8,128)(2,1)}, u32[]{:S(2)}) copy-start(bf16[256,256]{1,0:T(8,128)(2,1)} %param.7) | copy-start | bytes 393220
  0.6 1.5 copy-start.4
  0.7 1.5 copy-start.5
  2.2 21.6 %copy-start.2 = (s32[1024,256]{1,0:T(8,128)S(1)}, s32[1024,256]{1,0:T(8,128)}, u32[]{:S(2)}) copy-start(s32[1024,256]{1,0:T(8,128)} %param.4) | copy-start | bytes 3145732
  64.8 40.4 %copy-start.3 = (f32[64,256]{1,0:T(8,128)}, f32[64,256]{1,0:T(8,128)S(1)}, u32[]{:S(2)}) copy-start(f32[64,256]{1,0:T(8,128)S(1)} %convert_reduce_fusion) | copy-start | bytes 196612
  165.3 1.4 copy-start.1

commit v3 on v2

v3 whole, which is shorter than its diff:
```python
import jax
import jax.numpy as jnp
from jax import lax
from jax.sharding import PartitionSpec as P

K = 1024
B = 64
ITERS = 2
CELL_AXIS = "cells"
GENE_AXIS = "genes"

epsilon = 1e-06
cluster_spread = 0.1

f32 = jnp.float32
bf16 = jnp.bfloat16
trailing = (((1,), (1,)), ((), ()))
together = lax.optimization_barrier


def exchange(blocks, axis):
    return lax.all_to_all(blocks, axis, 0, 0, tiled=False)


def share(block, axis):
    return exchange(jnp.broadcast_to(block[None], (lax.axis_size(axis),) + block.shape), axis)


def gather(block, axis):
    return lax.all_gather(block, axis, tiled=True)


def dot(left, right):
    return jnp.dot(left, right, preferred_element_type=f32)


def dot_rows(left, right):
    return lax.dot_general(left, right, trailing, preferred_element_type=f32)


def hot_columns(labels, count):
    return (labels[None, :] == jnp.arange(count, dtype=f32)[:, None]).astype(bf16)


def halves(value):
    high = value.astype(bf16)
    return high, (value - high.astype(f32)).astype(bf16)


def unit(rows):
    scaled = rows * lax.rsqrt(jnp.sum(rows * rows, axis=1, keepdims=True) + epsilon)
    return scaled.astype(bf16)


def penalty_halves(observed, batch_total, total_cells):
    mass = jnp.sum(observed, axis=1, keepdims=True)
    ratio = (mass * batch_total / total_cells + 1.0) / (observed + 1.0)
    return jnp.concatenate(halves(ratio * ratio), axis=1)


def weigh(similarity, lookup):
    distance = 2.0 - 2.0 * similarity
    return jnp.exp(-distance / cluster_spread) * lookup


def per_device(counts, batch, seeds, loadings):
    n_cells, n_genes = lax.axis_size(CELL_AXIS), lax.axis_size(GENE_AXIS)
    group, own = counts.shape[0], batch.shape[0]
    total_cells = group * n_cells
    width = loadings.shape[1]
    mine = K // n_genes
    piece = mine // n_cells

    values = counts.astype(f32)
    own_hot = (batch == jnp.arange(B, dtype=jnp.int32)[None, :]).astype(f32)
    own_twice = jnp.concatenate([own_hot, own_hot], axis=1).astype(bf16)
    first = (lax.axis_index(GENE_AXIS) * mine).astype(f32)
    packet = jnp.concatenate(
        [
            jnp.sum(values, axis=1),
            batch[:, 0].astype(f32),
            seeds[:, 0].astype(f32),
            jnp.sum(own_hot, axis=0),
        ]
    )
    packet, own_twice, first = together((packet, own_twice, first))
    packets = share(packet, GENE_AXIS)
    depth_total = jnp.sum(packets[:, :group], axis=0)
    at = group
    group_batch = packets[:, at : at + own].reshape(group)
    group_seeds = packets[:, at + own : at + 2 * own].reshape(group)
    group_labels = jnp.sum(packets[:, at + 2 * own :], axis=0)

    logged = jnp.log1p(10000.0 * values / depth_total[:, None]).astype(bf16)
    partial = dot(logged, loadings)

    batch_hot = hot_columns(group_batch, B)
    assign = hot_columns(group_seeds - first, mine)
    first_observed = dot_rows(assign, batch_hot)

    block_mean = jnp.sum(partial, axis=0) / group
    high, low = halves(block_mean[None])
    beside = jnp.concatenate([high] * 4 + [low] * 4, axis=0)
    spread = jnp.concatenate(
        [
            (partial - block_mean[None]).astype(bf16).reshape(n_genes, own, width),
            jnp.broadcast_to(beside[None], (n_genes, 8, width)),
        ],
        axis=1,
    )
    batch_twice = jnp.concatenate([batch_hot, batch_hot], axis=0)
    first_observed = first_observed.reshape(n_cells, piece * B)
    spread, batch_hot, batch_twice, assign, first_observed = together(
        (spread, batch_hot, batch_twice, assign, first_observed)
    )
    shares = exchange(spread, GENE_AXIS).astype(f32)
    about = jnp.sum(shares[:, :own], axis=0)
    group_mean = jnp.sum(shares[:, own] + shares[:, own + 4], axis=0)

    everyone = jnp.concatenate([group_mean, group_labels])
    packet = jnp.concatenate(
        [
            jnp.broadcast_to(everyone[None], (n_cells, width + B)),
            first_observed,
        ],
        axis=1,
    )
    about_low = about.astype(bf16)
    packet, about_low, about = together((packet, about_low, about))
    packets = exchange(packet, CELL_AXIS)
    group_about = gather(about_low, GENE_AXIS)
    arrived = jnp.sum(packets, axis=0)
    shift = (group_mean - arrived[:width] / n_cells)[None]
    batch_total = arrived[width : width + B][None]
    observed = arrived[width + B :].reshape(piece, B)
    embedding = about + shift
    own_rows = unit(embedding)
    unit_rows = unit(group_about.astype(f32) + shift)
    penalty = penalty_halves(observed, batch_total, total_cells)

    for iteration in range(ITERS):
        if iteration == 0:
            sums = dot(assign, unit_rows)
            sums, own_rows, penalty, embedding = together((sums, own_rows, penalty, embedding))
            sums = jnp.sum(exchange(sums.reshape(n_cells, piece, width), CELL_AXIS), axis=0)
        else:
            weights = weigh(
                dot_rows(rows[:, :width], unit_rows), dot(rows[:, width:], batch_twice)
            )
            norm = jnp.sum(share(jnp.sum(weights, axis=0), GENE_AXIS), axis=0)
            rounded = (weights / norm[None, :]).astype(bf16)
            sums = jnp.concatenate(
                [dot(rounded, unit_rows), dot_rows(rounded, batch_hot)], axis=1
            )
            sums = jnp.sum(exchange(sums.reshape(n_cells, piece, width + B), CELL_AXIS), axis=0)
            penalty = penalty_halves(sums[:, width:], batch_total, total_cells)
            sums = sums[:, :width]
        rows = jnp.concatenate([unit(sums), penalty], axis=1)
        rows = share(rows, CELL_AXIS).reshape(mine, width + 2 * B)

    rows = gather(rows, GENE_AXIS)
    weights = weigh(dot_rows(own_rows, rows[:, :width]), dot_rows(own_twice, rows[:, width:]))
    assign = weights / jnp.sum(weights, axis=1, keepdims=True)
    return (embedding, assign, rows[:, :width])


def solution(mesh):
    placed = (
        P("cells", "genes"),
        P(("cells", "genes"), None),
        P(("cells", "genes"), None),
        P("genes", None),
    )
    return jax.shard_map(
        per_device,
        mesh=mesh,
        in_specs=placed,
        out_specs=(P(("cells", "genes"), None), P(("cells", "genes"), None), P()),
        check_vma=False,
    )
```

time: 167 us -> 168 us (level)
  blocking collectives: 157 us -> 146 us
  starting transfers between devices: 0 us -> 9.67 us
  other arithmetic: 4.9 us -> 6.79 us
    all_to_all x8 -> x7, blocking collectives: 122 us -> 110 us  [exchange(): return lax.all_to_all(blocks, axis, 0, 0, tiled=False)]
    all_to_all x0 -> x1, starting transfers between devices: none -> 9.67 us  [exchange(): return lax.all_to_all(blocks, axis, 0, 0, tiled=False)]
  transfers between devices with their start and end apart: 0 -> 1, of which waited for: 0 -> 0; matrix products, arithmetic and copies ran while one was open for 0% -> 0% of each run, Pallas kernels for 0% -> 0%
where the time goes in v3:
time: 168 us; the launch traced here: 167 us
  blocking collectives  146 us (87%)
  starting transfers between devices  9.67 us (6%)
  other arithmetic  6.79 us (4%)
  matrix products  2.88 us (2%)
    all_to_all x7, blocking collectives, exchange(): return lax.all_to_all(blocks, axis, 0, 0, tiled=False)  110 us
    all_gather x2, blocking collectives, gather(): return lax.all_gather(block, axis, tiled=True)  35.9 us
    all_to_all x1, starting transfers between devices, exchange(): return lax.all_to_all(blocks, axis, 0, 0, tiled=False)  9.67 us
  transfers between devices with their start and end apart: 1, of which 0 were waited for; matrix products, arithmetic and copies ran while one was open for 0% of the time, Pallas kernels for 0%

profile of v3, /device:TPU:1, one launch (start us, length us, event | category | flops | bytes accessed | tf_op | source)
XLA Modules:
  0.0 167.5 jit_solution(4379805164215635771)
XLA Ops:
  0.6 0.0 copy-start
  0.6 0.0 copy-start.2
  0.7 0.8 convert_reduce_fusion.1
  1.5 0.7 convert_convert_fusion
  2.2 0.7 convert_bitcast_fusion
  2.9 1.4 convert_reduce_fusion
  4.4 0.1 pad_maximum_fusion.4
  4.4 0.1 concatenate.34
  4.6 19.7 %all_to_all.49 = f32[16,1,1216]{2,1,0:T(1,128)S(1)} all-to-all(f32[16,1,1216]{2,1,0:T(1,128)S(1)} %broadcast_in_dim.12), channel_id=1, replica_groups=mesh['cells'=32,'genes'=16] {'genes'}, dimensions={0} | all-to-all | bytes 155648 | tf_op jit(solution)/shard_map/all_to_all | solution.py:22
  24.3 0.1 slice_reduce_fusion.2
  24.4 0.1 sub.52
  24.5 0.1 eq.44
  24.6 0.2 fusion.10
  24.8 0.0 copy-done
  24.8 0.0 copy-done.2
  24.8 0.6 fusion.21
  25.5 0.1 reshape.127
  25.6 0.1 subtract_convert_fusion
  25.8 21.5 %all_to_all.50 = bf16[16,72,256]{2,1,0:T(8,128)(2,1)S(1)} all-to-all(bf16[16,72,256]{2,1,0:T(8,128)(2,1)S(1)} %pad_maximum_fusion), channel_id=1, replica_groups=mesh['cells'=32,'genes'=16] {'genes'}, dimensions={0} | all-to-all | bytes 1179648 | tf_op jit(solution)/shard_map/all_to_all | solution.py:22
  47.3 0.1 convert_element_type.123
  47.4 0.1 slice_reduce_fusion
  47.5 0.1 pad_maximum_fusion.3
  47.6 0.7 all_to_all.34
  48.3 9.7 %all-to-all-start.2 = ((f32[32,1,448]{2,1,0:T(1,128)}), f32[32,1,448]{2,1,0:T(1,128)S(1)}, u32[]{:S(2)}, u32[]{:S(2)}) async-start(f32[32,1,448]{2,1,0:T(1,128)} %all_to_all.34), calls=%async_computation.2 | async-start | bytes 131072 | tf_op jit(solution)/shard_map/all_to_all | solution.py:22
  57.9 16.7 %all_gather.6 = bf16[1024,256]{1,0:T(8,128)(2,1)S(1)} all-gather(bf16[64,256]{1,0:T(8,128)(2,1)S(1)} %convert_element_type.124), channel_id=1, replica_groups=mesh['cells'=32,'genes'=16] {'genes'}, dimensions={0}, use_global_device_ids=true | all-gather | bytes 557056 | tf_op jit(solution)/shard_map/all_gather | solution.py:30
  74.6 0.0 all-to-all-done.2
  74.6 0.1 reduce_sum.178
  74.7 0.1 slice.65
  74.8 0.1 reshape.128
  74.9 0.1 reduce_sum.181
  75.0 0.1 multiply_reduce_fusion.1
  75.1 0.0 copy-start.3
  75.1 0.2 multiply_reduce_fusion
  75.3 0.1 subtract_convert_fusion.2
  75.4 0.1 pad_maximum_fusion.8
  75.5 0.1 multiply_convert_fusion.1
  75.6 0.4 fusion.20
  76.0 18.1 %all_to_all.51 = f32[32,2,256]{2,1,0:T(2,128)S(1)} all-to-all(f32[32,2,256]{2,1,0:T(2,128)S(1)} %reshape.129), channel_id=1, replica_groups=mesh['cells'=32,'genes'=16] {'cells'}, dimensions={0} | all-to-all | bytes 131072 | tf_op jit(solution)/shard_map/all_to_all | solution.py:22
  94.2 0.1 multiply_reduce_fusion.3
  94.3 0.1 multiply_convert_fusion.3
  94.4 11.9 %all_to_all.52 = bf16[32,2,384]{2,1,0:T(2,128)(2,1)S(1)} all-to-all(bf16[32,2,384]{2,1,0:T(2,128)(2,1)S(1)} %broadcast_in_dim.15), channel_id=1, replica_groups=mesh['cells'=32,'genes'=16] {'cells'}, dimensions={0} | all-to-all | bytes 98304 | tf_op jit(solution)/shard_map/all_to_all | solution.py:22
  106.3 0.4 fusion.7
  106.7 0.0 copy-done.3
  106.7 0.2 fusion.22
  107.0 14.3 %all_to_all.53 = f32[16,1,1024]{2,1,0:T(1,128)S(1)} all-to-all(f32[16,1,1024]{2,1,0:T(1,128)S(1)} %broadcast_in_dim.16), channel_id=1, replica_groups=mesh['cells'=32,'genes'=16] {'genes'}, dimensions={0} | all-to-all | bytes 131072 | tf_op jit(solution)/shard_map/all_to_all | solution.py:22
  121.2 0.1 reduce_sum.185
  121.3 0.4 fusion.19
  121.7 0.2 fusion.24
  121.9 0.1 reshape.131
  122.0 12.5 %all_to_all.54 = f32[32,2,320]{2,1,0:T(2,128)S(1)} all-to-all(f32[32,2,320]{2,1,0:T(2,128)S(1)} %reshape.131), channel_id=1, replica_groups=mesh['cells'=32,'genes'=16] {'cells'}, dimensions={0} | all-to-all | bytes 163840 | tf_op jit(solution)/shard_map/all_to_all | solution.py:22
  134.4 0.1 reduce_sum.186
  134.5 0.1 slice_reduce_fusion.3
  134.6 0.1 multiply_reduce_fusion.2
  134.7 0.1 subtract_convert_fusion.1
  134.8 0.1 multiply_convert_fusion.2
  134.9 0.1 pad_maximum_fusion.7
  135.0 11.7 %all_to_all.55 = bf16[32,2,384]{2,1,0:T(2,128)(2,1)S(1)} all-to-all(bf16[32,2,384]{2,1,0:T(2,128)(2,1)S(1)} %broadcast_in_dim.17), channel_id=1, replica_groups=mesh['cells'=32,'genes'=16] {'cells'}, dimensions={0} | all-to-all | bytes 98304 | tf_op jit(solution)/shard_map/all_to_all | solution.py:22
  146.7 19.2 %all_gather.7 = bf16[1024,384]{1,0:T(8,128)(2,1)S(1)} all-gather(bf16[64,384]{1,0:T(8,128)(2,1)S(1)} %reshape.132), channel_id=1, replica_groups=mesh['cells'=32,'genes'=16] {'genes'}, dimensions={0}, use_global_device_ids=true | all-gather | bytes 835584 | tf_op jit(solution)/shard_map/all_gather | solution.py:30
  166.0 0.0 copy-start.1
  166.0 0.3 fusion.3
  166.3 0.3 fusion.23
  166.6 0.8 broadcast_divide_fusion
  167.5 0.0 copy-done.1
  (32 shorter events, 0.7 us)
Async XLA Ops:
  0.6 24.2 %copy-start = (bf16[256,256]{1,0:T(8,128)(2,1)S(1)}, bf16[256,256]{1,0:T(8,128)(2,1)}, u32[]{:S(2)}) copy-start(bf16[256,256]{1,0:T(8,128)(2,1)} %param.7) | copy-start | bytes 393220
  0.6 24.2 %copy-start.2 = (s32[1024,256]{1,0:T(8,128)S(1)}, s32[1024,256]{1,0:T(8,128)}, u32[]{:S(2)}) copy-start(s32[1024,256]{1,0:T(8,128)} %param.4) | copy-start | bytes 3145732
  48.3 26.4 %all-to-all-start.2 = ((f32[32,1,448]{2,1,0:T(1,128)}), f32[32,1,448]{2,1,0:T(1,128)S(1)}, u32[]{:S(2)}, u32[]{:S(2)}) async-start(f32[32,1,448]{2,1,0:T(1,128)} %all_to_all.34), calls=%async_computation.2 | async-start | bytes 131072 | tf_op jit(solution)/shard_map/all_to_all | solution.py:22
  75.1 31.6 %copy-start.3 = (f32[64,256]{1,0:T(8,128)}, f32[64,256]{1,0:T(8,128)S(1)}, u32[]{:S(2)}) copy-start(f32[64,256]{1,0:T(8,128)S(1)} %get-tuple-element.15) | copy-start | bytes 196612
  166.0 1.4 copy-start.1

commit v4 on v3

--- a/solution.py
+++ b/solution.py
@@ -72,76 +72,50 @@
     piece = mine // n_cells
 
     values = counts.astype(f32)
-    own_hot = (batch == jnp.arange(B, dtype=jnp.int32)[None, :]).astype(f32)
-    own_twice = jnp.concatenate([own_hot, own_hot], axis=1).astype(bf16)
+    shares = dot_rows(jnp.ones((8, counts.shape[1]), bf16), counts.astype(bf16))
+    packet = jnp.concatenate([shares[0], batch[:, 0].astype(f32), seeds[:, 0].astype(f32)])
+    own_hot = (batch == jnp.arange(B, dtype=jnp.int32)[None, :]).astype(bf16)
+    own_twice = jnp.concatenate([own_hot, own_hot], axis=1)
     first = (lax.axis_index(GENE_AXIS) * mine).astype(f32)
-    packet = jnp.concatenate(
-        [
-            jnp.sum(values, axis=1),
-            batch[:, 0].astype(f32),
-            seeds[:, 0].astype(f32),
-            jnp.sum(own_hot, axis=0),
-        ]
-    )
     packet, own_twice, first = together((packet, own_twice, first))
     packets = share(packet, GENE_AXIS)
     depth_total = jnp.sum(packets[:, :group], axis=0)
-    at = group
-    group_batch = packets[:, at : at + own].reshape(group)
-    group_seeds = packets[:, at + own : at + 2 * own].reshape(group)
-    group_labels = jnp.sum(packets[:, at + 2 * own :], axis=0)
+    group_batch = packets[:, group : group + own].reshape(group)
+    group_seeds = packets[:, group + own :].reshape(group)
 
     logged = jnp.log1p(10000.0 * values / depth_total[:, None]).astype(bf16)
     partial = dot(logged, loadings)
 
     batch_hot = hot_columns(group_batch, B)
+    batch_twice = jnp.concatenate([batch_hot, batch_hot], axis=0)
     assign = hot_columns(group_seeds - first, mine)
     first_observed = dot_rows(assign, batch_hot)
+    group_labels = dot_rows(jnp.ones((8, group), bf16), batch_hot)[0]
 
-    block_mean = jnp.sum(partial, axis=0) / group
-    high, low = halves(block_mean[None])
-    beside = jnp.concatenate([high] * 4 + [low] * 4, axis=0)
-    spread = jnp.concatenate(
+    everyone = jnp.concatenate([jnp.sum(partial, axis=0), group_labels])
+    packet = jnp.concatenate(
         [
-            (partial - block_mean[None]).astype(bf16).reshape(n_genes, own, width),
-            jnp.broadcast_to(beside[None], (n_genes, 8, width)),
+            jnp.broadcast_to(everyone[None], (n_cells, width + B)),
+            first_observed.reshape(n_cells, piece * B),
         ],
         axis=1,
     )
-    batch_twice = jnp.concatenate([batch_hot, batch_hot], axis=0)
-    first_observed = first_observed.reshape(n_cells, piece * B)
-    spread, batch_hot, batch_twice, assign, first_observed = together(
-        (spread, batch_hot, batch_twice, assign, first_observed)
-    )
-    shares = exchange(spread, GENE_AXIS).astype(f32)
-    about = jnp.sum(shares[:, :own], axis=0)
-    group_mean = jnp.sum(shares[:, own] + shares[:, own + 4], axis=0)
-
-    everyone = jnp.concatenate([group_mean, group_labels])
-    packet = jnp.concatenate(
-        [
-            jnp.broadcast_to(everyone[None], (n_cells, width + B)),
-            first_observed,
-        ],
-        axis=1,
-    )
-    about_low = about.astype(bf16)
-    packet, about_low, about = together((packet, about_low, about))
-    packets = exchange(packet, CELL_AXIS)
-    group_about = gather(about_low, GENE_AXIS)
-    arrived = jnp.sum(packets, axis=0)
-    shift = (group_mean - arrived[:width] / n_cells)[None]
+    packet, batch_hot, batch_twice, assign = together((packet, batch_hot, batch_twice, assign))
+    arrived = jnp.sum(exchange(packet, CELL_AXIS), axis=0)
+    center = arrived[:width] / total_cells
     batch_total = arrived[width : width + B][None]
     observed = arrived[width + B :].reshape(piece, B)
-    embedding = about + shift
+    penalty = penalty_halves(observed, batch_total, total_cells)
+
+    centred = (partial - center[None]).astype(bf16).reshape(n_genes, own, width)
+    centred, penalty, batch_total = together((centred, penalty, batch_total))
+    embedding = jnp.sum(exchange(centred, GENE_AXIS).astype(f32), axis=0)
     own_rows = unit(embedding)
-    unit_rows = unit(group_about.astype(f32) + shift)
-    penalty = penalty_halves(observed, batch_total, total_cells)
+    unit_rows = gather(own_rows, GENE_AXIS)
 
     for iteration in range(ITERS):
         if iteration == 0:
             sums = dot(assign, unit_rows)
-            sums, own_rows, penalty, embedding = together((sums, own_rows, penalty, embedding))
             sums = jnp.sum(exchange(sums.reshape(n_cells, piece, width), CELL_AXIS), axis=0)
         else:
             weights = weigh(

time: 168 us -> 167 us (level)
  blocking collectives: 146 us -> 157 us
  starting transfers between devices: 9.67 us -> 0 us
  other arithmetic: 6.79 us -> 2.77 us
    all_to_all x7 -> x8, blocking collectives: 110 us -> 122 us  [exchange(): return lax.all_to_all(blocks, axis, 0, 0, tiled=False)]
    all_to_all x1 -> x0, starting transfers between devices: 9.67 us -> none  [exchange(): return lax.all_to_all(blocks, axis, 0, 0, tiled=False)]
    reduce_sum x6 -> x2, other arithmetic: 2.53 us -> 0.14 us  [the longest x1 0.08 us: per_device(): embedding = jnp.sum(exchange(centred, GENE_AXIS).astype(f32), axis=0)]
  transfers between devices with their start and end apart: 1 -> 0, of which waited for: 0 -> 0; matrix products, arithmetic and copies ran while one was open for 0% -> 0% of each run, Pallas kernels for 0% -> 0%
where the time goes in v4:
time: 167 us
  blocking collectives  157 us (94%)
  matrix products  4.24 us (3%)
  other arithmetic  2.77 us (2%)
    all_to_all x8, blocking collectives, exchange(): return lax.all_to_all(blocks, axis, 0, 0, tiled=False)  122 us
    all_gather x2, blocking collectives, gather(): return lax.all_gather(block, axis, tiled=True)  35.1 us

profile of v4, /device:TPU:1, one launch (start us, length us, event | category | flops | bytes accessed | tf_op | source)
XLA Modules:
  0.0 166.6 jit_solution(4893755947099377874)
XLA Ops:
  0.6 0.0 copy-start
  0.6 0.0 copy-start.4
  0.7 0.0 copy-start.5
  0.7 0.0 copy-start.2
  0.7 1.6 fusion.8
  2.2 0.0 copy-done.4
  2.2 0.0 copy-done.5
  2.3 0.1 iota_compare_fusion.5
  2.3 0.1 add_convert_fusion
  2.4 0.1 concatenate.30
  2.5 19.6 %all_to_all.49 = f32[16,1,1152]{2,1,0:T(1,128)S(1)} all-to-all(f32[16,1,1152]{2,1,0:T(1,128)S(1)} %broadcast_in_dim.17), channel_id=1, replica_groups=mesh['cells'=32,'genes'=16] {'genes'}, dimensions={0} | all-to-all | bytes 147456 | tf_op jit(solution)/shard_map/all_to_all | solution.py:22
  22.1 0.1 fusion.25
  22.2 0.1 eq.44
  22.3 0.2 convolution_bitcast_fusion
  22.5 0.1 sub.35
  22.6 0.2 fusion.13
  22.8 0.1 reshape.87
  22.9 0.0 copy-done
  22.9 0.0 copy-done.2
  22.9 0.6 fusion.26
  23.6 0.1 pad_maximum_fusion.2
  23.7 18.3 %all_to_all.50 = f32[32,1,448]{2,1,0:T(1,128)S(1)} all-to-all(f32[32,1,448]{2,1,0:T(1,128)S(1)} %all_to_all.33), channel_id=1, replica_groups=mesh['cells'=32,'genes'=16] {'cells'}, dimensions={0} | all-to-all | bytes 114688 | tf_op jit(solution)/shard_map/all_to_all | solution.py:22
  42.0 0.1 reduce_sum.128
  42.1 0.1 slice.57
  42.2 0.1 reshape.89
  42.2 0.1 reduce_sum.129
  42.4 0.1 subtract_convert_fusion.2
  42.4 0.1 pad_maximum_fusion.6
  42.5 0.1 subtract_convert_fusion
  42.6 21.3 %all_to_all.51 = bf16[16,64,256]{2,1,0:T(8,128)(2,1)S(1)} all-to-all(bf16[16,64,256]{2,1,0:T(8,128)(2,1)S(1)} %bitcast.26), channel_id=1, replica_groups=mesh['cells'=32,'genes'=16] {'genes'}, dimensions={0} | all-to-all | bytes 1048576 | tf_op jit(solution)/shard_map/all_to_all | solution.py:22
  63.9 0.1 convert_reduce_fusion
  64.0 0.0 copy-start.3
  64.0 0.1 multiply_reduce_fusion
  64.1 0.1 multiply_convert_fusion
  64.2 0.4 copy-done.3
  64.6 15.9 %all_gather.6 = bf16[1024,256]{1,0:T(8,128)(2,1)S(1)} all-gather(bf16[64,256]{1,0:T(8,128)(2,1)S(1)} %multiply_convert_fusion), channel_id=1, replica_groups=mesh['cells'=32,'genes'=16] {'genes'}, dimensions={0}, use_global_device_ids=true | all-gather | bytes 557056 | tf_op jit(solution)/shard_map/all_gather | solution.py:30
  80.5 0.2 fusion.29
  80.7 11.9 %all_to_all.52 = f32[32,2,256]{2,1,0:T(2,128)S(1)} all-to-all(f32[32,2,256]{2,1,0:T(2,128)S(1)} %reshape.90), channel_id=1, replica_groups=mesh['cells'=32,'genes'=16] {'cells'}, dimensions={0} | all-to-all | bytes 131072 | tf_op jit(solution)/shard_map/all_to_all | solution.py:22
  92.7 0.1 multiply_reduce_fusion.2
  92.8 0.1 multiply_convert_fusion.2
  93.0 11.7 %all_to_all.53 = bf16[32,2,384]{2,1,0:T(2,128)(2,1)S(1)} all-to-all(bf16[32,2,384]{2,1,0:T(2,128)(2,1)S(1)} %broadcast_in_dim.21), channel_id=1, replica_groups=mesh['cells'=32,'genes'=16] {'cells'}, dimensions={0} | all-to-all | bytes 98304 | tf_op jit(solution)/shard_map/all_to_all | solution.py:22
  104.7 0.3 fusion.7
  105.0 0.2 fusion.27
  105.2 15.1 %all_to_all.54 = f32[16,1,1024]{2,1,0:T(1,128)S(1)} all-to-all(f32[16,1,1024]{2,1,0:T(1,128)S(1)} %broadcast_in_dim.22), channel_id=1, replica_groups=mesh['cells'=32,'genes'=16] {'genes'}, dimensions={0} | all-to-all | bytes 131072 | tf_op jit(solution)/shard_map/all_to_all | solution.py:22
  120.4 0.1 reduce_sum.135
  120.5 0.2 fusion.30
  120.7 0.2 fusion.31
  120.9 0.1 reshape.92
  120.9 12.5 %all_to_all.55 = f32[32,2,320]{2,1,0:T(2,128)S(1)} all-to-all(f32[32,2,320]{2,1,0:T(2,128)S(1)} %reshape.92), channel_id=1, replica_groups=mesh['cells'=32,'genes'=16] {'cells'}, dimensions={0} | all-to-all | bytes 163840 | tf_op jit(solution)/shard_map/all_to_all | solution.py:22
  133.4 0.1 reduce_sum.136
  133.5 0.1 multiply_reduce_fusion.1
  133.6 0.1 slice_reduce_fusion.1
  133.7 0.1 multiply_convert_fusion.1
  133.8 0.1 subtract_convert_fusion.1
  133.9 0.1 pad_maximum_fusion.5
  134.0 11.7 %all_to_all.56 = bf16[32,2,384]{2,1,0:T(2,128)(2,1)S(1)} all-to-all(bf16[32,2,384]{2,1,0:T(2,128)(2,1)S(1)} %broadcast_in_dim.23), channel_id=1, replica_groups=mesh['cells'=32,'genes'=16] {'cells'}, dimensions={0} | all-to-all | bytes 98304 | tf_op jit(solution)/shard_map/all_to_all | solution.py:22
  145.7 19.2 %all_gather.7 = bf16[1024,384]{1,0:T(8,128)(2,1)S(1)} all-gather(bf16[64,384]{1,0:T(8,128)(2,1)S(1)} %reshape.93), channel_id=1, replica_groups=mesh['cells'=32,'genes'=16] {'genes'}, dimensions={0}, use_global_device_ids=true | all-gather | bytes 835584 | tf_op jit(solution)/shard_map/all_gather | solution.py:30
  165.0 0.0 copy-start.1
  165.0 0.3 fusion.3
  165.3 0.3 fusion.28
  165.6 0.2 copy-done.1
  165.8 0.8 broadcast_divide_fusion
  (25 shorter events, 0.6 us)
Async XLA Ops:
  0.6 22.3 %copy-start = (bf16[256,256]{1,0:T(8,128)(2,1)S(1)}, bf16[256,256]{1,0:T(8,128)(2,1)}, u32[]{:S(2)}) copy-start(bf16[256,256]{1,0:T(8,128)(2,1)} %param.7) | copy-start | bytes 393220
  0.6 1.6 copy-start.4
  0.7 1.6 copy-start.5
  0.7 22.2 %copy-start.2 = (s32[1024,256]{1,0:T(8,128)S(1)}, s32[1024,256]{1,0:T(8,128)}, u32[]{:S(2)}) copy-start(s32[1024,256]{1,0:T(8,128)} %param.4) | copy-start | bytes 3145732
  64.0 0.6 copy-start.3
  165.0 0.8 copy-start.1

commit v5 on v4

--- a/solution.py
+++ b/solution.py
@@ -7,7 +7,9 @@
 B = 64
 ITERS = 2
 CELL_AXIS = "cells"
-GENE_AXIS = "genes"
+Z_AXIS = "z"
+CORE_AXIS = "core"
+GENE_AXIS = (Z_AXIS, CORE_AXIS)
 
 epsilon = 1e-06
 cluster_spread = 0.1
@@ -65,6 +67,7 @@
 
 def per_device(counts, batch, seeds, loadings):
     n_cells, n_genes = lax.axis_size(CELL_AXIS), lax.axis_size(GENE_AXIS)
+    n_z, n_core = lax.axis_size(Z_AXIS), lax.axis_size(CORE_AXIS)
     group, own = counts.shape[0], batch.shape[0]
     total_cells = group * n_cells
     width = loadings.shape[1]
@@ -77,11 +80,13 @@
     own_hot = (batch == jnp.arange(B, dtype=jnp.int32)[None, :]).astype(bf16)
     own_twice = jnp.concatenate([own_hot, own_hot], axis=1)
     first = (lax.axis_index(GENE_AXIS) * mine).astype(f32)
-    packet, own_twice, first = together((packet, own_twice, first))
+    even = lax.axis_index(CORE_AXIS) == 0
+    packet, own_twice, first, even = together((packet, own_twice, first, even))
     packets = share(packet, GENE_AXIS)
     depth_total = jnp.sum(packets[:, :group], axis=0)
-    group_batch = packets[:, group : group + own].reshape(group)
-    group_seeds = packets[:, group + own :].reshape(group)
+    labels = packets[:, group:].reshape(n_z, n_core, 2, own).transpose(2, 1, 0, 3)
+    group_batch = labels[0].reshape(group)
+    group_seeds = labels[1].reshape(group)
 
     logged = jnp.log1p(10000.0 * values / depth_total[:, None]).astype(bf16)
     partial = dot(logged, loadings)
@@ -107,11 +112,15 @@
     observed = arrived[width + B :].reshape(piece, B)
     penalty = penalty_halves(observed, batch_total, total_cells)
 
-    centred = (partial - center[None]).astype(bf16).reshape(n_genes, own, width)
-    centred, penalty, batch_total = together((centred, penalty, batch_total))
-    embedding = jnp.sum(exchange(centred, GENE_AXIS).astype(f32), axis=0)
+    centred = (partial - center[None]).reshape(n_z, n_core, own, width)
+    kept = jnp.where(even, centred[:, 0], centred[:, 1])
+    given = jnp.where(even, centred[:, 1], centred[:, 0]).astype(bf16)
+    given, kept, penalty, batch_total = together((given, kept, penalty, batch_total))
+    taken = lax.ppermute(given, CORE_AXIS, [(0, 1), (1, 0)])
+    pairs = (kept + taken.astype(f32)).astype(bf16)
+    embedding = jnp.sum(exchange(pairs, Z_AXIS).astype(f32), axis=0)
     own_rows = unit(embedding)
-    unit_rows = gather(own_rows, GENE_AXIS)
+    unit_rows = gather(share(own_rows, Z_AXIS).reshape(n_z * own, width), CORE_AXIS)
 
     for iteration in range(ITERS):
         if iteration == 0:
@@ -139,16 +148,16 @@
 
 
 def solution(mesh):
-    placed = (
-        P("cells", "genes"),
-        P(("cells", "genes"), None),
-        P(("cells", "genes"), None),
-        P("genes", None),
+    cells, genes = mesh.devices.shape
+    mesh = jax.sharding.Mesh(
+        mesh.devices.reshape(cells, genes // 2, 2), (CELL_AXIS, Z_AXIS, CORE_AXIS)
     )
+    owners = P((CELL_AXIS, Z_AXIS, CORE_AXIS), None)
+    placed = (P(CELL_AXIS, GENE_AXIS), owners, owners, P(GENE_AXIS, None))
     return jax.shard_map(
         per_device,
         mesh=mesh,
         in_specs=placed,
-        out_specs=(P(("cells", "genes"), None), P(("cells", "genes"), None), P()),
+        out_specs=(owners, owners, P()),
         check_vma=False,
     )

time: 167 us -> 164 us (0.982)
  blocking collectives: 157 us -> 150 us
  starting transfers between devices: 0 us -> 3.44 us
    all_gather x2, blocking collectives: 35.1 us -> 22.1 us  [gather(): return lax.all_gather(block, axis, tiled=True)]
    all_to_all x8 -> x9, blocking collectives: 122 us -> 128 us  [exchange(): return lax.all_to_all(blocks, axis, 0, 0, tiled=False)]
    ppermute x0 -> x1, starting transfers between devices: none -> 3.44 us  [per_device(): taken = lax.ppermute(given, CORE_AXIS, [(0, 1), (1, 0)])]
  transfers between devices with their start and end apart: 0 -> 1, of which waited for: 0 -> 1; matrix products, arithmetic and copies ran while one was open for 0% -> 0% of each run, Pallas kernels for 0% -> 0%
where the time goes in v5:
time: 164 us
  blocking collectives  150 us (91%)
  matrix products  4.17 us (3%)
  starting transfers between devices  3.44 us (2%)
  other arithmetic  2.83 us (2%)
    all_to_all x9, blocking collectives, exchange(): return lax.all_to_all(blocks, axis, 0, 0, tiled=False)  128 us
    all_gather x2, blocking collectives, gather(): return lax.all_gather(block, axis, tiled=True)  22.1 us
    ppermute x1, starting transfers between devices, per_device(): taken = lax.ppermute(given, CORE_AXIS, [(0, 1), (1, 0)])  3.44 us
  transfers between devices with their start and end apart: 1, of which 1 were waited for; matrix products, arithmetic and copies ran while one was open for 0% of the time, Pallas kernels for 0%

profile of v5, /device:TPU:1, one launch (start us, length us, event | category | flops | bytes accessed | tf_op | source)
XLA Modules:
  0.0 163.9 jit_solution(8825868455768249990)
XLA Ops:
  0.6 0.0 copy-start
  0.7 0.0 copy-start.4
  0.7 0.0 copy-start.5
  0.7 1.5 fusion.9
  2.2 0.0 copy-done.4
  2.2 0.0 copy-done.5
  2.2 0.1 iota_compare_fusion.5
  2.3 0.1 add_convert_fusion.1
  2.4 0.1 concatenate.30
  2.5 19.6 %all_to_all.54 = f32[16,1,1152]{2,1,0:T(1,128)S(1)} all-to-all(f32[16,1,1152]{2,1,0:T(1,128)S(1)} %broadcast_in_dim.19), channel_id=1, replica_groups=mesh['cells'=32,'z'=8,'core'=2] {'z','core'}, dimensions={0} | all-to-all | bytes 147456 | tf_op jit(solution)/shard_map/all_to_all | solution.py:24
  22.1 0.1 reshape.113
  22.2 0.1 eq.48
  22.3 0.2 convolution_bitcast_fusion
  22.5 0.1 sub.35
  22.5 0.2 fusion.15
  22.8 0.1 reshape.114
  22.9 0.6 fusion.28
  23.6 0.1 pad_maximum_fusion.2
  23.7 18.3 %all_to_all.55 = f32[32,1,448]{2,1,0:T(1,128)S(1)} all-to-all(f32[32,1,448]{2,1,0:T(1,128)S(1)} %all_to_all.36), channel_id=1, replica_groups=mesh['cells'=32,'z'=8,'core'=2] {'cells'}, dimensions={0} | all-to-all | bytes 114688 | tf_op jit(solution)/shard_map/all_to_all | solution.py:24
  42.0 0.1 reduce_sum.128
  42.0 0.1 slice.71
  42.1 0.1 broadcast_subtract_fusion
  42.2 0.1 select_bitcast_fusion
  42.3 0.1 fusion.12
  42.3 0.1 reshape.116
  42.4 0.1 reduce_sum.129
  42.6 0.1 subtract_convert_fusion.1
  42.6 0.1 pad_maximum_fusion.6
  42.7 3.4 %collective-permute-start = (bf16[8,64,256]{2,1,0:T(8,128)(2,1)S(1)}, bf16[8,64,256]{2,1,0:T(8,128)(2,1)S(1)}, u32[]{:S(2)}, u32[]{:S(2)}) collective-permute-start(bf16[8,64,256]{2,1,0:T(8,128)(2,1)S(1)} %fusion.12), channel_id=1, source_target_pairs={{0,1},{1,0},{2,3},{3,2},{4,5},{5,4},{6,7},{7,6},{8,9},{9,8},{10,11... | collective-permute-start | bytes 786440 | tf_op jit(solution)/shard_map/ppermute | solution.py:119
  46.1 1.1 collective-permute-done
  47.3 0.1 add_convert_fusion
  47.4 14.7 %all_to_all.56 = bf16[8,64,256]{2,1,0:T(8,128)(2,1)S(1)} all-to-all(bf16[8,64,256]{2,1,0:T(8,128)(2,1)S(1)} %add_convert_fusion), channel_id=1, replica_groups=mesh['cells'=32,'z'=8,'core'=2] {'z'}, dimensions={0} | all-to-all | bytes 524288 | tf_op jit(solution)/shard_map/all_to_all | solution.py:24
  62.1 0.0 copy-start.3
  62.1 0.1 multiply_reduce_fusion
  62.3 0.1 multiply_convert_fusion
  62.3 0.4 copy-done.3
  62.8 14.2 %all_to_all.57 = bf16[8,64,256]{2,1,0:T(8,128)(2,1)S(1)} all-to-all(bf16[8,64,256]{2,1,0:T(8,128)(2,1)S(1)} %broadcast_in_dim.23), channel_id=1, replica_groups=mesh['cells'=32,'z'=8,'core'=2] {'z'}, dimensions={0} | all-to-all | bytes 524288 | tf_op jit(solution)/shard_map/all_to_all | solution.py:24
  77.0 2.8 %all_gather.6 = bf16[1024,256]{1,0:T(8,128)(2,1)S(1)} all-gather(bf16[512,256]{1,0:T(8,128)(2,1)S(1)} %bitcast.54), channel_id=1, replica_groups=mesh['cells'=32,'z'=8,'core'=2] {'core'}, dimensions={0}, use_global_device_ids=true | all-gather | bytes 786432 | tf_op jit(solution)/shard_map/all_gather | solution.py:32
  79.8 0.2 fusion.31
  80.1 11.8 %all_to_all.58 = f32[32,2,256]{2,1,0:T(2,128)S(1)} all-to-all(f32[32,2,256]{2,1,0:T(2,128)S(1)} %reshape.118), channel_id=1, replica_groups=mesh['cells'=32,'z'=8,'core'=2] {'cells'}, dimensions={0} | all-to-all | bytes 131072 | tf_op jit(solution)/shard_map/all_to_all | solution.py:24
  91.9 0.1 multiply_reduce_fusion.2
  92.1 0.1 multiply_convert_fusion.2
  92.2 11.8 %all_to_all.59 = bf16[32,2,384]{2,1,0:T(2,128)(2,1)S(1)} all-to-all(bf16[32,2,384]{2,1,0:T(2,128)(2,1)S(1)} %broadcast_in_dim.24), channel_id=1, replica_groups=mesh['cells'=32,'z'=8,'core'=2] {'cells'}, dimensions={0} | all-to-all | bytes 98304 | tf_op jit(solution)/shard_map/all_to_all | solution.py:24
  104.0 0.3 fusion.7
  104.3 0.2 fusion.29
  104.5 13.1 %all_to_all.60 = f32[16,1,1024]{2,1,0:T(1,128)S(1)} all-to-all(f32[16,1,1024]{2,1,0:T(1,128)S(1)} %broadcast_in_dim.25), channel_id=1, replica_groups=mesh['cells'=32,'z'=8,'core'=2] {'z','core'}, dimensions={0} | all-to-all | bytes 131072 | tf_op jit(solution)/shard_map/all_to_all | solution.py:24
  117.6 0.1 reduce_sum.135
  117.7 0.2 fusion.32
  117.9 0.2 fusion.33
  118.1 0.1 reshape.120
  118.2 12.5 %all_to_all.61 = f32[32,2,320]{2,1,0:T(2,128)S(1)} all-to-all(f32[32,2,320]{2,1,0:T(2,128)S(1)} %reshape.120), channel_id=1, replica_groups=mesh['cells'=32,'z'=8,'core'=2] {'cells'}, dimensions={0} | all-to-all | bytes 163840 | tf_op jit(solution)/shard_map/all_to_all | solution.py:24
  130.7 0.1 reduce_sum.136
  130.7 0.1 multiply_reduce_fusion.1
  130.8 0.1 slice_reduce_fusion.1
  130.9 0.1 multiply_convert_fusion.1
  131.0 0.1 subtract_convert_fusion
  131.1 0.1 pad_maximum_fusion.5
  131.2 11.7 %all_to_all.62 = bf16[32,2,384]{2,1,0:T(2,128)(2,1)S(1)} all-to-all(bf16[32,2,384]{2,1,0:T(2,128)(2,1)S(1)} %broadcast_in_dim.26), channel_id=1, replica_groups=mesh['cells'=32,'z'=8,'core'=2] {'cells'}, dimensions={0} | all-to-all | bytes 98304 | tf_op jit(solution)/shard_map/all_to_all | solution.py:24
  142.9 19.3 %all_gather.7 = bf16[1024,384]{1,0:T(8,128)(2,1)S(1)} all-gather(bf16[64,384]{1,0:T(8,128)(2,1)S(1)} %reshape.121), channel_id=1, replica_groups=mesh['cells'=32,'z'=8,'core'=2] {'z','core'}, dimensions={0}, use_global_device_ids=true | all-gather | bytes 835584 | tf_op jit(solution)/shard_map/all_gather | solution.py:32
  162.3 0.0 copy-start.1
  162.3 0.3 fusion.3
  162.6 0.3 fusion.30
  162.9 0.2 copy-done.1
  163.1 0.8 broadcast_divide_fusion
  (33 shorter events, 0.6 us)
Async XLA Ops:
  0.6 22.2 %copy-start = (bf16[256,256]{1,0:T(8,128)(2,1)S(1)}, bf16[256,256]{1,0:T(8,128)(2,1)}, u32[]{:S(2)}) copy-start(bf16[256,256]{1,0:T(8,128)(2,1)} %param.7) | copy-start | bytes 393220
  0.7 1.5 copy-start.4
  0.7 1.5 copy-start.5
  2.2 20.7 %copy-start.2 = (s32[1024,256]{1,0:T(8,128)S(1)}, s32[1024,256]{1,0:T(8,128)}, u32[]{:S(2)}) copy-start(s32[1024,256]{1,0:T(8,128)} %param.4) | copy-start | bytes 3145732
  42.7 4.6 %collective-permute-start = (bf16[8,64,256]{2,1,0:T(8,128)(2,1)S(1)}, bf16[8,64,256]{2,1,0:T(8,128)(2,1)S(1)}, u32[]{:S(2)}, u32[]{:S(2)}) collective-permute-start(bf16[8,64,256]{2,1,0:T(8,128)(2,1)S(1)} %fusion.12), channel_id=1, source_target_pairs={{0,1},{1,0},{2,3},{3,2},{4,5},{5,4},{6,7},{7,6},{8,9},{9,8},{10,11... | collective-permute-start | bytes 786440 | tf_op jit(solution)/shard_map/ppermute | solution.py:119
  62.1 0.6 copy-start.3
  162.3 0.8 copy-start.1

commit v6 on v5

--- a/solution.py
+++ b/solution.py
@@ -6,7 +6,10 @@
 K = 1024
 B = 64
 ITERS = 2
-CELL_AXIS = "cells"
+X_SIZE = 4
+Y_AXIS = "y"
+X_AXIS = "x"
+CELL_AXIS = (Y_AXIS, X_AXIS)
 Z_AXIS = "z"
 CORE_AXIS = "core"
 GENE_AXIS = (Z_AXIS, CORE_AXIS)
@@ -60,6 +63,29 @@
     return jnp.concatenate(halves(ratio * ratio), axis=1)
 
 
+def added(blocks):
+    total = blocks[0].astype(f32)
+    for at in range(1, blocks.shape[0]):
+        total = total + blocks[at].astype(f32)
+    return total
+
+
+def folded(observed):
+    half = observed.shape[0] // 2
+    return jnp.concatenate([observed[:half], observed[half:]], axis=1).astype(bf16)
+
+
+def everywhere(sums, fold):
+    half, lanes = sums.shape[0] // 2, sums.shape[1] // 2
+    sums = sums.astype(bf16)
+    block = jnp.concatenate([sums[:, :lanes], sums[:, lanes:], fold], axis=0)
+    for axis in (Y_AXIS, X_AXIS):
+        block = added(share(block.astype(bf16), axis))
+    sums = jnp.concatenate([block[: 2 * half], block[2 * half : 4 * half]], axis=1)
+    observed = jnp.concatenate([block[4 * half :, :B], block[4 * half :, B:]], axis=0)
+    return sums, observed
+
+
 def weigh(similarity, lookup):
     distance = 2.0 - 2.0 * similarity
     return jnp.exp(-distance / cluster_spread) * lookup
@@ -72,7 +98,6 @@
     total_cells = group * n_cells
     width = loadings.shape[1]
     mine = K // n_genes
-    piece = mine // n_cells
 
     values = counts.astype(f32)
     shares = dot_rows(jnp.ones((8, counts.shape[1]), bf16), counts.astype(bf16))
@@ -94,28 +119,21 @@
     batch_hot = hot_columns(group_batch, B)
     batch_twice = jnp.concatenate([batch_hot, batch_hot], axis=0)
     assign = hot_columns(group_seeds - first, mine)
-    first_observed = dot_rows(assign, batch_hot)
+    first_fold = folded(dot_rows(assign, batch_hot))
     group_labels = dot_rows(jnp.ones((8, group), bf16), batch_hot)[0]
 
-    everyone = jnp.concatenate([jnp.sum(partial, axis=0), group_labels])
-    packet = jnp.concatenate(
-        [
-            jnp.broadcast_to(everyone[None], (n_cells, width + B)),
-            first_observed.reshape(n_cells, piece * B),
-        ],
-        axis=1,
+    packet = jnp.concatenate([jnp.sum(partial, axis=0), group_labels])
+    packet, batch_hot, batch_twice, assign, first_fold = together(
+        (packet, batch_hot, batch_twice, assign, first_fold)
     )
-    packet, batch_hot, batch_twice, assign = together((packet, batch_hot, batch_twice, assign))
-    arrived = jnp.sum(exchange(packet, CELL_AXIS), axis=0)
+    arrived = jnp.sum(share(packet, CELL_AXIS), axis=0)
     center = arrived[:width] / total_cells
-    batch_total = arrived[width : width + B][None]
-    observed = arrived[width + B :].reshape(piece, B)
-    penalty = penalty_halves(observed, batch_total, total_cells)
+    batch_total = arrived[width:][None]
 
     centred = (partial - center[None]).reshape(n_z, n_core, own, width)
     kept = jnp.where(even, centred[:, 0], centred[:, 1])
     given = jnp.where(even, centred[:, 1], centred[:, 0]).astype(bf16)
-    given, kept, penalty, batch_total = together((given, kept, penalty, batch_total))
+    given, kept, batch_total = together((given, kept, batch_total))
     taken = lax.ppermute(given, CORE_AXIS, [(0, 1), (1, 0)])
     pairs = (kept + taken.astype(f32)).astype(bf16)
     embedding = jnp.sum(exchange(pairs, Z_AXIS).astype(f32), axis=0)
@@ -124,22 +142,15 @@
 
     for iteration in range(ITERS):
         if iteration == 0:
-            sums = dot(assign, unit_rows)
-            sums = jnp.sum(exchange(sums.reshape(n_cells, piece, width), CELL_AXIS), axis=0)
+            sums, fold = dot(assign, unit_rows), first_fold
         else:
-            weights = weigh(
-                dot_rows(rows[:, :width], unit_rows), dot(rows[:, width:], batch_twice)
-            )
+            weights = weigh(dot_rows(rows[:, :width], unit_rows), dot(rows[:, width:], batch_twice))
             norm = jnp.sum(share(jnp.sum(weights, axis=0), GENE_AXIS), axis=0)
             rounded = (weights / norm[None, :]).astype(bf16)
-            sums = jnp.concatenate(
-                [dot(rounded, unit_rows), dot_rows(rounded, batch_hot)], axis=1
-            )
-            sums = jnp.sum(exchange(sums.reshape(n_cells, piece, width + B), CELL_AXIS), axis=0)
-            penalty = penalty_halves(sums[:, width:], batch_total, total_cells)
-            sums = sums[:, :width]
+            sums, fold = dot(rounded, unit_rows), folded(dot_rows(rounded, batch_hot))
+        sums, observed = everywhere(sums, fold)
+        penalty = penalty_halves(observed, batch_total, total_cells)
         rows = jnp.concatenate([unit(sums), penalty], axis=1)
-        rows = share(rows, CELL_AXIS).reshape(mine, width + 2 * B)
 
     rows = gather(rows, GENE_AXIS)
     weights = weigh(dot_rows(own_rows, rows[:, :width]), dot_rows(own_twice, rows[:, width:]))
@@ -150,9 +161,10 @@
 def solution(mesh):
     cells, genes = mesh.devices.shape
     mesh = jax.sharding.Mesh(
-        mesh.devices.reshape(cells, genes // 2, 2), (CELL_AXIS, Z_AXIS, CORE_AXIS)
+        mesh.devices.reshape(cells // X_SIZE, X_SIZE, genes // 2, 2),
+        (Y_AXIS, X_AXIS, Z_AXIS, CORE_AXIS),
     )
-    owners = P((CELL_AXIS, Z_AXIS, CORE_AXIS), None)
+    owners = P((Y_AXIS, X_AXIS, Z_AXIS, CORE_AXIS), None)
     placed = (P(CELL_AXIS, GENE_AXIS), owners, owners, P(GENE_AXIS, None))
     return jax.shard_map(
         per_device,

time: 164 us -> 161 us (0.982)
  blocking collectives: 150 us -> 147 us
    all_to_all x9, blocking collectives: 128 us -> 126 us  [exchange(): return lax.all_to_all(blocks, axis, 0, 0, tiled=False)]
where the time goes in v6:
time: 161 us
  blocking collectives  147 us (91%)
  matrix products  4.25 us (3%)
  starting transfers between devices  3.36 us (2%)
  other arithmetic  2.81 us (2%)
    all_to_all x9, blocking collectives, exchange(): return lax.all_to_all(blocks, axis, 0, 0, tiled=False)  126 us
    all_gather x2, blocking collectives, gather(): return lax.all_gather(block, axis, tiled=True)  21 us
    ppermute x1, starting transfers between devices, per_device(): taken = lax.ppermute(given, CORE_AXIS, [(0, 1), (1, 0)])  3.36 us
  transfers between devices with their start and end apart: 1, of which 1 were waited for; matrix products, arithmetic and copies ran while one was open for 0% of the time, Pallas kernels for 0%

profile of v6, /device:TPU:1, one launch (start us, length us, event | category | flops | bytes accessed | tf_op | source)
XLA Modules:
  0.0 160.9 jit_solution(14211592122687259710)
XLA Ops:
  0.6 0.0 copy-start
  0.7 0.0 copy-start.4
  0.7 0.0 copy-start.5
  0.7 1.5 fusion.9
  2.2 0.0 copy-done.4
  2.2 0.0 copy-done.5
  2.2 0.0 copy-start.2
  2.2 0.1 iota_compare_fusion.5
  2.3 0.1 add_convert_fusion.3
  2.4 0.1 concatenate.47
  2.5 19.7 %all_to_all.51 = f32[16,1,1152]{2,1,0:T(1,128)S(1)} all-to-all(f32[16,1,1152]{2,1,0:T(1,128)S(1)} %broadcast_in_dim.27), channel_id=1, replica_groups=mesh['y'=8,'x'=4,'z'=8,'core'=2] {'z','core'}, dimensions={0} | all-to-all | bytes 147456 | tf_op jit(solution)/shard_map/all_to_all | solution.py:27
  22.2 0.1 reshape.107
  22.3 0.1 eq.48
  22.4 0.2 convolution_bitcast_fusion
  22.6 0.1 sub.35
  22.7 0.2 convolution_convert_fusion.3
  22.9 0.1 pad_maximum_fusion.7
  23.0 0.0 copy-done
  23.0 0.0 copy-done.2
  23.0 0.6 fusion.44
  23.7 18.2 %all_to_all.52 = f32[32,1,320]{2,1,0:T(1,128)S(1)} all-to-all(f32[32,1,320]{2,1,0:T(1,128)S(1)} %broadcast_in_dim.29), channel_id=1, replica_groups=mesh['y'=8,'x'=4,'z'=8,'core'=2] {'y','x'}, dimensions={0} | all-to-all | bytes 81920 | tf_op jit(solution)/shard_map/all_to_all | solution.py:27
  42.0 0.1 reduce_sum.110
  42.0 0.1 broadcast_subtract_fusion
  42.1 0.1 fusion.12
  42.2 0.1 select_bitcast_fusion
  42.3 3.4 %collective-permute-start = (bf16[8,64,256]{2,1,0:T(8,128)(2,1)S(1)}, bf16[8,64,256]{2,1,0:T(8,128)(2,1)S(1)}, u32[]{:S(2)}, u32[]{:S(2)}) collective-permute-start(bf16[8,64,256]{2,1,0:T(8,128)(2,1)S(1)} %fusion.12), channel_id=1, source_target_pairs={{0,1},{1,0},{2,3},{3,2},{4,5},{5,4},{6,7},{7,6},{8,9},{9,8},{10,11... | collective-permute-start | bytes 786440 | tf_op jit(solution)/shard_map/ppermute | solution.py:137
  45.6 1.1 collective-permute-done
  46.8 0.1 add_convert_fusion
  46.9 14.7 %all_to_all.53 = bf16[8,64,256]{2,1,0:T(8,128)(2,1)S(1)} all-to-all(bf16[8,64,256]{2,1,0:T(8,128)(2,1)S(1)} %add_convert_fusion), channel_id=1, replica_groups=mesh['y'=8,'x'=4,'z'=8,'core'=2] {'z'}, dimensions={0} | all-to-all | bytes 524288 | tf_op jit(solution)/shard_map/all_to_all | solution.py:27
  61.6 0.0 copy-start.3
  61.6 0.1 multiply_reduce_fusion.2
  61.8 0.1 multiply_convert_fusion.2
  61.8 0.4 copy-done.3
  62.3 14.2 %all_to_all.54 = bf16[8,64,256]{2,1,0:T(8,128)(2,1)S(1)} all-to-all(bf16[8,64,256]{2,1,0:T(8,128)(2,1)S(1)} %broadcast_in_dim.31), channel_id=1, replica_groups=mesh['y'=8,'x'=4,'z'=8,'core'=2] {'z'}, dimensions={0} | all-to-all | bytes 524288 | tf_op jit(solution)/shard_map/all_to_all | solution.py:27
  76.5 2.8 %all_gather.6 = bf16[1024,256]{1,0:T(8,128)(2,1)S(1)} all-gather(bf16[512,256]{1,0:T(8,128)(2,1)S(1)} %bitcast.68), channel_id=1, replica_groups=mesh['y'=8,'x'=4,'z'=8,'core'=2] {'core'}, dimensions={0}, use_global_device_ids=true | all-gather | bytes 786432 | tf_op jit(solution)/shard_map/all_gather | solution.py:35
  79.3 0.2 convolution_convert_fusion.1
  79.6 15.5 %all_to_all.55 = bf16[8,160,128]{2,1,0:T(8,128)(2,1)S(1)} all-to-all(bf16[8,160,128]{2,1,0:T(8,128)(2,1)S(1)} %broadcast_in_dim.32), channel_id=1, replica_groups=mesh['y'=8,'x'=4,'z'=8,'core'=2] {'y'}, dimensions={0} | all-to-all | bytes 655360 | tf_op jit(solution)/shard_map/all_to_all | solution.py:27
  95.2 7.4 %all_to_all.56 = bf16[4,160,128]{2,1,0:T(8,128)(2,1)S(1)} all-to-all(bf16[4,160,128]{2,1,0:T(8,128)(2,1)S(1)} %broadcast_in_dim.34), channel_id=1, replica_groups=mesh['y'=8,'x'=4,'z'=8,'core'=2] {'x'}, dimensions={0} | all-to-all | bytes 327680 | tf_op jit(solution)/shard_map/all_to_all | solution.py:27
  102.6 0.1 fusion.39
  102.7 0.1 multiply_reduce_fusion.1
  102.8 0.3 fusion.7
  103.2 0.1 fusion.23
  103.3 0.1 subtract_convert_fusion.1
  103.4 0.2 fusion.45
  103.7 12.6 %all_to_all.57 = f32[16,1,1024]{2,1,0:T(1,128)S(1)} all-to-all(f32[16,1,1024]{2,1,0:T(1,128)S(1)} %broadcast_in_dim.35), channel_id=1, replica_groups=mesh['y'=8,'x'=4,'z'=8,'core'=2] {'z','core'}, dimensions={0} | all-to-all | bytes 131072 | tf_op jit(solution)/shard_map/all_to_all | solution.py:27
  116.2 0.1 reduce_sum.116
  116.3 0.2 convolution_convert_fusion
  116.5 0.2 convolution_convert_fusion.2
  116.7 0.1 maximum_maximum_fusion
  116.8 16.2 %all_to_all.58 = bf16[8,160,128]{2,1,0:T(8,128)(2,1)S(1)} all-to-all(bf16[8,160,128]{2,1,0:T(8,128)(2,1)S(1)} %broadcast_in_dim.36), channel_id=1, replica_groups=mesh['y'=8,'x'=4,'z'=8,'core'=2] {'y'}, dimensions={0} | all-to-all | bytes 655360 | tf_op jit(solution)/shard_map/all_to_all | solution.py:27
  133.1 7.4 %all_to_all.59 = bf16[4,160,128]{2,1,0:T(8,128)(2,1)S(1)} all-to-all(bf16[4,160,128]{2,1,0:T(8,128)(2,1)S(1)} %broadcast_in_dim.38), channel_id=1, replica_groups=mesh['y'=8,'x'=4,'z'=8,'core'=2] {'x'}, dimensions={0} | all-to-all | bytes 327680 | tf_op jit(solution)/shard_map/all_to_all | solution.py:27
  140.5 0.1 fusion.38
  140.6 0.1 fusion.22
  140.7 0.1 subtract_convert_fusion
  140.8 0.1 multiply_reduce_fusion
  140.9 0.1 multiply_convert_fusion
  141.0 0.1 pad_maximum_fusion.3
  141.1 18.2 %all_gather.7 = bf16[1024,384]{1,0:T(8,128)(2,1)S(1)} all-gather(bf16[64,384]{1,0:T(8,128)(2,1)S(1)} %pad_maximum_fusion.3), channel_id=1, replica_groups=mesh['y'=8,'x'=4,'z'=8,'core'=2] {'z','core'}, dimensions={0}, use_global_device_ids=true | all-gather | bytes 835584 | tf_op jit(solution)/shard_map/all_gather | solution.py:35
  159.3 0.0 copy-start.1
  159.4 0.3 fusion.3
  159.7 0.3 fusion.46
  160.0 0.2 copy-done.1
  160.1 0.8 broadcast_divide_fusion
  (38 shorter events, 0.7 us)
Async XLA Ops:
  0.6 22.4 %copy-start = (bf16[256,256]{1,0:T(8,128)(2,1)S(1)}, bf16[256,256]{1,0:T(8,128)(2,1)}, u32[]{:S(2)}) copy-start(bf16[256,256]{1,0:T(8,128)(2,1)} %param.7) | copy-start | bytes 393220
  0.7 1.5 copy-start.4
  0.7 1.5 copy-start.5
  2.2 20.9 %copy-start.2 = (s32[1024,256]{1,0:T(8,128)S(1)}, s32[1024,256]{1,0:T(8,128)}, u32[]{:S(2)}) copy-start(s32[1024,256]{1,0:T(8,128)} %param.4) | copy-start | bytes 3145732
  42.3 4.5 %collective-permute-start = (bf16[8,64,256]{2,1,0:T(8,128)(2,1)S(1)}, bf16[8,64,256]{2,1,0:T(8,128)(2,1)S(1)}, u32[]{:S(2)}, u32[]{:S(2)}) collective-permute-start(bf16[8,64,256]{2,1,0:T(8,128)(2,1)S(1)} %fusion.12), channel_id=1, source_target_pairs={{0,1},{1,0},{2,3},{3,2},{4,5},{5,4},{6,7},{7,6},{8,9},{9,8},{10,11... | collective-permute-start | bytes 786440 | tf_op jit(solution)/shard_map/ppermute | solution.py:137
  61.6 0.6 copy-start.3
  159.3 0.8 copy-start.1

commit v7 on v6

--- a/solution.py
+++ b/solution.py
@@ -1,6 +1,8 @@
 import jax
 import jax.numpy as jnp
 from jax import lax
+from jax.experimental import pallas as pl
+from jax.experimental.pallas import tpu as pltpu
 from jax.sharding import PartitionSpec as P
 
 K = 1024
@@ -91,6 +93,83 @@
     return jnp.exp(-distance / cluster_spread) * lookup
 
 
+def start_kernel(counts_hbm, shares_ref, low_ref, held, sems):
+    rows = held.shape[1]
+    copies = [
+        pltpu.make_async_copy(counts_hbm.at[pl.ds(at * rows, rows)], held.at[at], sems.at[at])
+        for at in range(held.shape[0])
+    ]
+    for copy in copies:
+        copy.start()
+    ones = jnp.ones((8, held.shape[2]), bf16)
+    for at, copy in enumerate(copies):
+        copy.wait()
+        low = held[at].astype(f32).astype(bf16)
+        low_ref[pl.ds(at * rows, rows), :] = low
+        shares_ref[:, pl.ds(at * rows, rows)] = dot_rows(ones, low)
+
+
+def start(counts):
+    group, genes = counts.shape
+    chunks = 4
+    return pl.pallas_call(
+        start_kernel,
+        out_shape=(
+            jax.ShapeDtypeStruct((8, group), f32),
+            jax.ShapeDtypeStruct((group, genes), bf16),
+        ),
+        in_specs=[pl.BlockSpec(memory_space=pltpu.HBM)],
+        out_specs=(pl.BlockSpec(memory_space=pltpu.VMEM),) * 2,
+        scratch_shapes=[
+            pltpu.VMEM((chunks, group // chunks, genes), jnp.int32),
+            pltpu.SemaphoreType.DMA((chunks,)),
+        ],
+        compiler_params=pltpu.CompilerParams(vmem_limit_bytes=8 << 20),
+    )(pltpu.with_memory_space_constraint(counts, pltpu.HBM))
+
+
+def finish_kernel(
+    own_ref, twice_ref, rows_ref, emb_ref, emb_hbm, assign_hbm, cent_hbm, held, sems
+):
+    width = own_ref.shape[1]
+    copies = [
+        pltpu.make_async_copy(rows_ref.at[:, pl.ds(0, width)], cent_hbm, sems.at[0]),
+        pltpu.make_async_copy(emb_ref, emb_hbm, sems.at[1]),
+    ]
+    for copy in copies:
+        copy.start()
+    similarity = dot_rows(own_ref[...], rows_ref[:, :width])
+    lookup = dot_rows(twice_ref[...], rows_ref[:, width:])
+    weights = weigh(similarity, lookup)
+    total = jnp.sum(weights, axis=1, keepdims=True)
+    rows = held.shape[0] // 4
+    for at in range(4):
+        part = pl.ds(at * rows, rows)
+        held[part, :] = weights[at * rows : (at + 1) * rows] / total[at * rows : (at + 1) * rows]
+        copy = pltpu.make_async_copy(held.at[part], assign_hbm.at[part], sems.at[2 + at])
+        copy.start()
+        copies.append(copy)
+    for copy in copies:
+        copy.wait()
+
+
+def finish(own_rows, own_twice, rows, embedding):
+    own, width = own_rows.shape
+    outside = pl.BlockSpec(memory_space=pltpu.HBM)
+    return pl.pallas_call(
+        finish_kernel,
+        out_shape=(
+            jax.ShapeDtypeStruct((own, width), f32),
+            jax.ShapeDtypeStruct((own, K), f32),
+            jax.ShapeDtypeStruct((K, width), bf16),
+        ),
+        in_specs=[pl.BlockSpec(memory_space=pltpu.VMEM)] * 4,
+        out_specs=(outside,) * 3,
+        scratch_shapes=[pltpu.VMEM((own, K), f32), pltpu.SemaphoreType.DMA((6,))],
+        compiler_params=pltpu.CompilerParams(vmem_limit_bytes=8 << 20),
+    )(own_rows, own_twice, rows, embedding)
+
+
 def per_device(counts, batch, seeds, loadings):
     n_cells, n_genes = lax.axis_size(CELL_AXIS), lax.axis_size(GENE_AXIS)
     n_z, n_core = lax.axis_size(Z_AXIS), lax.axis_size(CORE_AXIS)
@@ -99,8 +178,7 @@
     width = loadings.shape[1]
     mine = K // n_genes
 
-    values = counts.astype(f32)
-    shares = dot_rows(jnp.ones((8, counts.shape[1]), bf16), counts.astype(bf16))
+    shares, values = start(counts)
     packet = jnp.concatenate([shares[0], batch[:, 0].astype(f32), seeds[:, 0].astype(f32)])
     own_hot = (batch == jnp.arange(B, dtype=jnp.int32)[None, :]).astype(bf16)
     own_twice = jnp.concatenate([own_hot, own_hot], axis=1)
@@ -113,7 +191,7 @@
     group_batch = labels[0].reshape(group)
     group_seeds = labels[1].reshape(group)
 
-    logged = jnp.log1p(10000.0 * values / depth_total[:, None]).astype(bf16)
+    logged = jnp.log1p(10000.0 * values.astype(f32) / depth_total[:, None]).astype(bf16)
     partial = dot(logged, loadings)
 
     batch_hot = hot_columns(group_batch, B)
@@ -153,9 +231,7 @@
         rows = jnp.concatenate([unit(sums), penalty], axis=1)
 
     rows = gather(rows, GENE_AXIS)
-    weights = weigh(dot_rows(own_rows, rows[:, :width]), dot_rows(own_twice, rows[:, width:]))
-    assign = weights / jnp.sum(weights, axis=1, keepdims=True)
-    return (embedding, assign, rows[:, :width])
+    return finish(own_rows, own_twice, rows, embedding)
 
 
 def solution(mesh):

time: 161 us -> 161 us (level)
  Pallas kernels: 0 us -> 2.93 us
  matrix products: 4.25 us -> 2.14 us
    pallas_call x0 -> x2, Pallas kernels: none -> 2.93 us  [the longest x1 1.73 us: start(): pl.pallas_call(start_kernel, out_shape=(jax.ShapeDtypeStruct((8, group),...]
    dot_general x7 -> x4, matrix products: 2.95 us -> 0.84 us  [dot_rows(): return lax.dot_general(left, right, trailing, preferred_element_type=f32)]
where the time goes in v7:
time: 161 us
  blocking collectives  147 us (91%)
  starting transfers between devices  3.36 us (2%)
  Pallas kernels  2.93 us (2%)
  matrix products  2.14 us (1%)
  other arithmetic  2.01 us (1%)
    all_to_all x9, blocking collectives, exchange(): return lax.all_to_all(blocks, axis, 0, 0, tiled=False)  126 us
    all_gather x2, blocking collectives, gather(): return lax.all_gather(block, axis, tiled=True)  21 us
    ppermute x1, starting transfers between devices, per_device(): taken = lax.ppermute(given, CORE_AXIS, [(0, 1), (1, 0)])  3.36 us
  transfers between devices with their start and end apart: 1, of which 1 were waited for; matrix products, arithmetic and copies ran while one was open for 0% of the time, Pallas kernels for 0%

profile of v7, /device:TPU:1, one launch (start us, length us, event | category | flops | bytes accessed | tf_op | source)
XLA Modules:
  0.0 160.8 jit_solution(668764046457653857)
XLA Ops:
  0.6 0.0 copy-start
  0.7 0.0 copy-start.1
  0.7 0.0 copy-start.2
  0.7 0.7 copy-done.1
  1.3 0.0 copy-done.2
  1.4 0.1 iota_compare_fusion.5
  1.4 0.1 add_convert_fusion.3.twice_ref
  1.5 1.7 %shard_map.67 = (f32[8,1024]{1,0:T(8,128)S(1)}, bf16[1024,256]{1,0:T(8,128)(2,1)S(1)}) custom-call(s32[1024,256]{1,0:T(8,128)} %counts_hbm.1), custom_call_target="tpu_custom_call" | custom-call | tf_op jit(solution)/shard_map/pallas_call | solution.py:115
  3.3 0.1 concatenate.47
  3.4 19.6 %all_to_all.51 = f32[16,1,1152]{2,1,0:T(1,128)S(1)} all-to-all(f32[16,1,1152]{2,1,0:T(1,128)S(1)} %broadcast_in_dim.24), channel_id=1, replica_groups=mesh['y'=8,'x'=4,'z'=8,'core'=2] {'z','core'}, dimensions={0} | all-to-all | bytes 147456 | tf_op jit(solution)/shard_map/all_to_all | solution.py:29
  23.0 0.1 reshape.106
  23.1 0.1 eq.48
  23.2 0.2 convolution_bitcast_fusion
  23.4 0.1 sub.32
  23.4 0.2 convolution_convert_fusion.3
  23.7 0.1 pad_maximum_fusion.7
  23.8 0.0 copy-done
  23.8 0.6 fusion.37
  24.5 18.2 %all_to_all.52 = f32[32,1,320]{2,1,0:T(1,128)S(1)} all-to-all(f32[32,1,320]{2,1,0:T(1,128)S(1)} %broadcast_in_dim.26), channel_id=1, replica_groups=mesh['y'=8,'x'=4,'z'=8,'core'=2] {'y','x'}, dimensions={0} | all-to-all | bytes 81920 | tf_op jit(solution)/shard_map/all_to_all | solution.py:29
  42.7 0.1 reduce_sum.101
  42.8 0.1 broadcast_subtract_fusion
  42.9 0.1 fusion.8
  43.0 0.1 select_bitcast_fusion
  43.0 3.4 %collective-permute-start = (bf16[8,64,256]{2,1,0:T(8,128)(2,1)S(1)}, bf16[8,64,256]{2,1,0:T(8,128)(2,1)S(1)}, u32[]{:S(2)}, u32[]{:S(2)}) collective-permute-start(bf16[8,64,256]{2,1,0:T(8,128)(2,1)S(1)} %fusion.8), channel_id=1, source_target_pairs={{0,1},{1,0},{2,3},{3,2},{4,5},{5,4},{6,7},{7,6},{8,9},{9,8},{10,11... | collective-permute-start | bytes 786440 | tf_op jit(solution)/shard_map/ppermute | solution.py:215
  46.4 1.1 collective-permute-done
  47.5 0.1 add_convert_fusion
  47.6 14.7 %all_to_all.53 = bf16[8,64,256]{2,1,0:T(8,128)(2,1)S(1)} all-to-all(bf16[8,64,256]{2,1,0:T(8,128)(2,1)S(1)} %add_convert_fusion), channel_id=1, replica_groups=mesh['y'=8,'x'=4,'z'=8,'core'=2] {'z'}, dimensions={0} | all-to-all | bytes 524288 | tf_op jit(solution)/shard_map/all_to_all | solution.py:29
  62.4 0.1 multiply_reduce_fusion.2
  62.5 0.1 multiply_convert_fusion.2.own_ref
  62.6 14.2 %all_to_all.54 = bf16[8,64,256]{2,1,0:T(8,128)(2,1)S(1)} all-to-all(bf16[8,64,256]{2,1,0:T(8,128)(2,1)S(1)} %broadcast_in_dim.28), channel_id=1, replica_groups=mesh['y'=8,'x'=4,'z'=8,'core'=2] {'z'}, dimensions={0} | all-to-all | bytes 524288 | tf_op jit(solution)/shard_map/all_to_all | solution.py:29
  76.8 2.8 %all_gather.6 = bf16[1024,256]{1,0:T(8,128)(2,1)S(1)} all-gather(bf16[512,256]{1,0:T(8,128)(2,1)S(1)} %bitcast.65), channel_id=1, replica_groups=mesh['y'=8,'x'=4,'z'=8,'core'=2] {'core'}, dimensions={0}, use_global_device_ids=true | all-gather | bytes 786432 | tf_op jit(solution)/shard_map/all_gather | solution.py:37
  79.7 0.2 convolution_convert_fusion.1
  79.9 15.5 %all_to_all.55 = bf16[8,160,128]{2,1,0:T(8,128)(2,1)S(1)} all-to-all(bf16[8,160,128]{2,1,0:T(8,128)(2,1)S(1)} %broadcast_in_dim.29), channel_id=1, replica_groups=mesh['y'=8,'x'=4,'z'=8,'core'=2] {'y'}, dimensions={0} | all-to-all | bytes 655360 | tf_op jit(solution)/shard_map/all_to_all | solution.py:29
  95.6 7.4 %all_to_all.56 = bf16[4,160,128]{2,1,0:T(8,128)(2,1)S(1)} all-to-all(bf16[4,160,128]{2,1,0:T(8,128)(2,1)S(1)} %broadcast_in_dim.31), channel_id=1, replica_groups=mesh['y'=8,'x'=4,'z'=8,'core'=2] {'x'}, dimensions={0} | all-to-all | bytes 327680 | tf_op jit(solution)/shard_map/all_to_all | solution.py:29
  103.0 0.1 fusion.32
  103.1 0.1 multiply_reduce_fusion.1
  103.2 0.3 fusion.3
  103.5 0.1 fusion.18
  103.6 0.1 subtract_convert_fusion.1
  103.7 0.2 fusion.38
  104.0 12.6 %all_to_all.57 = f32[16,1,1024]{2,1,0:T(1,128)S(1)} all-to-all(f32[16,1,1024]{2,1,0:T(1,128)S(1)} %broadcast_in_dim.32), channel_id=1, replica_groups=mesh['y'=8,'x'=4,'z'=8,'core'=2] {'z','core'}, dimensions={0} | all-to-all | bytes 131072 | tf_op jit(solution)/shard_map/all_to_all | solution.py:29
  116.6 0.1 reduce_sum.107
  116.7 0.2 convolution_convert_fusion
  116.9 0.2 convolution_convert_fusion.2
  117.1 0.1 maximum_maximum_fusion
  117.2 16.2 %all_to_all.58 = bf16[8,160,128]{2,1,0:T(8,128)(2,1)S(1)} all-to-all(bf16[8,160,128]{2,1,0:T(8,128)(2,1)S(1)} %broadcast_in_dim.33), channel_id=1, replica_groups=mesh['y'=8,'x'=4,'z'=8,'core'=2] {'y'}, dimensions={0} | all-to-all | bytes 655360 | tf_op jit(solution)/shard_map/all_to_all | solution.py:29
  133.4 7.4 %all_to_all.59 = bf16[4,160,128]{2,1,0:T(8,128)(2,1)S(1)} all-to-all(bf16[4,160,128]{2,1,0:T(8,128)(2,1)S(1)} %broadcast_in_dim.35), channel_id=1, replica_groups=mesh['y'=8,'x'=4,'z'=8,'core'=2] {'x'}, dimensions={0} | all-to-all | bytes 327680 | tf_op jit(solution)/shard_map/all_to_all | solution.py:29
  140.8 0.1 fusion.31
  140.9 0.1 fusion.17
  141.1 0.1 subtract_convert_fusion
  141.2 0.1 multiply_reduce_fusion
  141.3 0.1 multiply_convert_fusion
  141.4 0.1 pad_maximum_fusion.3
  141.4 18.2 %all_gather.7.rows_ref = bf16[1024,384]{1,0:T(8,128)(2,1)S(1)} all-gather(bf16[64,384]{1,0:T(8,128)(2,1)S(1)} %pad_maximum_fusion.3), channel_id=1, replica_groups=mesh['y'=8,'x'=4,'z'=8,'core'=2] {'z','core'}, dimensions={0}, use_global_device_ids=true | all-gather | bytes 835584 | tf_op jit(solution)/shard_map/all_gather | solution.py:37
  159.7 1.2 shard_map.68
  (38 shorter events, 0.7 us)
Async XLA Ops:
  0.6 23.2 %copy-start = (bf16[256,256]{1,0:T(8,128)(2,1)S(1)}, bf16[256,256]{1,0:T(8,128)(2,1)}, u32[]{:S(2)}) copy-start(bf16[256,256]{1,0:T(8,128)(2,1)} %param.7) | copy-start | bytes 393220
  0.7 0.7 copy-start.1
  0.7 0.7 copy-start.2
  43.0 4.5 %collective-permute-start = (bf16[8,64,256]{2,1,0:T(8,128)(2,1)S(1)}, bf16[8,64,256]{2,1,0:T(8,128)(2,1)S(1)}, u32[]{:S(2)}, u32[]{:S(2)}) collective-permute-start(bf16[8,64,256]{2,1,0:T(8,128)(2,1)S(1)} %fusion.8), channel_id=1, source_target_pairs={{0,1},{1,0},{2,3},{3,2},{4,5},{5,4},{6,7},{7,6},{8,9},{9,8},{10,11... | collective-permute-start | bytes 786440 | tf_op jit(solution)/shard_map/ppermute | solution.py:215

commit v8 on v7

--- a/solution.py
+++ b/solution.py
@@ -91,41 +91,6 @@
 def weigh(similarity, lookup):
     distance = 2.0 - 2.0 * similarity
     return jnp.exp(-distance / cluster_spread) * lookup
-
-
-def start_kernel(counts_hbm, shares_ref, low_ref, held, sems):
-    rows = held.shape[1]
-    copies = [
-        pltpu.make_async_copy(counts_hbm.at[pl.ds(at * rows, rows)], held.at[at], sems.at[at])
-        for at in range(held.shape[0])
-    ]
-    for copy in copies:
-        copy.start()
-    ones = jnp.ones((8, held.shape[2]), bf16)
-    for at, copy in enumerate(copies):
-        copy.wait()
-        low = held[at].astype(f32).astype(bf16)
-        low_ref[pl.ds(at * rows, rows), :] = low
-        shares_ref[:, pl.ds(at * rows, rows)] = dot_rows(ones, low)
-
-
-def start(counts):
-    group, genes = counts.shape
-    chunks = 4
-    return pl.pallas_call(
-        start_kernel,
-        out_shape=(
-            jax.ShapeDtypeStruct((8, group), f32),
-            jax.ShapeDtypeStruct((group, genes), bf16),
-        ),
-        in_specs=[pl.BlockSpec(memory_space=pltpu.HBM)],
-        out_specs=(pl.BlockSpec(memory_space=pltpu.VMEM),) * 2,
-        scratch_shapes=[
-            pltpu.VMEM((chunks, group // chunks, genes), jnp.int32),
-            pltpu.SemaphoreType.DMA((chunks,)),
-        ],
-        compiler_params=pltpu.CompilerParams(vmem_limit_bytes=8 << 20),
-    )(pltpu.with_memory_space_constraint(counts, pltpu.HBM))
 
 
 def finish_kernel(
@@ -178,7 +143,8 @@
     width = loadings.shape[1]
     mine = K // n_genes
 
-    shares, values = start(counts)
+    values = counts.astype(f32)
+    shares = dot_rows(jnp.ones((8, counts.shape[1]), bf16), counts.astype(bf16))
     packet = jnp.concatenate([shares[0], batch[:, 0].astype(f32), seeds[:, 0].astype(f32)])
     own_hot = (batch == jnp.arange(B, dtype=jnp.int32)[None, :]).astype(bf16)
     own_twice = jnp.concatenate([own_hot, own_hot], axis=1)
@@ -191,7 +157,7 @@
     group_batch = labels[0].reshape(group)
     group_seeds = labels[1].reshape(group)
 
-    logged = jnp.log1p(10000.0 * values.astype(f32) / depth_total[:, None]).astype(bf16)
+    logged = jnp.log1p(10000.0 * values / depth_total[:, None]).astype(bf16)
     partial = dot(logged, loadings)
 
     batch_hot = hot_columns(group_batch, B)
@@ -212,7 +178,8 @@
     kept = jnp.where(even, centred[:, 0], centred[:, 1])
     given = jnp.where(even, centred[:, 1], centred[:, 0]).astype(bf16)
     given, kept, batch_total = together((given, kept, batch_total))
-    taken = lax.ppermute(given, CORE_AXIS, [(0, 1), (1, 0)])
+    both = lax.all_gather(given, CORE_AXIS)
+    taken = jnp.where(even, both[1], both[0])
     pairs = (kept + taken.astype(f32)).astype(bf16)
     embedding = jnp.sum(exchange(pairs, Z_AXIS).astype(f32), axis=0)
     own_rows = unit(embedding)

time: 161 us -> 159 us (0.988)
  starting transfers between devices: 3.36 us -> 0 us
  blocking collectives: 147 us -> 150 us
  Pallas kernels: 2.93 us -> 1.19 us
    ppermute x1 -> x0, starting transfers between devices: 3.36 us -> none  [per_device(): taken = lax.ppermute(given, CORE_AXIS, [(0, 1), (1, 0)])]
    all_gather x0 -> x1, blocking collectives: none -> 3.26 us  [per_device(): both = lax.all_gather(given, CORE_AXIS)]
    pallas_call x1 -> x0, Pallas kernels: 1.73 us -> none  [start(): pl.pallas_call(start_kernel, out_shape=(jax.ShapeDtypeStruct((8, group),...]
  transfers between devices with their start and end apart: 1 -> 0, of which waited for: 1 -> 0; matrix products, arithmetic and copies ran while one was open for 0% -> 0% of each run, Pallas kernels for 0% -> 0%
where the time goes in v8:
time: 159 us
  blocking collectives  150 us (94%)
  matrix products  3.64 us (2%)
  other arithmetic  2.03 us (1%)
    all_to_all x9, blocking collectives, exchange(): return lax.all_to_all(blocks, axis, 0, 0, tiled=False)  126 us
    all_gather x2, blocking collectives, gather(): return lax.all_gather(block, axis, tiled=True)  21 us
    all_gather x1, blocking collectives, per_device(): both = lax.all_gather(given, CORE_AXIS)  3.26 us

profile of v8, /device:TPU:1, one launch (start us, length us, event | category | flops | bytes accessed | tf_op | source)
XLA Modules:
  0.0 158.9 jit_solution(18010210347129645554)
XLA Ops:
  0.6 0.0 copy-start
  0.7 0.0 copy-start.2
  0.7 0.0 copy-start.3
  0.7 1.5 fusion.5
  2.2 0.0 copy-done.2
  2.2 0.0 copy-done.3
  2.2 0.0 copy-start.1
  2.2 0.1 iota_compare_fusion.5
  2.3 0.1 add_convert_fusion.2.twice_ref
  2.4 0.1 concatenate.47
  2.5 19.7 %all_to_all.51 = f32[16,1,1152]{2,1,0:T(1,128)S(1)} all-to-all(f32[16,1,1152]{2,1,0:T(1,128)S(1)} %broadcast_in_dim.27), channel_id=1, replica_groups=mesh['y'=8,'x'=4,'z'=8,'core'=2] {'z','core'}, dimensions={0} | all-to-all | bytes 147456 | tf_op jit(solution)/shard_map/all_to_all | solution.py:29
  22.2 0.1 reshape.110
  22.3 0.1 eq.48
  22.4 0.2 convolution_bitcast_fusion
  22.6 0.1 sub.32
  22.7 0.2 convolution_convert_fusion.3
  22.9 0.1 pad_maximum_fusion.7
  23.0 0.0 copy-done
  23.0 0.0 copy-done.1
  23.0 0.6 fusion.39
  23.7 18.2 %all_to_all.52 = f32[32,1,320]{2,1,0:T(1,128)S(1)} all-to-all(f32[32,1,320]{2,1,0:T(1,128)S(1)} %broadcast_in_dim.29), channel_id=1, replica_groups=mesh['y'=8,'x'=4,'z'=8,'core'=2] {'y','x'}, dimensions={0} | all-to-all | bytes 81920 | tf_op jit(solution)/shard_map/all_to_all | solution.py:29
  42.0 0.1 reduce_sum.101
  42.0 0.1 broadcast_subtract_fusion
  42.1 0.1 fusion.8
  42.2 0.1 select_bitcast_fusion
  42.3 3.3 %all-gather = bf16[16,64,256]{2,1,0:T(8,128)(2,1)S(1)} all-gather(bf16[8,64,256]{2,1,0:T(8,128)(2,1)S(1)} %fusion.8), channel_id=2, replica_groups=mesh['y'=8,'x'=4,'z'=8,'core'=2] {'core'}, dimensions={0}, use_global_device_ids=true | all-gather | bytes 786432 | tf_op jit(solution)/shard_map/all_gather | solution.py:181
  45.5 0.1 fusion.4
  45.6 14.7 %all_to_all.53 = bf16[8,64,256]{2,1,0:T(8,128)(2,1)S(1)} all-to-all(bf16[8,64,256]{2,1,0:T(8,128)(2,1)S(1)} %fusion.4), channel_id=1, replica_groups=mesh['y'=8,'x'=4,'z'=8,'core'=2] {'z'}, dimensions={0} | all-to-all | bytes 524288 | tf_op jit(solution)/shard_map/all_to_all | solution.py:29
  60.4 0.1 multiply_reduce_fusion.2
  60.5 0.1 multiply_convert_fusion.2.own_ref
  60.6 14.2 %all_to_all.54 = bf16[8,64,256]{2,1,0:T(8,128)(2,1)S(1)} all-to-all(bf16[8,64,256]{2,1,0:T(8,128)(2,1)S(1)} %broadcast_in_dim.31), channel_id=1, replica_groups=mesh['y'=8,'x'=4,'z'=8,'core'=2] {'z'}, dimensions={0} | all-to-all | bytes 524288 | tf_op jit(solution)/shard_map/all_to_all | solution.py:29
  74.8 2.8 %all_gather.14 = bf16[1024,256]{1,0:T(8,128)(2,1)S(1)} all-gather(bf16[512,256]{1,0:T(8,128)(2,1)S(1)} %bitcast.67), channel_id=1, replica_groups=mesh['y'=8,'x'=4,'z'=8,'core'=2] {'core'}, dimensions={0}, use_global_device_ids=true | all-gather | bytes 786432 | tf_op jit(solution)/shard_map/all_gather | solution.py:37
  77.7 0.2 convolution_convert_fusion.1
  77.9 15.5 %all_to_all.55 = bf16[8,160,128]{2,1,0:T(8,128)(2,1)S(1)} all-to-all(bf16[8,160,128]{2,1,0:T(8,128)(2,1)S(1)} %broadcast_in_dim.32), channel_id=1, replica_groups=mesh['y'=8,'x'=4,'z'=8,'core'=2] {'y'}, dimensions={0} | all-to-all | bytes 655360 | tf_op jit(solution)/shard_map/all_to_all | solution.py:29
  93.6 7.4 %all_to_all.56 = bf16[4,160,128]{2,1,0:T(8,128)(2,1)S(1)} all-to-all(bf16[4,160,128]{2,1,0:T(8,128)(2,1)S(1)} %broadcast_in_dim.34), channel_id=1, replica_groups=mesh['y'=8,'x'=4,'z'=8,'core'=2] {'x'}, dimensions={0} | all-to-all | bytes 327680 | tf_op jit(solution)/shard_map/all_to_all | solution.py:29
  101.0 0.1 fusion.34
  101.1 0.1 multiply_reduce_fusion.1
  101.2 0.3 fusion.3
  101.5 0.1 fusion.18
  101.6 0.1 subtract_convert_fusion.1
  101.7 0.2 fusion.40
  102.0 12.6 %all_to_all.57 = f32[16,1,1024]{2,1,0:T(1,128)S(1)} all-to-all(f32[16,1,1024]{2,1,0:T(1,128)S(1)} %broadcast_in_dim.35), channel_id=1, replica_groups=mesh['y'=8,'x'=4,'z'=8,'core'=2] {'z','core'}, dimensions={0} | all-to-all | bytes 131072 | tf_op jit(solution)/shard_map/all_to_all | solution.py:29
  114.6 0.1 reduce_sum.107
  114.7 0.2 convolution_convert_fusion
  114.9 0.2 convolution_convert_fusion.2
  115.1 0.1 maximum_maximum_fusion
  115.2 16.2 %all_to_all.58 = bf16[8,160,128]{2,1,0:T(8,128)(2,1)S(1)} all-to-all(bf16[8,160,128]{2,1,0:T(8,128)(2,1)S(1)} %broadcast_in_dim.36), channel_id=1, replica_groups=mesh['y'=8,'x'=4,'z'=8,'core'=2] {'y'}, dimensions={0} | all-to-all | bytes 655360 | tf_op jit(solution)/shard_map/all_to_all | solution.py:29
  131.4 7.4 %all_to_all.59 = bf16[4,160,128]{2,1,0:T(8,128)(2,1)S(1)} all-to-all(bf16[4,160,128]{2,1,0:T(8,128)(2,1)S(1)} %broadcast_in_dim.38), channel_id=1, replica_groups=mesh['y'=8,'x'=4,'z'=8,'core'=2] {'x'}, dimensions={0} | all-to-all | bytes 327680 | tf_op jit(solution)/shard_map/all_to_all | solution.py:29
  138.8 0.1 fusion.33
  138.9 0.1 fusion.17
  139.1 0.1 subtract_convert_fusion
  139.2 0.1 multiply_reduce_fusion
  139.3 0.1 multiply_convert_fusion
  139.4 0.1 pad_maximum_fusion.3
  139.4 18.2 %all_gather.15.rows_ref = bf16[1024,384]{1,0:T(8,128)(2,1)S(1)} all-gather(bf16[64,384]{1,0:T(8,128)(2,1)S(1)} %pad_maximum_fusion.3), channel_id=1, replica_groups=mesh['y'=8,'x'=4,'z'=8,'core'=2] {'z','core'}, dimensions={0}, use_global_device_ids=true | all-gather | bytes 835584 | tf_op jit(solution)/shard_map/all_gather | solution.py:37
  157.7 1.2 shard_map.67
  (37 shorter events, 0.7 us)
Async XLA Ops:
  0.6 22.4 %copy-start = (bf16[256,256]{1,0:T(8,128)(2,1)S(1)}, bf16[256,256]{1,0:T(8,128)(2,1)}, u32[]{:S(2)}) copy-start(bf16[256,256]{1,0:T(8,128)(2,1)} %param.7) | copy-start | bytes 393220
  0.7 1.5 copy-start.2
  0.7 1.5 copy-start.3
  2.2 20.9 %copy-start.1 = (s32[1024,256]{1,0:T(8,128)S(1)}, s32[1024,256]{1,0:T(8,128)}, u32[]{:S(2)}) copy-start(s32[1024,256]{1,0:T(8,128)} %param.4) | copy-start | bytes 3145732

commit v9 on v8

--- a/solution.py
+++ b/solution.py
@@ -1,3 +1,5 @@
+from functools import partial as partial_of
+
 import jax
 import jax.numpy as jnp
 from jax import lax
@@ -59,12 +61,6 @@
     return scaled.astype(bf16)
 
 
-def penalty_halves(observed, batch_total, total_cells):
-    mass = jnp.sum(observed, axis=1, keepdims=True)
-    ratio = (mass * batch_total / total_cells + 1.0) / (observed + 1.0)
-    return jnp.concatenate(halves(ratio * ratio), axis=1)
-
-
 def added(blocks):
     total = blocks[0].astype(f32)
     for at in range(1, blocks.shape[0]):
@@ -77,20 +73,87 @@
     return jnp.concatenate([observed[:half], observed[half:]], axis=1).astype(bf16)
 
 
-def everywhere(sums, fold):
-    half, lanes = sums.shape[0] // 2, sums.shape[1] // 2
+def block_of(sums, fold):
+    lanes = sums.shape[1] // 2
     sums = sums.astype(bf16)
-    block = jnp.concatenate([sums[:, :lanes], sums[:, lanes:], fold], axis=0)
-    for axis in (Y_AXIS, X_AXIS):
-        block = added(share(block.astype(bf16), axis))
-    sums = jnp.concatenate([block[: 2 * half], block[2 * half : 4 * half]], axis=1)
-    observed = jnp.concatenate([block[4 * half :, :B], block[4 * half :, B:]], axis=0)
-    return sums, observed
+    return jnp.concatenate([sums[:, :lanes], sums[:, lanes:], fold], axis=0)
+
+
+def everywhere(block):
+    return share(added(share(block, Y_AXIS)).astype(bf16), X_AXIS)
 
 
 def weigh(similarity, lookup):
     distance = 2.0 - 2.0 * similarity
     return jnp.exp(-distance / cluster_spread) * lookup
+
+
+def tables(blocks_ref, twice_ref, total_cells, clusters):
+    total = added(blocks_ref)
+    left, right = total[:clusters], total[clusters : 2 * clusters]
+    observed = total[2 * clusters :]
+    scale = lax.rsqrt(jnp.sum(left * left + right * right, axis=1, keepdims=True) + epsilon)
+    unit_rows = jnp.concatenate([left * scale, right * scale], axis=1).astype(bf16)
+    low_lanes = lax.broadcasted_iota(jnp.int32, observed.shape, 1) < B
+    zero = jnp.zeros_like(observed)
+    mass = jnp.where(
+        low_lanes,
+        jnp.sum(jnp.where(low_lanes, observed, zero), axis=1, keepdims=True),
+        jnp.sum(jnp.where(low_lanes, zero, observed), axis=1, keepdims=True),
+    )
+    ratio = (mass * twice_ref[...] / total_cells + 1.0) / (observed + 1.0)
+    high, low = halves(ratio * ratio)
+    return unit_rows, high.astype(f32), low.astype(f32), low_lanes
+
+
+def weights_kernel(total_cells, blocks_ref, twice_ref, rows_ref, hot_ref, weights_ref, sum_ref):
+    clusters = weights_ref.shape[0]
+    centroids, high, low, low_lanes = tables(blocks_ref, twice_ref, total_cells, clusters)
+    zero = jnp.zeros_like(high)
+    upper = jnp.concatenate(
+        [jnp.where(low_lanes, high, zero), jnp.where(low_lanes, low, zero)], axis=1
+    )
+    lower = jnp.concatenate(
+        [jnp.where(low_lanes, zero, high), jnp.where(low_lanes, zero, low)], axis=1
+    )
+    penalty = jnp.concatenate([upper, lower], axis=0).astype(bf16)
+    weights = weigh(dot_rows(centroids, rows_ref[...]), dot(penalty, hot_ref[...]))
+    weights_ref[...] = weights
+    sum_ref[...] = jnp.sum(weights, axis=0, keepdims=True)
+
+
+def sums_kernel(weights_ref, norm_ref, rows_ref, hot_ref, block_ref):
+    clusters, lanes = weights_ref.shape[0], rows_ref.shape[1] // 2
+    rounded = (weights_ref[...] / norm_ref[...]).astype(bf16)
+    sums = dot(rounded, rows_ref[...])
+    observed = dot_rows(rounded, hot_ref[: 2 * B, :])
+    half = clusters // 2
+    low_lanes = lax.broadcasted_iota(jnp.int32, (half, 2 * B), 1) < B
+    block_ref[:clusters, :] = sums[:, :lanes].astype(bf16)
+    block_ref[clusters : 2 * clusters, :] = sums[:, lanes:].astype(bf16)
+    block_ref[2 * clusters :, :] = jnp.where(
+        low_lanes, observed[:half], observed[half:]
+    ).astype(bf16)
+
+
+def pack_kernel(total_cells, blocks_ref, twice_ref, rows_ref):
+    clusters, width = rows_ref.shape[0], rows_ref.shape[1] - 2 * B
+    centroids, high, low, low_lanes = tables(blocks_ref, twice_ref, total_cells, clusters)
+    rows_ref[:, :width] = centroids
+    upper = jnp.where(low_lanes, high, pltpu.roll(low, B, 1))
+    lower = jnp.where(low_lanes, pltpu.roll(high, B, 1), low)
+    rows_ref[:, width:] = jnp.concatenate([upper, lower], axis=0).astype(bf16)
+
+
+def local(kernel, shapes, *operands):
+    inside = pl.BlockSpec(memory_space=pltpu.VMEM)
+    return pl.pallas_call(
+        kernel,
+        out_shape=shapes,
+        in_specs=[inside] * len(operands),
+        out_specs=jax.tree.map(lambda _: inside, shapes),
+        compiler_params=pltpu.CompilerParams(vmem_limit_bytes=8 << 20),
+    )(*operands)
 
 
 def finish_kernel(
@@ -146,10 +209,10 @@
     values = counts.astype(f32)
     shares = dot_rows(jnp.ones((8, counts.shape[1]), bf16), counts.astype(bf16))
     packet = jnp.concatenate([shares[0], batch[:, 0].astype(f32), seeds[:, 0].astype(f32)])
+    first = (lax.axis_index(GENE_AXIS) * mine).astype(f32)
+    even = lax.axis_index(CORE_AXIS) == 0
     own_hot = (batch == jnp.arange(B, dtype=jnp.int32)[None, :]).astype(bf16)
     own_twice = jnp.concatenate([own_hot, own_hot], axis=1)
-    first = (lax.axis_index(GENE_AXIS) * mine).astype(f32)
-    even = lax.axis_index(CORE_AXIS) == 0
     packet, own_twice, first, even = together((packet, own_twice, first, even))
     packets = share(packet, GENE_AXIS)
     depth_total = jnp.sum(packets[:, :group], axis=0)
@@ -161,23 +224,20 @@
     partial = dot(logged, loadings)
 
     batch_hot = hot_columns(group_batch, B)
-    batch_twice = jnp.concatenate([batch_hot, batch_hot], axis=0)
+    hot_four = jnp.concatenate([batch_hot] * 4, axis=0)
     assign = hot_columns(group_seeds - first, mine)
     first_fold = folded(dot_rows(assign, batch_hot))
     group_labels = dot_rows(jnp.ones((8, group), bf16), batch_hot)[0]
-
     packet = jnp.concatenate([jnp.sum(partial, axis=0), group_labels])
-    packet, batch_hot, batch_twice, assign, first_fold = together(
-        (packet, batch_hot, batch_twice, assign, first_fold)
-    )
+    packet, hot_four, assign, first_fold = together((packet, hot_four, assign, first_fold))
     arrived = jnp.sum(share(packet, CELL_AXIS), axis=0)
     center = arrived[:width] / total_cells
-    batch_total = arrived[width:][None]
+    twice_total = jnp.concatenate([arrived[width:], arrived[width:]])[None]
 
     centred = (partial - center[None]).reshape(n_z, n_core, own, width)
     kept = jnp.where(even, centred[:, 0], centred[:, 1])
     given = jnp.where(even, centred[:, 1], centred[:, 0]).astype(bf16)
-    given, kept, batch_total = together((given, kept, batch_total))
+    given, kept, twice_total = together((given, kept, twice_total))
     both = lax.all_gather(given, CORE_AXIS)
     taken = jnp.where(even, both[1], both[0])
     pairs = (kept + taken.astype(f32)).astype(bf16)
@@ -185,18 +245,33 @@
     own_rows = unit(embedding)
     unit_rows = gather(share(own_rows, Z_AXIS).reshape(n_z * own, width), CORE_AXIS)
 
-    for iteration in range(ITERS):
-        if iteration == 0:
-            sums, fold = dot(assign, unit_rows), first_fold
-        else:
-            weights = weigh(dot_rows(rows[:, :width], unit_rows), dot(rows[:, width:], batch_twice))
-            norm = jnp.sum(share(jnp.sum(weights, axis=0), GENE_AXIS), axis=0)
-            rounded = (weights / norm[None, :]).astype(bf16)
-            sums, fold = dot(rounded, unit_rows), folded(dot_rows(rounded, batch_hot))
-        sums, observed = everywhere(sums, fold)
-        penalty = penalty_halves(observed, batch_total, total_cells)
-        rows = jnp.concatenate([unit(sums), penalty], axis=1)
-
+    blocks = everywhere(block_of(dot(assign, unit_rows), first_fold))
+    for _ in range(1, ITERS):
+        weights, shares = local(
+            partial_of(weights_kernel, total_cells),
+            (jax.ShapeDtypeStruct((mine, group), f32), jax.ShapeDtypeStruct((1, group), f32)),
+            blocks,
+            twice_total,
+            unit_rows,
+            hot_four,
+        )
+        norm = jnp.sum(share(shares, GENE_AXIS), axis=0)
+        block = local(
+            sums_kernel,
+            jax.ShapeDtypeStruct(blocks.shape[1:], bf16),
+            weights,
+            norm,
+            unit_rows,
+            hot_four,
+        )
+        blocks = everywhere(block)
+
+    rows = local(
+        partial_of(pack_kernel, total_cells),
+        jax.ShapeDtypeStruct((mine, width + 2 * B), bf16),
+        blocks,
+        twice_total,
+    )
     rows = gather(rows, GENE_AXIS)
     return finish(own_rows, own_twice, rows, embedding)
 

time: 159 us -> 158 us (level)
  no operation moved by 1% of the time
where the time goes in v9:
time: 158 us
  blocking collectives  150 us (95%)
  matrix products  2.72 us (2%)
  Pallas kernels  2.08 us (1%)
    all_to_all x9, blocking collectives, exchange(): return lax.all_to_all(blocks, axis, 0, 0, tiled=False)  126 us
    all_gather x2, blocking collectives, gather(): return lax.all_gather(block, axis, tiled=True)  21 us
    all_gather x1, blocking collectives, per_device(): both = lax.all_gather(given, CORE_AXIS)  3.25 us

profile of v9, /device:TPU:1, one launch (start us, length us, event | category | flops | bytes accessed | tf_op | source)
XLA Modules:
  0.0 157.7 jit_solution(4641039679391784153)
XLA Ops:
  0.6 0.0 copy-start
  0.7 0.0 copy-start.2
  0.7 0.0 copy-start.3
  0.7 1.5 fusion.1
  2.2 0.0 copy-done.2
  2.2 0.0 copy-done.3
  2.2 0.0 copy-start.1
  2.2 0.1 iota_compare_fusion.5
  2.3 0.1 add_convert_fusion.3.twice_ref
  2.4 0.1 concatenate.28
  2.5 19.7 %all_to_all.50 = f32[16,1,1152]{2,1,0:T(1,128)S(1)} all-to-all(f32[16,1,1152]{2,1,0:T(1,128)S(1)} %broadcast_in_dim.29), channel_id=1, replica_groups=mesh['y'=8,'x'=4,'z'=8,'core'=2] {'z','core'}, dimensions={0} | all-to-all | bytes 147456 | tf_op jit(solution)/shard_map/all_to_all | solution.py:31
  22.2 0.1 reshape.75
  22.3 0.1 eq.48
  22.4 0.2 convolution_bitcast_fusion
  22.6 0.1 sub.23
  22.7 0.2 convolution_convert_fusion.1
  22.9 0.1 add_convert_fusion.hot_ref
  23.0 0.1 pad_maximum_fusion.1
  23.1 0.0 copy-done
  23.1 0.0 copy-done.1
  23.1 0.6 fusion.18
  23.8 18.2 %all_to_all.51 = f32[32,1,320]{2,1,0:T(1,128)S(1)} all-to-all(f32[32,1,320]{2,1,0:T(1,128)S(1)} %broadcast_in_dim.31), channel_id=1, replica_groups=mesh['y'=8,'x'=4,'z'=8,'core'=2] {'y','x'}, dimensions={0} | all-to-all | bytes 81920 | tf_op jit(solution)/shard_map/all_to_all | solution.py:31
  42.0 0.1 reduce_sum.58
  42.1 0.1 broadcast_subtract_fusion
  42.2 0.1 fusion.4
  42.2 0.1 select_bitcast_fusion
  42.3 0.1 maximum_bitcast_fusion.twice_ref
  42.4 3.2 %all-gather = bf16[16,64,256]{2,1,0:T(8,128)(2,1)S(1)} all-gather(bf16[8,64,256]{2,1,0:T(8,128)(2,1)S(1)} %fusion.4), channel_id=2, replica_groups=mesh['y'=8,'x'=4,'z'=8,'core'=2] {'core'}, dimensions={0}, use_global_device_ids=true | all-gather | bytes 786432 | tf_op jit(solution)/shard_map/all_gather | solution.py:241
  45.6 0.1 fusion
  45.7 14.7 %all_to_all.52 = bf16[8,64,256]{2,1,0:T(8,128)(2,1)S(1)} all-to-all(bf16[8,64,256]{2,1,0:T(8,128)(2,1)S(1)} %fusion), channel_id=1, replica_groups=mesh['y'=8,'x'=4,'z'=8,'core'=2] {'z'}, dimensions={0} | all-to-all | bytes 524288 | tf_op jit(solution)/shard_map/all_to_all | solution.py:31
  60.5 0.1 multiply_reduce_fusion
  60.6 0.1 multiply_convert_fusion.own_ref
  60.7 14.2 %all_to_all.53 = bf16[8,64,256]{2,1,0:T(8,128)(2,1)S(1)} all-to-all(bf16[8,64,256]{2,1,0:T(8,128)(2,1)S(1)} %broadcast_in_dim.33), channel_id=1, replica_groups=mesh['y'=8,'x'=4,'z'=8,'core'=2] {'z'}, dimensions={0} | all-to-all | bytes 524288 | tf_op jit(solution)/shard_map/all_to_all | solution.py:31
  75.0 2.8 %all_gather.14.rows_ref = bf16[1024,256]{1,0:T(8,128)(2,1)S(1)} all-gather(bf16[512,256]{1,0:T(8,128)(2,1)S(1)} %bitcast.54), channel_id=1, replica_groups=mesh['y'=8,'x'=4,'z'=8,'core'=2] {'core'}, dimensions={0}, use_global_device_ids=true | all-gather | bytes 786432 | tf_op jit(solution)/shard_map/all_gather | solution.py:39
  77.8 0.2 convolution_convert_fusion
  78.1 15.5 %all_to_all.54 = bf16[8,160,128]{2,1,0:T(8,128)(2,1)S(1)} all-to-all(bf16[8,160,128]{2,1,0:T(8,128)(2,1)S(1)} %broadcast_in_dim.34), channel_id=1, replica_groups=mesh['y'=8,'x'=4,'z'=8,'core'=2] {'y'}, dimensions={0} | all-to-all | bytes 655360 | tf_op jit(solution)/shard_map/all_to_all | solution.py:31
  93.7 7.4 %all_to_all.55.blocks_ref = bf16[4,160,128]{2,1,0:T(8,128)(2,1)S(1)} all-to-all(bf16[4,160,128]{2,1,0:T(8,128)(2,1)S(1)} %broadcast_in_dim.36), channel_id=1, replica_groups=mesh['y'=8,'x'=4,'z'=8,'core'=2] {'x'}, dimensions={0} | all-to-all | bytes 327680 | tf_op jit(solution)/shard_map/all_to_all | solution.py:31
  101.1 0.4 shard_map.67
  101.5 12.6 %all_to_all.56 = f32[16,1,1024]{2,1,0:T(1,128)S(1)} all-to-all(f32[16,1,1024]{2,1,0:T(1,128)S(1)} %broadcast_in_dim.38), channel_id=1, replica_groups=mesh['y'=8,'x'=4,'z'=8,'core'=2] {'z','core'}, dimensions={0} | all-to-all | bytes 131072 | tf_op jit(solution)/shard_map/all_to_all | solution.py:31
  114.1 0.1 reduce_sum.61
  114.2 0.3 shard_map.68
  114.5 16.2 %all_to_all.57 = bf16[8,160,128]{2,1,0:T(8,128)(2,1)S(1)} all-to-all(bf16[8,160,128]{2,1,0:T(8,128)(2,1)S(1)} %broadcast_in_dim.39), channel_id=1, replica_groups=mesh['y'=8,'x'=4,'z'=8,'core'=2] {'y'}, dimensions={0} | all-to-all | bytes 655360 | tf_op jit(solution)/shard_map/all_to_all | solution.py:31
  130.8 7.4 %all_to_all.58.blocks_ref = bf16[4,160,128]{2,1,0:T(8,128)(2,1)S(1)} all-to-all(bf16[4,160,128]{2,1,0:T(8,128)(2,1)S(1)} %broadcast_in_dim.41), channel_id=1, replica_groups=mesh['y'=8,'x'=4,'z'=8,'core'=2] {'x'}, dimensions={0} | all-to-all | bytes 327680 | tf_op jit(solution)/shard_map/all_to_all | solution.py:31
  138.1 0.2 shard_map.69
  138.3 18.2 %all_gather.15.rows_ref = bf16[1024,384]{1,0:T(8,128)(2,1)S(1)} all-gather(bf16[64,384]{1,0:T(8,128)(2,1)S(1)} %shard_map.69), channel_id=1, replica_groups=mesh['y'=8,'x'=4,'z'=8,'core'=2] {'z','core'}, dimensions={0}, use_global_device_ids=true | all-gather | bytes 835584 | tf_op jit(solution)/shard_map/all_gather | solution.py:39
  156.5 1.2 shard_map.70
  (26 shorter events, 0.6 us)
Async XLA Ops:
  0.6 22.4 %copy-start = (bf16[256,256]{1,0:T(8,128)(2,1)S(1)}, bf16[256,256]{1,0:T(8,128)(2,1)}, u32[]{:S(2)}) copy-start(bf16[256,256]{1,0:T(8,128)(2,1)} %param.7) | copy-start | bytes 393220
  0.7 1.5 copy-start.2
  0.7 1.5 copy-start.3
  2.2 20.9 %copy-start.1 = (s32[1024,256]{1,0:T(8,128)S(1)}, s32[1024,256]{1,0:T(8,128)}, u32[]{:S(2)}) copy-start(s32[1024,256]{1,0:T(8,128)} %param.4) | copy-start | bytes 3145732

commit v10 on v9

--- a/solution.py
+++ b/solution.py
@@ -47,10 +47,6 @@
     return lax.dot_general(left, right, trailing, preferred_element_type=f32)
 
 
-def hot_columns(labels, count):
-    return (labels[None, :] == jnp.arange(count, dtype=f32)[:, None]).astype(bf16)
-
-
 def halves(value):
     high = value.astype(bf16)
     return high, (value - high.astype(f32)).astype(bf16)
@@ -68,15 +64,10 @@
     return total
 
 
-def folded(observed):
-    half = observed.shape[0] // 2
-    return jnp.concatenate([observed[:half], observed[half:]], axis=1).astype(bf16)
-
-
-def block_of(sums, fold):
+def block_of(sums, beside):
     lanes = sums.shape[1] // 2
     sums = sums.astype(bf16)
-    return jnp.concatenate([sums[:, :lanes], sums[:, lanes:], fold], axis=0)
+    return jnp.concatenate([sums[:, :lanes], sums[:, lanes:], beside], axis=0)
 
 
 def everywhere(block):
@@ -88,10 +79,9 @@
     return jnp.exp(-distance / cluster_spread) * lookup
 
 
-def tables(blocks_ref, twice_ref, total_cells, clusters):
-    total = added(blocks_ref)
-    left, right = total[:clusters], total[clusters : 2 * clusters]
-    observed = total[2 * clusters :]
+def tables(sums, observed, twice_ref, total_cells):
+    clusters = sums.shape[0] // 2
+    left, right = sums[:clusters], sums[clusters:]
     scale = lax.rsqrt(jnp.sum(left * left + right * right, axis=1, keepdims=True) + epsilon)
     unit_rows = jnp.concatenate([left * scale, right * scale], axis=1).astype(bf16)
     low_lanes = lax.broadcasted_iota(jnp.int32, observed.shape, 1) < B
@@ -106,9 +96,46 @@
     return unit_rows, high.astype(f32), low.astype(f32), low_lanes
 
 
+def labels_kernel(labels_ref, hot_ref, assign_ref, fold_ref, twice_ref):
+    group = labels_ref.shape[1]
+    batch, seeds = labels_ref[0:1, :], labels_ref[1:2, :]
+
+    def hot(labels, row):
+        return (labels.astype(jnp.int32) == row).astype(f32).astype(bf16)
+
+    def iota(count):
+        return lax.broadcasted_iota(jnp.int32, (count, group), 0)
+
+    twice = hot(batch, iota(2 * B) % B)
+    hot_ref[: 2 * B, :] = twice
+    hot_ref[2 * B :, :] = twice
+    clusters = assign_ref.shape[0]
+    assign_ref[...] = hot(seeds, iota(clusters))
+    half = clusters // 2
+    row = iota(half)
+    row = (row % X_SIZE) * (half // X_SIZE) + row // X_SIZE
+    low_lanes = lax.broadcasted_iota(jnp.int32, (half, 2 * B), 1) < B
+    fold_ref[...] = jnp.where(
+        low_lanes,
+        dot_rows(hot(seeds, row), twice),
+        dot_rows(hot(seeds, row + half), twice),
+    )
+    twice_ref[...] = dot_rows(jnp.ones((8, group), bf16), twice)
+
+
 def weights_kernel(total_cells, blocks_ref, twice_ref, rows_ref, hot_ref, weights_ref, sum_ref):
-    clusters = weights_ref.shape[0]
-    centroids, high, low, low_lanes = tables(blocks_ref, twice_ref, total_cells, clusters)
+    sums = 2 * weights_ref.shape[0]
+    rows = (blocks_ref.shape[1] - sums) // 2
+    observed = jnp.concatenate(
+        [
+            blocks_ref[at, sums : sums + rows].astype(f32)
+            + blocks_ref[at, sums + rows :].astype(f32)
+            for at in range(blocks_ref.shape[0])
+        ],
+        axis=0,
+    )
+    total = added(blocks_ref)[:sums]
+    centroids, high, low, low_lanes = tables(total, observed, twice_ref, total_cells)
     zero = jnp.zeros_like(high)
     upper = jnp.concatenate(
         [jnp.where(low_lanes, high, zero), jnp.where(low_lanes, low, zero)], axis=1
@@ -138,7 +165,10 @@
 
 def pack_kernel(total_cells, blocks_ref, twice_ref, rows_ref):
     clusters, width = rows_ref.shape[0], rows_ref.shape[1] - 2 * B
-    centroids, high, low, low_lanes = tables(blocks_ref, twice_ref, total_cells, clusters)
+    total = added(blocks_ref)
+    centroids, high, low, low_lanes = tables(
+        total[: 2 * clusters], total[2 * clusters :], twice_ref, total_cells
+    )
     rows_ref[:, :width] = centroids
     upper = jnp.where(low_lanes, high, pltpu.roll(low, B, 1))
     lower = jnp.where(low_lanes, pltpu.roll(high, B, 1), low)
@@ -217,27 +247,36 @@
     packets = share(packet, GENE_AXIS)
     depth_total = jnp.sum(packets[:, :group], axis=0)
     labels = packets[:, group:].reshape(n_z, n_core, 2, own).transpose(2, 1, 0, 3)
-    group_batch = labels[0].reshape(group)
-    group_seeds = labels[1].reshape(group)
+    labels = jnp.stack([labels[0].reshape(group), labels[1].reshape(group) - first])
+    hot_four, assign, fold, group_labels = local(
+        labels_kernel,
+        (
+            jax.ShapeDtypeStruct((4 * B, group), bf16),
+            jax.ShapeDtypeStruct((mine, group), bf16),
+            jax.ShapeDtypeStruct((mine // 2, 2 * B), f32),
+            jax.ShapeDtypeStruct((8, 2 * B), f32),
+        ),
+        labels,
+    )
 
     logged = jnp.log1p(10000.0 * values / depth_total[:, None]).astype(bf16)
     partial = dot(logged, loadings)
 
-    batch_hot = hot_columns(group_batch, B)
-    hot_four = jnp.concatenate([batch_hot] * 4, axis=0)
-    assign = hot_columns(group_seeds - first, mine)
-    first_fold = folded(dot_rows(assign, batch_hot))
-    group_labels = dot_rows(jnp.ones((8, group), bf16), batch_hot)[0]
-    packet = jnp.concatenate([jnp.sum(partial, axis=0), group_labels])
-    packet, hot_four, assign, first_fold = together((packet, hot_four, assign, first_fold))
-    arrived = jnp.sum(share(packet, CELL_AXIS), axis=0)
+    everyone = jnp.concatenate([jnp.sum(partial, axis=0), group_labels[0]])
+    packet = jnp.concatenate(
+        [jnp.broadcast_to(everyone[None], (n_cells, width + 2 * B)), fold], axis=1
+    )
+    packet, hot_four, assign = together((packet, hot_four, assign))
+    arrived = jnp.sum(exchange(packet, CELL_AXIS), axis=0)
     center = arrived[:width] / total_cells
-    twice_total = jnp.concatenate([arrived[width:], arrived[width:]])[None]
+    twice_total = arrived[width : width + 2 * B][None]
+    high, low = halves(arrived[width + 2 * B :][None])
+    counted = jnp.concatenate([high] * 4 + [low] * 4, axis=0)
 
     centred = (partial - center[None]).reshape(n_z, n_core, own, width)
     kept = jnp.where(even, centred[:, 0], centred[:, 1])
     given = jnp.where(even, centred[:, 1], centred[:, 0]).astype(bf16)
-    given, kept, twice_total = together((given, kept, twice_total))
+    given, kept, twice_total, counted = together((given, kept, twice_total, counted))
     both = lax.all_gather(given, CORE_AXIS)
     taken = jnp.where(even, both[1], both[0])
     pairs = (kept + taken.astype(f32)).astype(bf16)
@@ -245,7 +284,10 @@
     own_rows = unit(embedding)
     unit_rows = gather(share(own_rows, Z_AXIS).reshape(n_z * own, width), CORE_AXIS)
 
-    blocks = everywhere(block_of(dot(assign, unit_rows), first_fold))
+    arrived = share(block_of(dot(assign, unit_rows), counted), Y_AXIS)
+    sums = added(arrived[:, : 2 * mine]).astype(bf16)
+    blocks = jnp.concatenate([sums, arrived[:, 2 * mine], arrived[:, 2 * mine + 4]], axis=0)
+    blocks = share(blocks, X_AXIS)
     for _ in range(1, ITERS):
         weights, shares = local(
             partial_of(weights_kernel, total_cells),
@@ -258,7 +300,7 @@
         norm = jnp.sum(share(shares, GENE_AXIS), axis=0)
         block = local(
             sums_kernel,
-            jax.ShapeDtypeStruct(blocks.shape[1:], bf16),
+            jax.ShapeDtypeStruct((2 * mine + mine // 2, 2 * B), bf16),
             weights,
             norm,
             unit_rows,

time: 158 us -> 157 us (level)
  no operation moved by 1% of the time
where the time goes in v10:
time: 157 us
  blocking collectives  149 us (95%)
  Pallas kernels  2.46 us (2%)
  matrix products  2.41 us (2%)
    all_to_all x9, blocking collectives, exchange(): return lax.all_to_all(blocks, axis, 0, 0, tiled=False)  125 us
    all_gather x2, blocking collectives, gather(): return lax.all_gather(block, axis, tiled=True)  21 us
    all_gather x1, blocking collectives, per_device(): both = lax.all_gather(given, CORE_AXIS)  3.34 us

profile of v10, /device:TPU:1, one launch (start us, length us, event | category | flops | bytes accessed | tf_op | source)
XLA Modules:
  0.0 156.5 jit_solution(5976670320554846378)
XLA Ops:
  0.6 0.0 copy-start
  0.6 0.0 copy-start.1
  0.7 0.0 copy-start.2
  0.7 0.0 copy-start.3
  0.7 1.6 fusion.1
  2.2 0.0 copy-done.2
  2.2 0.0 copy-done.3
  2.3 0.1 iota_compare_fusion
  2.3 0.1 add_convert_fusion.2.twice_ref
  2.4 0.1 concatenate.24
  2.5 19.6 %all_to_all.53 = f32[16,1,1152]{2,1,0:T(1,128)S(1)} all-to-all(f32[16,1,1152]{2,1,0:T(1,128)S(1)} %broadcast_in_dim.25), channel_id=1, replica_groups=mesh['y'=8,'x'=4,'z'=8,'core'=2] {'z','core'}, dimensions={0} | all-to-all | bytes 147456 | tf_op jit(solution)/shard_map/all_to_all | solution.py:31
  22.1 0.1 reshape.96
  22.2 0.1 sub.30
  22.3 0.1 stack_reshape_squeeze.3
  22.4 0.4 shard_map.67
  22.8 0.0 copy-done
  22.8 0.0 copy-done.1
  22.8 0.6 fusion.13
  23.5 18.3 %all_to_all.54 = f32[32,1,512]{2,1,0:T(1,128)S(1)} all-to-all(f32[32,1,512]{2,1,0:T(1,128)S(1)} %all_to_all.35), channel_id=1, replica_groups=mesh['y'=8,'x'=4,'z'=8,'core'=2] {'y','x'}, dimensions={0} | all-to-all | bytes 131072 | tf_op jit(solution)/shard_map/all_to_all | solution.py:31
  41.8 0.1 reduce_sum.58
  41.9 0.1 broadcast_subtract_fusion
  42.0 0.1 fusion.4
  42.1 0.1 select_bitcast_fusion
  42.2 3.3 %all-gather = bf16[16,64,256]{2,1,0:T(8,128)(2,1)S(1)} all-gather(bf16[8,64,256]{2,1,0:T(8,128)(2,1)S(1)} %fusion.4), channel_id=2, replica_groups=mesh['y'=8,'x'=4,'z'=8,'core'=2] {'core'}, dimensions={0}, use_global_device_ids=true | all-gather | bytes 786432 | tf_op jit(solution)/shard_map/all_gather | solution.py:280
  45.5 0.1 fusion
  45.6 14.7 %all_to_all.55 = bf16[8,64,256]{2,1,0:T(8,128)(2,1)S(1)} all-to-all(bf16[8,64,256]{2,1,0:T(8,128)(2,1)S(1)} %fusion), channel_id=1, replica_groups=mesh['y'=8,'x'=4,'z'=8,'core'=2] {'z'}, dimensions={0} | all-to-all | bytes 524288 | tf_op jit(solution)/shard_map/all_to_all | solution.py:31
  60.4 0.1 multiply_reduce_fusion
  60.5 0.1 multiply_convert_fusion.own_ref
  60.6 14.2 %all_to_all.56 = bf16[8,64,256]{2,1,0:T(8,128)(2,1)S(1)} all-to-all(bf16[8,64,256]{2,1,0:T(8,128)(2,1)S(1)} %broadcast_in_dim.28), channel_id=1, replica_groups=mesh['y'=8,'x'=4,'z'=8,'core'=2] {'z'}, dimensions={0} | all-to-all | bytes 524288 | tf_op jit(solution)/shard_map/all_to_all | solution.py:31
  74.9 2.8 %all_gather.14.rows_ref = bf16[1024,256]{1,0:T(8,128)(2,1)S(1)} all-gather(bf16[512,256]{1,0:T(8,128)(2,1)S(1)} %bitcast.64), channel_id=1, replica_groups=mesh['y'=8,'x'=4,'z'=8,'core'=2] {'core'}, dimensions={0}, use_global_device_ids=true | all-gather | bytes 786432 | tf_op jit(solution)/shard_map/all_gather | solution.py:39
  77.7 0.2 convolution_convert_fusion
  78.0 15.0 %all_to_all.57 = bf16[8,136,128]{2,1,0:T(8,128)(2,1)S(1)} all-to-all(bf16[8,136,128]{2,1,0:T(8,128)(2,1)S(1)} %broadcast_in_dim.29), channel_id=1, replica_groups=mesh['y'=8,'x'=4,'z'=8,'core'=2] {'y'}, dimensions={0} | all-to-all | bytes 557056 | tf_op jit(solution)/shard_map/all_to_all | solution.py:31
  93.1 7.3 %all_to_all.58.blocks_ref = bf16[4,144,128]{2,1,0:T(8,128)(2,1)S(1)} all-to-all(bf16[4,144,128]{2,1,0:T(8,128)(2,1)S(1)} %broadcast_in_dim.30), channel_id=1, replica_groups=mesh['y'=8,'x'=4,'z'=8,'core'=2] {'x'}, dimensions={0} | all-to-all | bytes 294912 | tf_op jit(solution)/shard_map/all_to_all | solution.py:31
  100.4 0.4 shard_map.68
  100.8 12.1 %all_to_all.59 = f32[16,1,1024]{2,1,0:T(1,128)S(1)} all-to-all(f32[16,1,1024]{2,1,0:T(1,128)S(1)} %broadcast_in_dim.32), channel_id=1, replica_groups=mesh['y'=8,'x'=4,'z'=8,'core'=2] {'z','core'}, dimensions={0} | all-to-all | bytes 131072 | tf_op jit(solution)/shard_map/all_to_all | solution.py:31
  112.9 0.1 reduce_sum.61
  113.0 0.3 shard_map.69
  113.3 16.2 %all_to_all.60 = bf16[8,160,128]{2,1,0:T(8,128)(2,1)S(1)} all-to-all(bf16[8,160,128]{2,1,0:T(8,128)(2,1)S(1)} %broadcast_in_dim.33), channel_id=1, replica_groups=mesh['y'=8,'x'=4,'z'=8,'core'=2] {'y'}, dimensions={0} | all-to-all | bytes 655360 | tf_op jit(solution)/shard_map/all_to_all | solution.py:31
  129.6 7.4 %all_to_all.61.blocks_ref = bf16[4,160,128]{2,1,0:T(8,128)(2,1)S(1)} all-to-all(bf16[4,160,128]{2,1,0:T(8,128)(2,1)S(1)} %broadcast_in_dim.35), channel_id=1, replica_groups=mesh['y'=8,'x'=4,'z'=8,'core'=2] {'x'}, dimensions={0} | all-to-all | bytes 327680 | tf_op jit(solution)/shard_map/all_to_all | solution.py:31
  136.9 0.2 shard_map.70
  137.1 18.2 %all_gather.15.rows_ref = bf16[1024,384]{1,0:T(8,128)(2,1)S(1)} all-gather(bf16[64,384]{1,0:T(8,128)(2,1)S(1)} %shard_map.70), channel_id=1, replica_groups=mesh['y'=8,'x'=4,'z'=8,'core'=2] {'z','core'}, dimensions={0}, use_global_device_ids=true | all-gather | bytes 835584 | tf_op jit(solution)/shard_map/all_gather | solution.py:39
  155.3 1.2 shard_map.71
  (32 shorter events, 0.6 us)
Async XLA Ops:
  0.6 22.2 %copy-start = (bf16[256,256]{1,0:T(8,128)(2,1)S(1)}, bf16[256,256]{1,0:T(8,128)(2,1)}, u32[]{:S(2)}) copy-start(bf16[256,256]{1,0:T(8,128)(2,1)} %param.7) | copy-start | bytes 393220
  0.6 22.2 %copy-start.1 = (s32[1024,256]{1,0:T(8,128)S(1)}, s32[1024,256]{1,0:T(8,128)}, u32[]{:S(2)}) copy-start(s32[1024,256]{1,0:T(8,128)} %param.4) | copy-start | bytes 3145732
  0.7 1.6 %copy-start.2 = (s32[64,1]{0,1:T(1,128)S(1)}, s32[64,1]{0,1:T(1,128)}, u32[]{:S(2)}) copy-start(s32[64,1]{0,1:T(1,128)} %param.5) | copy-start | bytes 772
  0.7 1.6 %copy-start.3 = (s32[64,1]{0,1:T(1,128)S(1)}, s32[64,1]{0,1:T(1,128)}, u32[]{:S(2)}) copy-start(s32[64,1]{0,1:T(1,128)} %param.6) | copy-start | bytes 772

commit v11 on v10

--- a/solution.py
+++ b/solution.py
@@ -163,16 +163,15 @@
     ).astype(bf16)
 
 
-def pack_kernel(total_cells, blocks_ref, twice_ref, rows_ref):
-    clusters, width = rows_ref.shape[0], rows_ref.shape[1] - 2 * B
+def pack_kernel(total_cells, blocks_ref, twice_ref, packed_ref):
+    sums = packed_ref.shape[0] * 4 // 5
+    half = sums // 2
     total = added(blocks_ref)
-    centroids, high, low, low_lanes = tables(
-        total[: 2 * clusters], total[2 * clusters :], twice_ref, total_cells
-    )
-    rows_ref[:, :width] = centroids
-    upper = jnp.where(low_lanes, high, pltpu.roll(low, B, 1))
-    lower = jnp.where(low_lanes, pltpu.roll(high, B, 1), low)
-    rows_ref[:, width:] = jnp.concatenate([upper, lower], axis=0).astype(bf16)
+    centroids, high, _, _ = tables(total[:sums], total[sums:], twice_ref, total_cells)
+    lanes = centroids.shape[1] // 2
+    packed_ref[:half, :] = centroids[:, :lanes]
+    packed_ref[half:sums, :] = centroids[:, lanes:]
+    packed_ref[sums:, :] = high.astype(bf16)
 
 
 def local(kernel, shapes, *operands):
@@ -187,17 +186,28 @@
 
 
 def finish_kernel(
-    own_ref, twice_ref, rows_ref, emb_ref, emb_hbm, assign_hbm, cent_hbm, held, sems
+    own_ref, twice_ref, packed_ref, emb_ref, emb_hbm, assign_hbm, cent_hbm, cent, held, sems
 ):
-    width = own_ref.shape[1]
+    lanes = packed_ref.shape[2]
+    clusters = cent.shape[0] // packed_ref.shape[0]
+    left = packed_ref[:, :clusters, :].reshape(K, lanes)
+    right = packed_ref[:, clusters : 2 * clusters, :].reshape(K, lanes)
+    cent[:, :lanes] = left
+    cent[:, lanes:] = right
     copies = [
-        pltpu.make_async_copy(rows_ref.at[:, pl.ds(0, width)], cent_hbm, sems.at[0]),
+        pltpu.make_async_copy(cent, cent_hbm, sems.at[0]),
         pltpu.make_async_copy(emb_ref, emb_hbm, sems.at[1]),
     ]
     for copy in copies:
         copy.start()
-    similarity = dot_rows(own_ref[...], rows_ref[:, :width])
-    lookup = dot_rows(twice_ref[...], rows_ref[:, width:])
+    similarity = dot_rows(own_ref[:, :lanes], left) + dot_rows(own_ref[:, lanes:], right)
+    fold = packed_ref[:, 2 * clusters :, :].astype(f32)
+    low_lanes = lax.broadcasted_iota(jnp.int32, fold.shape, 2) < B
+    zero = jnp.zeros_like(fold)
+    penalty = jnp.concatenate(
+        [jnp.where(low_lanes, fold, zero), jnp.where(low_lanes, zero, fold)], axis=1
+    )
+    lookup = dot_rows(twice_ref[...], penalty.reshape(K, lanes).astype(bf16))
     weights = weigh(similarity, lookup)
     total = jnp.sum(weights, axis=1, keepdims=True)
     rows = held.shape[0] // 4
@@ -211,7 +221,7 @@
         copy.wait()
 
 
-def finish(own_rows, own_twice, rows, embedding):
+def finish(own_rows, own_twice, packed, embedding):
     own, width = own_rows.shape
     outside = pl.BlockSpec(memory_space=pltpu.HBM)
     return pl.pallas_call(
@@ -223,9 +233,13 @@
         ),
         in_specs=[pl.BlockSpec(memory_space=pltpu.VMEM)] * 4,
         out_specs=(outside,) * 3,
-        scratch_shapes=[pltpu.VMEM((own, K), f32), pltpu.SemaphoreType.DMA((6,))],
+        scratch_shapes=[
+            pltpu.VMEM((K, width), bf16),
+            pltpu.VMEM((own, K), f32),
+            pltpu.SemaphoreType.DMA((6,)),
+        ],
         compiler_params=pltpu.CompilerParams(vmem_limit_bytes=8 << 20),
-    )(own_rows, own_twice, rows, embedding)
+    )(own_rows, own_twice, packed, embedding)
 
 
 def per_device(counts, batch, seeds, loadings):
@@ -308,14 +322,14 @@
         )
         blocks = everywhere(block)
 
-    rows = local(
+    packed = local(
         partial_of(pack_kernel, total_cells),
-        jax.ShapeDtypeStruct((mine, width + 2 * B), bf16),
+        jax.ShapeDtypeStruct(blocks.shape[1:], bf16),
         blocks,
         twice_total,
     )
-    rows = gather(rows, GENE_AXIS)
-    return finish(own_rows, own_twice, rows, embedding)
+    packed = gather(packed, GENE_AXIS).reshape((n_genes,) + packed.shape)
+    return finish(own_rows, own_twice, packed, embedding)
 
 
 def solution(mesh):

time: 157 us -> 157 us (level)
  no operation moved by 1% of the time
where the time goes in v11:
time: 157 us; the launch traced here: 156 us
  blocking collectives  149 us (95%)
  Pallas kernels  2.44 us (2%)
  matrix products  2.41 us (2%)
    all_to_all x9, blocking collectives, exchange(): return lax.all_to_all(blocks, axis, 0, 0, tiled=False)  125 us
    all_gather x2, blocking collectives, gather(): return lax.all_gather(block, axis, tiled=True)  20.7 us
    all_gather x1, blocking collectives, per_device(): both = lax.all_gather(given, CORE_AXIS)  3.34 us

profile of v11, /device:TPU:1, one launch (start us, length us, event | category | flops | bytes accessed | tf_op | source)
XLA Modules:
  0.0 156.2 jit_solution(15275818633365463667)
XLA Ops:
  0.6 0.0 copy-start
  0.6 0.0 copy-start.1
  0.7 0.0 copy-start.2
  0.7 0.0 copy-start.3
  0.7 1.6 fusion.1
  2.2 0.0 copy-done.2
  2.2 0.0 copy-done.3
  2.3 0.1 iota_compare_fusion
  2.3 0.1 add_convert_fusion.2.twice_ref
  2.4 0.1 concatenate.24
  2.5 19.6 %all_to_all.53 = f32[16,1,1152]{2,1,0:T(1,128)S(1)} all-to-all(f32[16,1,1152]{2,1,0:T(1,128)S(1)} %broadcast_in_dim.25), channel_id=1, replica_groups=mesh['y'=8,'x'=4,'z'=8,'core'=2] {'z','core'}, dimensions={0} | all-to-all | bytes 147456 | tf_op jit(solution)/shard_map/all_to_all | solution.py:31
  22.1 0.1 reshape.99
  22.2 0.1 sub.30
  22.3 0.1 stack_reshape_squeeze.3
  22.4 0.4 shard_map.67
  22.8 0.0 copy-done
  22.8 0.0 copy-done.1
  22.8 0.6 fusion.13
  23.5 18.3 %all_to_all.54 = f32[32,1,512]{2,1,0:T(1,128)S(1)} all-to-all(f32[32,1,512]{2,1,0:T(1,128)S(1)} %all_to_all.35), channel_id=1, replica_groups=mesh['y'=8,'x'=4,'z'=8,'core'=2] {'y','x'}, dimensions={0} | all-to-all | bytes 131072 | tf_op jit(solution)/shard_map/all_to_all | solution.py:31
  41.8 0.1 reduce_sum.58
  41.9 0.1 broadcast_subtract_fusion
  42.0 0.1 fusion.4
  42.1 0.1 select_bitcast_fusion
  42.2 3.3 %all-gather = bf16[16,64,256]{2,1,0:T(8,128)(2,1)S(1)} all-gather(bf16[8,64,256]{2,1,0:T(8,128)(2,1)S(1)} %fusion.4), channel_id=2, replica_groups=mesh['y'=8,'x'=4,'z'=8,'core'=2] {'core'}, dimensions={0}, use_global_device_ids=true | all-gather | bytes 786432 | tf_op jit(solution)/shard_map/all_gather | solution.py:294
  45.5 0.1 fusion
  45.6 14.7 %all_to_all.55 = bf16[8,64,256]{2,1,0:T(8,128)(2,1)S(1)} all-to-all(bf16[8,64,256]{2,1,0:T(8,128)(2,1)S(1)} %fusion), channel_id=1, replica_groups=mesh['y'=8,'x'=4,'z'=8,'core'=2] {'z'}, dimensions={0} | all-to-all | bytes 524288 | tf_op jit(solution)/shard_map/all_to_all | solution.py:31
  60.4 0.1 multiply_reduce_fusion
  60.5 0.1 multiply_convert_fusion.own_ref
  60.6 14.2 %all_to_all.56 = bf16[8,64,256]{2,1,0:T(8,128)(2,1)S(1)} all-to-all(bf16[8,64,256]{2,1,0:T(8,128)(2,1)S(1)} %broadcast_in_dim.28), channel_id=1, replica_groups=mesh['y'=8,'x'=4,'z'=8,'core'=2] {'z'}, dimensions={0} | all-to-all | bytes 524288 | tf_op jit(solution)/shard_map/all_to_all | solution.py:31
  74.9 2.8 %all_gather.14.rows_ref = bf16[1024,256]{1,0:T(8,128)(2,1)S(1)} all-gather(bf16[512,256]{1,0:T(8,128)(2,1)S(1)} %bitcast.66), channel_id=1, replica_groups=mesh['y'=8,'x'=4,'z'=8,'core'=2] {'core'}, dimensions={0}, use_global_device_ids=true | all-gather | bytes 786432 | tf_op jit(solution)/shard_map/all_gather | solution.py:39
  77.7 0.2 convolution_convert_fusion
  78.0 15.0 %all_to_all.57 = bf16[8,136,128]{2,1,0:T(8,128)(2,1)S(1)} all-to-all(bf16[8,136,128]{2,1,0:T(8,128)(2,1)S(1)} %broadcast_in_dim.29), channel_id=1, replica_groups=mesh['y'=8,'x'=4,'z'=8,'core'=2] {'y'}, dimensions={0} | all-to-all | bytes 557056 | tf_op jit(solution)/shard_map/all_to_all | solution.py:31
  93.1 7.3 %all_to_all.58.blocks_ref = bf16[4,144,128]{2,1,0:T(8,128)(2,1)S(1)} all-to-all(bf16[4,144,128]{2,1,0:T(8,128)(2,1)S(1)} %broadcast_in_dim.30), channel_id=1, replica_groups=mesh['y'=8,'x'=4,'z'=8,'core'=2] {'x'}, dimensions={0} | all-to-all | bytes 294912 | tf_op jit(solution)/shard_map/all_to_all | solution.py:31
  100.4 0.4 shard_map.68
  100.8 12.1 %all_to_all.59 = f32[16,1,1024]{2,1,0:T(1,128)S(1)} all-to-all(f32[16,1,1024]{2,1,0:T(1,128)S(1)} %broadcast_in_dim.32), channel_id=1, replica_groups=mesh['y'=8,'x'=4,'z'=8,'core'=2] {'z','core'}, dimensions={0} | all-to-all | bytes 131072 | tf_op jit(solution)/shard_map/all_to_all | solution.py:31
  112.9 0.1 reduce_sum.61
  113.0 0.3 shard_map.69
  113.3 16.2 %all_to_all.60 = bf16[8,160,128]{2,1,0:T(8,128)(2,1)S(1)} all-to-all(bf16[8,160,128]{2,1,0:T(8,128)(2,1)S(1)} %broadcast_in_dim.33), channel_id=1, replica_groups=mesh['y'=8,'x'=4,'z'=8,'core'=2] {'y'}, dimensions={0} | all-to-all | bytes 655360 | tf_op jit(solution)/shard_map/all_to_all | solution.py:31
  129.6 7.4 %all_to_all.61.blocks_ref = bf16[4,160,128]{2,1,0:T(8,128)(2,1)S(1)} all-to-all(bf16[4,160,128]{2,1,0:T(8,128)(2,1)S(1)} %broadcast_in_dim.35), channel_id=1, replica_groups=mesh['y'=8,'x'=4,'z'=8,'core'=2] {'x'}, dimensions={0} | all-to-all | bytes 327680 | tf_op jit(solution)/shard_map/all_to_all | solution.py:31
  136.9 0.1 shard_map.70
  137.0 17.9 %all_gather.15 = bf16[2560,128]{1,0:T(8,128)(2,1)S(1)} all-gather(bf16[160,128]{1,0:T(8,128)(2,1)S(1)} %shard_map.70), channel_id=1, replica_groups=mesh['y'=8,'x'=4,'z'=8,'core'=2] {'z','core'}, dimensions={0}, use_global_device_ids=true | all-gather | bytes 696320 | tf_op jit(solution)/shard_map/all_gather | solution.py:39
  154.9 1.2 shard_map.71
  (32 shorter events, 0.6 us)
Async XLA Ops:
  0.6 22.2 %copy-start = (bf16[256,256]{1,0:T(8,128)(2,1)S(1)}, bf16[256,256]{1,0:T(8,128)(2,1)}, u32[]{:S(2)}) copy-start(bf16[256,256]{1,0:T(8,128)(2,1)} %param.7) | copy-start | bytes 393220
  0.6 22.2 %copy-start.1 = (s32[1024,256]{1,0:T(8,128)S(1)}, s32[1024,256]{1,0:T(8,128)}, u32[]{:S(2)}) copy-start(s32[1024,256]{1,0:T(8,128)} %param.4) | copy-start | bytes 3145732
  0.7 1.6 %copy-start.2 = (s32[64,1]{0,1:T(1,128)S(1)}, s32[64,1]{0,1:T(1,128)}, u32[]{:S(2)}) copy-start(s32[64,1]{0,1:T(1,128)} %param.5) | copy-start | bytes 772
  0.7 1.6 %copy-start.3 = (s32[64,1]{0,1:T(1,128)S(1)}, s32[64,1]{0,1:T(1,128)}, u32[]{:S(2)}) copy-start(s32[64,1]{0,1:T(1,128)} %param.6) | copy-start | bytes 772

commit v12 on v10

--- a/solution.py
+++ b/solution.py
@@ -97,8 +97,19 @@
 
 
 def labels_kernel(labels_ref, hot_ref, assign_ref, fold_ref, twice_ref):
-    group = labels_ref.shape[1]
-    batch, seeds = labels_ref[0:1, :], labels_ref[1:2, :]
+    group = assign_ref.shape[1]
+    given = labels_ref[...]
+    turned = pltpu.roll(given, B, 1)
+    low = lax.broadcasted_iota(jnp.int32, (1, 2 * B), 1) < B
+    batch, seeds = [], []
+    for core in range(2):
+        for at in range(core, given.shape[0], 4):
+            here, there = slice(at, at + 1), slice(at + 2, at + 3)
+            batch.append(jnp.where(low, given[here], turned[there]))
+            seeds.append(jnp.where(low, turned[here], given[there]))
+    batch = jnp.concatenate(batch, axis=1)
+    own = lax.axis_index(Z_AXIS) * lax.axis_size(CORE_AXIS) + lax.axis_index(CORE_AXIS)
+    seeds = jnp.concatenate(seeds, axis=1) - (own * assign_ref.shape[0]).astype(f32)
 
     def hot(labels, row):
         return (labels.astype(jnp.int32) == row).astype(f32).astype(bf16)
@@ -239,15 +250,12 @@
     values = counts.astype(f32)
     shares = dot_rows(jnp.ones((8, counts.shape[1]), bf16), counts.astype(bf16))
     packet = jnp.concatenate([shares[0], batch[:, 0].astype(f32), seeds[:, 0].astype(f32)])
-    first = (lax.axis_index(GENE_AXIS) * mine).astype(f32)
     even = lax.axis_index(CORE_AXIS) == 0
     own_hot = (batch == jnp.arange(B, dtype=jnp.int32)[None, :]).astype(bf16)
     own_twice = jnp.concatenate([own_hot, own_hot], axis=1)
-    packet, own_twice, first, even = together((packet, own_twice, first, even))
+    packet, own_twice, even = together((packet, own_twice, even))
     packets = share(packet, GENE_AXIS)
     depth_total = jnp.sum(packets[:, :group], axis=0)
-    labels = packets[:, group:].reshape(n_z, n_core, 2, own).transpose(2, 1, 0, 3)
-    labels = jnp.stack([labels[0].reshape(group), labels[1].reshape(group) - first])
     hot_four, assign, fold, group_labels = local(
         labels_kernel,
         (
@@ -256,7 +264,7 @@
             jax.ShapeDtypeStruct((mine // 2, 2 * B), f32),
             jax.ShapeDtypeStruct((8, 2 * B), f32),
         ),
-        labels,
+        packets[:, group:],
     )
 
     logged = jnp.log1p(10000.0 * values / depth_total[:, None]).astype(bf16)

time: 157 us -> 157 us (level)
  no operation moved by 1% of the time
where the time goes in v12:
time: 157 us; the launch traced here: 156 us
  blocking collectives  149 us (95%)
  Pallas kernels  2.52 us (2%)
  matrix products  2.4 us (2%)
    all_to_all x9, blocking collectives, exchange(): return lax.all_to_all(blocks, axis, 0, 0, tiled=False)  125 us
    all_gather x2, blocking collectives, gather(): return lax.all_gather(block, axis, tiled=True)  21 us
    all_gather x1, blocking collectives, per_device(): both = lax.all_gather(given, CORE_AXIS)  3.34 us

profile of v12, /device:TPU:1, one launch (start us, length us, event | category | flops | bytes accessed | tf_op | source)
XLA Modules:
  0.0 156.3 jit_solution(14469952352948295426)
XLA Ops:
  0.6 0.0 copy-start
  0.6 0.0 copy-start.1
  0.7 0.0 copy-start.2
  0.7 0.0 copy-start.3
  0.7 1.6 fusion.1
  2.2 0.0 copy-done.2
  2.2 0.0 copy-done.3
  2.3 0.1 iota_compare_fusion
  2.3 0.1 add_convert_fusion.2.twice_ref
  2.4 0.1 concatenate.24
  2.5 19.6 %all_to_all.53 = f32[16,1,1152]{2,1,0:T(1,128)S(1)} all-to-all(f32[16,1,1152]{2,1,0:T(1,128)S(1)} %broadcast_in_dim.25), channel_id=1, replica_groups=mesh['y'=8,'x'=4,'z'=8,'core'=2] {'z','core'}, dimensions={0} | all-to-all | bytes 147456 | tf_op jit(solution)/shard_map/all_to_all | solution.py:31
  22.1 0.5 shard_map.67
  22.6 0.0 copy-done
  22.6 0.0 copy-done.1
  22.6 0.6 fusion.12
  23.4 18.3 %all_to_all.54 = f32[32,1,512]{2,1,0:T(1,128)S(1)} all-to-all(f32[32,1,512]{2,1,0:T(1,128)S(1)} %all_to_all.35), channel_id=1, replica_groups=mesh['y'=8,'x'=4,'z'=8,'core'=2] {'y','x'}, dimensions={0} | all-to-all | bytes 131072 | tf_op jit(solution)/shard_map/all_to_all | solution.py:31
  41.6 0.1 reduce_sum.58
  41.7 0.1 broadcast_subtract_fusion
  41.8 0.1 fusion.4
  41.9 0.1 select_bitcast_fusion
  42.0 3.3 %all-gather = bf16[16,64,256]{2,1,0:T(8,128)(2,1)S(1)} all-gather(bf16[8,64,256]{2,1,0:T(8,128)(2,1)S(1)} %fusion.4), channel_id=2, replica_groups=mesh['y'=8,'x'=4,'z'=8,'core'=2] {'core'}, dimensions={0}, use_global_device_ids=true | all-gather | bytes 786432 | tf_op jit(solution)/shard_map/all_gather | solution.py:288
  45.3 0.1 fusion
  45.5 14.7 %all_to_all.55 = bf16[8,64,256]{2,1,0:T(8,128)(2,1)S(1)} all-to-all(bf16[8,64,256]{2,1,0:T(8,128)(2,1)S(1)} %fusion), channel_id=1, replica_groups=mesh['y'=8,'x'=4,'z'=8,'core'=2] {'z'}, dimensions={0} | all-to-all | bytes 524288 | tf_op jit(solution)/shard_map/all_to_all | solution.py:31
  60.2 0.1 multiply_reduce_fusion
  60.3 0.1 multiply_convert_fusion.own_ref
  60.5 14.2 %all_to_all.56 = bf16[8,64,256]{2,1,0:T(8,128)(2,1)S(1)} all-to-all(bf16[8,64,256]{2,1,0:T(8,128)(2,1)S(1)} %broadcast_in_dim.28), channel_id=1, replica_groups=mesh['y'=8,'x'=4,'z'=8,'core'=2] {'z'}, dimensions={0} | all-to-all | bytes 524288 | tf_op jit(solution)/shard_map/all_to_all | solution.py:31
  74.7 2.8 %all_gather.14.rows_ref = bf16[1024,256]{1,0:T(8,128)(2,1)S(1)} all-gather(bf16[512,256]{1,0:T(8,128)(2,1)S(1)} %bitcast.57), channel_id=1, replica_groups=mesh['y'=8,'x'=4,'z'=8,'core'=2] {'core'}, dimensions={0}, use_global_device_ids=true | all-gather | bytes 786432 | tf_op jit(solution)/shard_map/all_gather | solution.py:39
  77.5 0.2 convolution_convert_fusion
  77.8 15.0 %all_to_all.57 = bf16[8,136,128]{2,1,0:T(8,128)(2,1)S(1)} all-to-all(bf16[8,136,128]{2,1,0:T(8,128)(2,1)S(1)} %broadcast_in_dim.29), channel_id=1, replica_groups=mesh['y'=8,'x'=4,'z'=8,'core'=2] {'y'}, dimensions={0} | all-to-all | bytes 557056 | tf_op jit(solution)/shard_map/all_to_all | solution.py:31
  92.9 7.3 %all_to_all.58.blocks_ref = bf16[4,144,128]{2,1,0:T(8,128)(2,1)S(1)} all-to-all(bf16[4,144,128]{2,1,0:T(8,128)(2,1)S(1)} %broadcast_in_dim.30), channel_id=1, replica_groups=mesh['y'=8,'x'=4,'z'=8,'core'=2] {'x'}, dimensions={0} | all-to-all | bytes 294912 | tf_op jit(solution)/shard_map/all_to_all | solution.py:31
  100.2 0.4 shard_map.68
  100.7 12.1 %all_to_all.59 = f32[16,1,1024]{2,1,0:T(1,128)S(1)} all-to-all(f32[16,1,1024]{2,1,0:T(1,128)S(1)} %broadcast_in_dim.32), channel_id=1, replica_groups=mesh['y'=8,'x'=4,'z'=8,'core'=2] {'z','core'}, dimensions={0} | all-to-all | bytes 131072 | tf_op jit(solution)/shard_map/all_to_all | solution.py:31
  112.7 0.1 reduce_sum.61
  112.8 0.3 shard_map.69
  113.1 16.2 %all_to_all.60 = bf16[8,160,128]{2,1,0:T(8,128)(2,1)S(1)} all-to-all(bf16[8,160,128]{2,1,0:T(8,128)(2,1)S(1)} %broadcast_in_dim.33), channel_id=1, replica_groups=mesh['y'=8,'x'=4,'z'=8,'core'=2] {'y'}, dimensions={0} | all-to-all | bytes 655360 | tf_op jit(solution)/shard_map/all_to_all | solution.py:31
  129.4 7.4 %all_to_all.61.blocks_ref = bf16[4,160,128]{2,1,0:T(8,128)(2,1)S(1)} all-to-all(bf16[4,160,128]{2,1,0:T(8,128)(2,1)S(1)} %broadcast_in_dim.35), channel_id=1, replica_groups=mesh['y'=8,'x'=4,'z'=8,'core'=2] {'x'}, dimensions={0} | all-to-all | bytes 327680 | tf_op jit(solution)/shard_map/all_to_all | solution.py:31
  136.7 0.2 shard_map.70
  136.9 18.2 %all_gather.15.rows_ref = bf16[1024,384]{1,0:T(8,128)(2,1)S(1)} all-gather(bf16[64,384]{1,0:T(8,128)(2,1)S(1)} %shard_map.70), channel_id=1, replica_groups=mesh['y'=8,'x'=4,'z'=8,'core'=2] {'z','core'}, dimensions={0}, use_global_device_ids=true | all-gather | bytes 835584 | tf_op jit(solution)/shard_map/all_gather | solution.py:39
  155.1 1.2 shard_map.71
  (29 shorter events, 0.5 us)
Async XLA Ops:
  0.6 22.0 %copy-start = (bf16[256,256]{1,0:T(8,128)(2,1)S(1)}, bf16[256,256]{1,0:T(8,128)(2,1)}, u32[]{:S(2)}) copy-start(bf16[256,256]{1,0:T(8,128)(2,1)} %param.7) | copy-start | bytes 393220
  0.6 22.0 %copy-start.1 = (s32[1024,256]{1,0:T(8,128)S(1)}, s32[1024,256]{1,0:T(8,128)}, u32[]{:S(2)}) copy-start(s32[1024,256]{1,0:T(8,128)} %param.4) | copy-start | bytes 3145732
  0.7 1.6 %copy-start.2 = (s32[64,1]{0,1:T(1,128)S(1)}, s32[64,1]{0,1:T(1,128)}, u32[]{:S(2)}) copy-start(s32[64,1]{0,1:T(1,128)} %param.5) | copy-start | bytes 772
  0.7 1.6 %copy-start.3 = (s32[64,1]{0,1:T(1,128)S(1)}, s32[64,1]{0,1:T(1,128)}, u32[]{:S(2)}) copy-start(s32[64,1]{0,1:T(1,128)} %param.6) | copy-start | bytes 772
